TPU v7x, 128 devices: a whole 4x4x4 slice. The times are simulated.
128 devices in a mesh: gz: 16 (over x, y), gy: 8 (over z, core).
Axes of the slice: x: 4, y: 4, z: 4, core: 2. Of those that a mesh axis runs over, the one named last changes fastest.
Arguments:
- orbitals: bfloat16 [256, 256, 1024], P(('gz', 'gy')), may hold values from -2 to 2
- points: int32 [1024], replicated, may hold values from 0 to 262143, as said below
- coulomb: float32 [256, 1024], P(None, 'gy'), may hold values from 10 to 1000
Outputs:
- potentials: bfloat16 [256, 1024, 1024], P('gz', 'gy')
Inputs may be any that keep to these rules, and one draw needn't show every extreme that they name: `points`: 1024 distinct grid cells.
All inputs are finite; a program needn't handle non-finite values.
Results may differ from a plain program's by a relative error of at most 0.0025.
Values may be sent and summed in bfloat16 or wider, within the bound.
A program may use at most 192 MiB of HBM per device.

v0:
```python
import math

import jax
import jax.numpy as jnp
from jax import lax
from jax.sharding import PartitionSpec as P


def transform(values_in, kernel):
    planes, col_width, item_count = values_in.shape
    positions = jnp.arange(planes, dtype=jnp.int32)
    angles = (
        2.0
        * math.pi
        / planes
        * (positions[:, None] * positions[None, :] % planes).astype(jnp.float32)
    )
    cosine = jnp.cos(angles)
    sine_table = jnp.sin(angles)
    stacked = values_in.reshape(planes, col_width * item_count)
    real_part = jnp.dot(
        cosine, stacked, precision=lax.Precision.HIGHEST, preferred_element_type=jnp.float32
    )
    imag_part = jnp.dot(
        sine_table, stacked, precision=lax.Precision.HIGHEST, preferred_element_type=jnp.float32
    )
    real_part = (real_part.reshape(planes, col_width, item_count) * kernel[:, :, None]).reshape(
        planes, -1
    )
    imag_part = (imag_part.reshape(planes, col_width, item_count) * kernel[:, :, None]).reshape(
        planes, -1
    )
    back = jnp.dot(
        cosine, real_part, precision=lax.Precision.HIGHEST, preferred_element_type=jnp.float32
    )
    back = back + jnp.dot(
        sine_table, imag_part, precision=lax.Precision.HIGHEST, preferred_element_type=jnp.float32
    )
    return (back / planes).reshape(planes, col_width, item_count)


def per_device(orbitals, points, coulomb):
    gz_count = lax.axis_size("gz")
    gy_count = lax.axis_size("gy")
    bands_local, planes, columns = orbitals.shape
    col_block = columns // gy_count
    col_pencil = col_block // gz_count
    slab_planes = planes // gz_count
    point_count = points.shape[0]
    total_bands = bands_local * gz_count * gy_count
    regrouped = lax.all_to_all(
        lax.all_to_all(orbitals, "gz", split_axis=1, concat_axis=0, tiled=True),
        "gy",
        split_axis=2,
        concat_axis=0,
        tiled=True,
    )
    plane_start = lax.axis_index("gz") * slab_planes
    col_start = lax.axis_index("gy") * col_block
    plane_ids = plane_start + jnp.arange(slab_planes, dtype=jnp.int32)
    column_ids = col_start + jnp.arange(col_block, dtype=jnp.int32)
    cell_ids = (plane_ids[:, None] * columns + column_ids[None, :]).reshape(-1)
    flattened = regrouped.reshape(total_bands, -1)
    selector = (cell_ids[:, None] == points[None, :]).astype(jnp.bfloat16)
    partial_rows = jnp.dot(flattened, selector, preferred_element_type=jnp.float32)
    at_points = lax.psum(partial_rows, ("gz", "gy")).astype(jnp.bfloat16)
    pair_base = lax.dot_general(
        at_points, at_points, (((0,), (0,)), ((), ())), preferred_element_type=jnp.float32
    )
    pair_gram = pair_base * pair_base
    factor = jnp.linalg.cholesky(pair_gram)
    inverse = jax.scipy.linalg.cho_solve((factor, True), jnp.eye(point_count, dtype=jnp.float32))
    sums = lax.dot_general(
        flattened, at_points, (((0,), (0,)), ((), ())), preferred_element_type=jnp.float32
    )
    fitted = jnp.dot(
        sums * sums, inverse, precision=lax.Precision.HIGHEST, preferred_element_type=jnp.float32
    )
    kernel = lax.dynamic_slice_in_dim(coulomb, lax.axis_index("gz") * col_pencil, col_pencil, 1)
    slab_fields = fitted.reshape(slab_planes, col_block, point_count)
    potential = transform(
        lax.all_to_all(slab_fields, "gz", split_axis=1, concat_axis=0, tiled=True), kernel
    ).astype(jnp.bfloat16)
    return lax.all_to_all(potential, "gz", split_axis=0, concat_axis=1, tiled=True)


def solution(mesh):
    return jax.shard_map(
        per_device,
        mesh=mesh,
        in_specs=(P(("gz", "gy"), None, None), P(), P(None, "gy")),
        out_specs=P("gz", "gy", None),
        check_vma=False,
    )
```

profile of v0, /device:TPU:0, one launch (start us, length us, event | category | flops | bytes accessed | tf_op | source)
XLA Modules:
  0.0 868.4 jit_solution(17116670366874837091)
XLA Ops:
  2.3 23.8 %all_to_all.66 = bf16[2,256,1024]{2,0,1:T(2,128)(2,1)S(1)} all-to-all(bf16[2,256,1024]{2,0,1:T(2,128)(2,1)S(1)} %copy.46), channel_id=1, replica_groups=mesh['gz'=16,'gy'=8] {'gz'}, dimensions={1} | all-to-all | bytes 2097152 | tf_op jit(solution)/shard_map/all_to_all | solution.py:52
  47.7 13.0 %all-to-all-done.1 = bf16[8,2,32768]{2,1,0:T(2,128)(2,1)S(1)} async-done(((bf16[8,2,32768]{2,1,0:T(2,128)(2,1)}), bf16[8,2,32768]{2,1,0:T(2,128)(2,1)S(1)}, u32[]{:S(2)}, u32[]{:S(2)}) %all-to-all-start.1) | async-done | bytes 1048608 | tf_op jit(solution)/shard_map/all_to_all | solution.py:51
  73.2 67.8 %all-reduce.2 = bf16[256,1024]{0,1:T(8,128)(2,1)S(1)} all-reduce(f32[256,1024]{0,1:T(8,128)} %fusion.36), channel_id=1, replica_groups=mesh['gz'=16,'gy'=8] {'gz','gy'}, use_global_device_ids=true, to_apply=%region_0.0 | all-reduce | flops 262144 | bytes 1572864 | tf_op jit(solution)/shard_map/psum | solution.py:66
  160.2 11.7 %cholesky.223 = f32[128,128]{1,0:T(8,128)S(1)} custom-call(f32[128,128]{1,0:T(8,128)S(1)} %cholesky.580), custom_call_target="Cholesky" | custom-call | tf_op jit(solution)/shard_map/jit(cholesky)/cholesky | solution.py:71
  172.0 9.8 %custom-call.66 = f32[1,128,128]{1,2,0:T(8,128)S(1)} custom-call(f32[1,128,128]{2,1,0:T(8,128)S(1)} %get-tuple-element.61), custom_call_target="InvertDiagBlocksLowerTriangular" | custom-call | tf_op jit(solution)/shard_map/jit(cholesky)/cholesky | solution.py:71
  188.2 12.1 %cholesky.244 = f32[128,128]{1,0:T(8,128)S(1)} custom-call(f32[128,128]{1,0:T(8,128)S(1)} %cholesky.584), custom_call_target="Cholesky" | custom-call | tf_op jit(solution)/shard_map/jit(cholesky)/cholesky | solution.py:71
  200.9 9.8 %custom-call.67 = f32[1,128,128]{1,2,0:T(8,128)S(1)} custom-call(f32[1,128,128]{2,1,0:T(8,128)S(1)} %get-tuple-element.58), custom_call_target="InvertDiagBlocksLowerTriangular" | custom-call | tf_op jit(solution)/shard_map/jit(cholesky)/cholesky | solution.py:71
  214.1 11.7 %cholesky.468 = f32[128,128]{1,0:T(8,128)S(1)} custom-call(f32[128,128]{1,0:T(8,128)S(1)} %cholesky.589), custom_call_target="Cholesky" | custom-call | tf_op jit(solution)/shard_map/jit(cholesky)/cholesky | solution.py:71
  227.1 9.8 %custom-call.68 = f32[1,128,128]{1,2,0:T(8,128)S(1)} custom-call(f32[1,128,128]{2,1,0:T(8,128)S(1)} %get-tuple-element.55), custom_call_target="InvertDiagBlocksLowerTriangular" | custom-call | tf_op jit(solution)/shard_map/jit(cholesky)/cholesky | solution.py:71
  240.4 11.8 %cholesky.487 = f32[128,128]{1,0:T(8,128)S(1)} custom-call(f32[128,128]{1,0:T(8,128)S(1)} %cholesky.594), custom_call_target="Cholesky" | custom-call | tf_op jit(solution)/shard_map/jit(cholesky)/cholesky | solution.py:71
  253.6 9.8 %custom-call.69 = f32[1,128,128]{1,2,0:T(8,128)S(1)} custom-call(f32[1,128,128]{2,1,0:T(8,128)S(1)} %get-tuple-element.52), custom_call_target="InvertDiagBlocksLowerTriangular" | custom-call | tf_op jit(solution)/shard_map/jit(cholesky)/cholesky | solution.py:71
  266.9 11.7 %cholesky.506 = f32[128,128]{1,0:T(8,128)S(1)} custom-call(f32[128,128]{1,0:T(8,128)S(1)} %cholesky.599), custom_call_target="Cholesky" | custom-call | tf_op jit(solution)/shard_map/jit(cholesky)/cholesky | solution.py:71
  279.9 10.0 %custom-call.70 = f32[1,128,128]{1,2,0:T(8,128)S(1)} custom-call(f32[1,128,128]{2,1,0:T(8,128)S(1)} %get-tuple-element.49), custom_call_target="InvertDiagBlocksLowerTriangular" | custom-call | tf_op jit(solution)/shard_map/jit(cholesky)/cholesky | solution.py:71
  293.2 11.7 %cholesky.526 = f32[128,128]{1,0:T(8,128)S(1)} custom-call(f32[128,128]{1,0:T(8,128)S(1)} %cholesky.604), custom_call_target="Cholesky" | custom-call | tf_op jit(solution)/shard_map/jit(cholesky)/cholesky | solution.py:71
  306.2 9.8 %custom-call.71 = f32[1,128,128]{1,2,0:T(8,128)S(1)} custom-call(f32[1,128,128]{2,1,0:T(8,128)S(1)} %get-tuple-element.46), custom_call_target="InvertDiagBlocksLowerTriangular" | custom-call | tf_op jit(solution)/shard_map/jit(cholesky)/cholesky | solution.py:71
  319.1 12.1 %cholesky.546 = f32[128,128]{1,0:T(8,128)S(1)} custom-call(f32[128,128]{1,0:T(8,128)S(1)} %cholesky.609), custom_call_target="Cholesky" | custom-call | tf_op jit(solution)/shard_map/jit(cholesky)/cholesky | solution.py:71
  332.5 9.8 %custom-call.72 = f32[1,128,128]{1,2,0:T(8,128)S(1)} custom-call(f32[1,128,128]{2,1,0:T(8,128)S(1)} %get-tuple-element.43), custom_call_target="InvertDiagBlocksLowerTriangular" | custom-call | tf_op jit(solution)/shard_map/jit(cholesky)/cholesky | solution.py:71
  344.9 11.7 %cholesky.564 = f32[128,128]{1,0:T(8,128)S(1)} custom-call(f32[128,128]{1,0:T(8,128)S(1)} %convolution_subtract_fusion.16), custom_call_target="Cholesky" | custom-call | tf_op jit(solution)/shard_map/jit(cholesky)/cholesky | solution.py:71
  368.6 23.6 %while.1 = (s32[]{:T(128)}, f32[1024,1024]{1,0:T(8,128)}, s32[8,2]{0,1:T(2,128)S(1)}, f32[8,128,128]{2,1,0:T(8,128)S(1)}, s32[]{:T(128)}) while((s32[]{:T(128)}, f32[1024,1024]{1,0:T(8,128)}, s32[8,2]{0,1:T(2,128)S(1)}, f32[8,128,128]{2,1,0:T(8,128)S(1)}, s32[]{:T(128)}) %tuple.56), condition=%wide.while_cond, body=%wide.while_body.sunk | while | flops 2 | bytes 131181 | solution.py:72
  392.1 78.8 %custom-call.73 = f32[8,128,128]{1,2,0:T(8,128)S(1)} custom-call(f32[8,128,128]{2,1,0:T(8,128)S(1)} %get-tuple-element.12), custom_call_target="InvertDiagBlocksLowerTriangular" | custom-call | tf_op jit(solution)/shard_map/jit(_cho_solve)/triangular_solve | solution.py:72
  505.8 26.9 %fusion.2 = f32[2048,1024]{1,0:T(8,128)S(1)} fusion(f32[1024,1024]{1,0:T(8,128)S(1)} %constant_dynamic-update-slice_fusion.36, f32[1024,2048]{1,0:T(8,128)S(1)} %bitcast.187), kind=kOutput, calls=%fused_computation.5 | convolution fusion | flops 25771900928 | bytes 20971520 | tf_op jit(solution)/shard_map/dot_general | solution.py:76
  546.2 146.7 %all-to-all-done.2 = f32[16,128,1024]{2,0,1:T(8,128)} async-done(((f32[16,128,1024]{2,0,1:T(8,128)}), f32[16,128,1024]{2,0,1:T(8,128)}, u32[]{:S(2)}, u32[]{:S(2)}) %all-to-all-start.2) | async-done | bytes 8388640 | tf_op jit(solution)/shard_map/all_to_all | solution.py:82
  692.8 9.9 %copy.56 = f32[16,16,8,1024]{3,2,1,0:T(8,128)S(1)} copy(f32[16,16,8,1024]{3,1,2,0:T(8,128)} %bitcast.34) | data formatting | bytes 16777216 | tf_op jit(solution)/shard_map/all_to_all | solution.py:82
  702.7 10.9 %copy.65 = f32[32,8,8,1024]{3,1,2,0:T(8,128)} copy(f32[32,8,8,1024]{3,2,1,0:T(8,128)S(1)} %bitcast.183) | data formatting | bytes 16777216
  713.6 9.0 %copy.57 = f32[8192,256]{1,0:T(8,128)} copy(f32[8192,256]{0,1:T(8,128)} %bitcast.184) | data formatting | bytes 16777216 | tf_op jit(solution)/shard_map/dot_general | solution.py:21
  722.7 14.2 %broadcast_multiply_fusion.1 = f32[256,8,1024]{2,0,1:T(8,128)} fusion(f32[256,8]{0,1:T(8,128)S(1)} %copy.58, f32[8,1024,256]{2,1,0:T(8,128)} %bitcast.180), kind=kOutput, calls=%fused_computation.14 | convolution fusion | flops 6445465600 | bytes 16785408 | tf_op jit(solution)/shard_map/dot_general | solution.py:21
  736.9 11.7 %broadcast_multiply_fusion = f32[256,8,1024]{2,0,1:T(8,128)} fusion(f32[256,8]{0,1:T(8,128)S(1)} %copy.58, f32[8,1024,256]{2,1,0:T(8,128)S(1)} %bitcast.181), kind=kOutput, calls=%fused_computation.13 | convolution fusion | flops 6445465600 | bytes 16785408 | tf_op jit(solution)/shard_map/dot_general | solution.py:24
  748.6 9.1 %copy.59 = f32[256,8,1024]{0,2,1:T(8,128)} copy(f32[256,8,1024]{2,0,1:T(8,128)} %broadcast_multiply_fusion.1) | data formatting | bytes 16777216 | tf_op jit(solution)/shard_map/mul | solution.py:27
  757.7 13.4 %fusion.105 = f32[256,8192]{1,0:T(8,128)} fusion(f32[256,8192]{0,1:T(8,128)} %bitcast.185), kind=kOutput, calls=%fused_computation.136 | convolution fusion | flops 6443368448 | bytes 16777216 | tf_op jit(solution)/shard_map/dot_general | solution.py:33
  771.2 9.1 %copy.60 = f32[256,8,1024]{0,2,1:T(8,128)} copy(f32[256,8,1024]{2,0,1:T(8,128)} %broadcast_multiply_fusion) | data formatting | bytes 16777216 | tf_op jit(solution)/shard_map/mul | solution.py:30
  780.3 23.1 %fusion.1 = bf16[256,8192]{1,0:T(8,128)(2,1)S(1)} fusion(f32[256,8192]{1,0:T(8,128)} %fusion.105, f32[256,8192]{0,1:T(8,128)} %bitcast.182), kind=kOutput, calls=%fused_computation.4 | convolution fusion | flops 6449659904 | bytes 20971520 | tf_op jit(solution)/shard_map/dot_general | solution.py:36
  807.7 57.7 %all_to_all.67 = bf16[256,8,1024]{2,1,0:T(8,128)(2,1)S(1)} all-to-all(bf16[256,8,1024]{2,1,0:T(8,128)(2,1)S(1)} %bitcast.191), channel_id=1, replica_groups=mesh['gz'=16,'gy'=8] {'gz'}, dimensions={0} | all-to-all | bytes 8388608 | tf_op jit(solution)/shard_map/all_to_all | solution.py:84
  (158 shorter events, 173.2 us)
Async XLA Ops:
  0.0 546.0 %copy-start = (f32[256,128]{1,0:T(8,128)S(1)}, f32[256,128]{1,0:T(8,128)}, u32[]{:S(2)}) copy-start(f32[256,128]{1,0:T(8,128)} %param.5) | copy-start | bytes 393220
  39.4 21.3 %all-to-all-start.1 = ((bf16[8,2,32768]{2,1,0:T(2,128)(2,1)}), bf16[8,2,32768]{2,1,0:T(2,128)(2,1)S(1)}, u32[]{:S(2)}, u32[]{:S(2)}) async-start(bf16[8,2,32768]{2,1,0:T(2,128)(2,1)} %reshape.178), calls=%async_computation.1 | async-start | bytes 2097152 | tf_op jit(solution)/shard_map/all_to_all | solution.py:51
  47.7 22.9 %copy-start.5 = (s32[1024]{0:T(1024)S(1)}, s32[1024]{0:T(1024)}, u32[]{:S(2)}) copy-start(s32[1024]{0:T(1024)} %param.4) | copy-start | bytes 12292
  158.2 2.0 copy-start.4
  470.9 3.2 copy-start.2
  473.4 3.6 copy-start.3
  501.3 3.3 slice-start
  503.7 2.2 slice-start.1
  540.8 152.0 %all-to-all-start.2 = ((f32[16,128,1024]{2,0,1:T(8,128)}), f32[16,128,1024]{2,0,1:T(8,128)}, u32[]{:S(2)}, u32[]{:S(2)}) async-start(f32[16,128,1024]{2,0,1:T(8,128)} %copy.54), calls=%async_computation.2 | async-start | bytes 16777216 | tf_op jit(solution)/shard_map/all_to_all | solution.py:82
  722.7 14.3 %copy-start.1 = (f32[8192,256]{1,0:T(8,128)S(1)}, f32[8192,256]{1,0:T(8,128)}, u32[]{:S(2)}) copy-start(f32[8192,256]{1,0:T(8,128)} %copy.57) | copy-start | bytes 25165828
where the time goes:
time: 886 us; the launch traced here: 868 us
  other arithmetic  264 us (30%)
  waiting for transfers between devices  160 us (18%)
  matrix products  155 us (17%)
  blocking collectives  149 us (17%)
  local copies, waits for them, and re-layouts  124 us (14%)
  starting transfers between devices  10.5 us (1%)
    another operation x30, other arithmetic, per_device(): factor = jnp.linalg.cholesky(pair_gram)  173 us
    all_to_all x1, waiting for transfers between devices, per_device(): lax.all_to_all(slab_fields, 'gz', split_axis=1, concat_axis=0, tiled=True)  147 us
    another operation x3, other arithmetic, per_device(): jax.scipy.linalg.cho_solve((factor, True), jnp.eye(point_count, dtype=jnp...  83.7 us
    psum x1, blocking collectives, per_device(): at_points = lax.psum(partial_rows, ('gz', 'gy')).astype(jnp.bfloat16)  67.8 us
    all_to_all x1, blocking collectives, per_device(): lax.all_to_all(potential, 'gz', split_axis=0, concat_axis=1, tiled=True)  57.7 us
    unnamed x39, local copies, waits for them, and re-layouts  33.8 us
    another operation x30, matrix products, per_device(): jax.scipy.linalg.cho_solve((factor, True), jnp.eye(point_count, dtype=jnp...  32.3 us
    dot_general x1, matrix products, per_device(): jnp.dot(sums * sums, inverse, precision=lax.Precision.HIGHEST, preferred_...  26.9 us
  transfers between devices with their start and end apart: 2, of which 2 were waited for; matrix products, arithmetic and copies ran while one was open for 0% of the time, Pallas kernels for 0%

commit v1 on v0

v1 whole, which is shorter than its diff:
```python
import functools
import math

import jax
import jax.numpy as jnp
from jax import lax
from jax.experimental import pallas as pl
from jax.experimental.pallas import tpu as pltpu
from jax.sharding import PartitionSpec as P

FULL = lax.Precision.HIGHEST
F32 = jnp.float32


def point_kernel(orbital_ref, points_ref, out_ref):
    bands, planes, columns = orbital_ref.shape
    points = points_ref[...]
    point_planes = points // columns
    point_columns = points - point_planes * columns
    count = points.shape[1]
    column_pick = (
        lax.broadcasted_iota(jnp.int32, (columns, count), 0) == point_columns
    ).astype(jnp.bfloat16)
    plane_pick = lax.broadcasted_iota(jnp.int32, (planes, count), 0) == point_planes
    for band in range(bands):
        picked = jnp.dot(orbital_ref[band], column_pick, preferred_element_type=F32)
        out_ref[band : band + 1, :] = jnp.sum(
            jnp.where(plane_pick, picked, 0.0), axis=0, keepdims=True
        ).astype(jnp.bfloat16)


def values_at_points(orbitals, points):
    bands = orbitals.shape[0]
    count = points.shape[0]
    return pl.pallas_call(
        point_kernel,
        out_shape=jax.ShapeDtypeStruct((bands, count), jnp.bfloat16),
        compiler_params=pltpu.CompilerParams(vmem_limit_bytes=24 << 20),
        cost_estimate=pl.CostEstimate(
            flops=2 * bands * orbitals.shape[1] * orbitals.shape[2] * count,
            bytes_accessed=orbitals.size * 2,
            transcendentals=0,
        ),
    )(orbitals, points.reshape(1, count))


def small_inverse(block):
    size = block.shape[0]
    lane = lax.broadcasted_iota(jnp.int32, (1, size), 1)
    sub = lax.broadcasted_iota(jnp.int32, (size, 1), 0)
    for j in range(size):
        row = block[j : j + 1, :]
        column = block[:, j : j + 1]
        recip = 1.0 / block[j : j + 1, j : j + 1]
        scaled = jnp.where(lane == j, recip, row * recip)
        rest = jnp.where(lane == j, 0.0, block)
        block = jnp.where(sub == j, scaled, rest - column * scaled)
    return block


def inverse_kernel(width, gram_ref, out_ref):
    size = gram_ref.shape[0]
    blocks = size // width
    dot = functools.partial(jnp.dot, precision=FULL, preferred_element_type=F32)
    out_ref[...] = gram_ref[...]

    def eliminate(k, carry):
        at = pl.ds(pl.multiple_of(k * width, width), width)
        pivot = small_inverse(out_ref[at, at])
        panel = dot(pivot, out_ref[at, :])
        out_ref[at, :] = panel

        def update(i, carry):
            @pl.when(i != k)
            def _():
                rows = pl.ds(pl.multiple_of(i * width, width), width)
                left = out_ref[rows, at]
                out_ref[rows, :] = out_ref[rows, :] - dot(left, panel)
                out_ref[rows, at] = -dot(left, pivot)

            return carry

        lax.fori_loop(0, blocks, update, 0)
        out_ref[at, at] = pivot
        return carry

    lax.fori_loop(0, blocks, eliminate, 0)


def spd_inverse(gram):
    size = gram.shape[0]
    return pl.pallas_call(
        functools.partial(inverse_kernel, 128),
        out_shape=jax.ShapeDtypeStruct(gram.shape, F32),
        compiler_params=pltpu.CompilerParams(vmem_limit_bytes=24 << 20),
        cost_estimate=pl.CostEstimate(
            flops=60 * size**3, bytes_accessed=8 * size * size, transcendentals=0
        ),
    )(gram)


def circulants(kernel):
    planes = kernel.shape[0]
    positions = jnp.arange(planes, dtype=jnp.int32)
    angles = (
        2.0 * math.pi / planes
    ) * (positions[:, None] * positions[None, :] % planes).astype(F32)
    waves = jnp.concatenate([jnp.cos(angles), jnp.sin(angles)], axis=1)
    weights = jnp.concatenate([kernel, kernel], axis=0).T / planes
    return lax.dot_general(
        waves[None] * weights[:, None, :],
        jnp.broadcast_to(waves, (weights.shape[0],) + waves.shape),
        (((2,), (2,)), ((0,), (0,))),
        precision=FULL,
        preferred_element_type=F32,
    )


def per_device(orbitals, points, coulomb):
    gz_count = lax.axis_size("gz")
    col_pencil = coulomb.shape[1] // gz_count
    at_points = lax.all_gather(
        values_at_points(orbitals, points), ("gz", "gy"), axis=0, tiled=True
    )
    blocks = lax.all_to_all(orbitals, "gy", split_axis=2, concat_axis=0, tiled=True)
    pencils = lax.all_to_all(
        jnp.transpose(blocks, (2, 0, 1)), "gz", split_axis=0, concat_axis=1, tiled=True
    )
    pair_base = lax.dot_general(
        at_points, at_points, (((0,), (0,)), ((), ())), preferred_element_type=F32
    )
    inverse = spd_inverse(pair_base * pair_base)
    sums = lax.dot_general(
        pencils, at_points, (((1,), (0,)), ((), ())), preferred_element_type=F32
    )
    kernel = lax.dynamic_slice_in_dim(coulomb, lax.axis_index("gz") * col_pencil, col_pencil, 1)
    smoothed = lax.dot_general(
        circulants(kernel),
        sums * sums,
        (((2,), (1,)), ((0,), (0,))),
        precision=lax.Precision.HIGH,
        preferred_element_type=F32,
    )
    slab = lax.all_to_all(smoothed, "gz", split_axis=1, concat_axis=0, tiled=True)
    slab = jnp.transpose(slab, (1, 0, 2))
    return lax.dot_general(
        slab,
        inverse,
        (((2,), (0,)), ((), ())),
        precision=lax.Precision.HIGH,
        preferred_element_type=F32,
    ).astype(jnp.bfloat16)


def solution(mesh):
    return jax.shard_map(
        per_device,
        mesh=mesh,
        in_specs=(P(("gz", "gy"), None, None), P(), P(None, "gy")),
        out_specs=P("gz", "gy", None),
        check_vma=False,
    )
```

time: 886 us -> 273 us (0.31); the launches traced: 868 us -> 270 us
  other arithmetic: 264 us -> 1.09 us
  Pallas kernels: 0 us -> 130 us
  matrix products: 155 us -> 29 us
  waiting for transfers between devices: 160 us -> 35.7 us
  blocking collectives: 149 us -> 39.9 us
  local copies, waits for them, and re-layouts: 124 us -> 17.2 us
    another operation x33 -> x0, other arithmetic: 256 us -> none  [the longest x30 173 us: per_device(): factor = jnp.linalg.cholesky(pair_gram)]
    pallas_call x0 -> x2, Pallas kernels: none -> 130 us  [the longest x1 129 us: spd_inverse(): pl.pallas_call(functools.partial(inverse_kernel, 128), out_shape=jax.Shap...]
    all_to_all x2 -> x3, waiting for transfers between devices: 160 us -> 35.7 us  [the longest x1 19.9 us: per_device(): lax.all_to_all(smoothed, 'gz', split_axis=1, concat_axis=0, tiled=True)]
    all_to_all x2 -> x0, blocking collectives: 81.5 us -> none  [the longest x1 57.7 us: per_device(): lax.all_to_all(potential, 'gz', split_axis=0, concat_axis=1, tiled=True)]
    dot_general x7 -> x4, matrix products: 96.5 us -> 28.3 us  [the longest x1 17.9 us: per_device(): lax.dot_general(slab, inverse, (((2,), (0,)), ((), ())), precision=lax.Pr...]
    psum x1 -> x0, blocking collectives: 67.8 us -> none  [per_device(): at_points = lax.psum(partial_rows, ('gz', 'gy')).astype(jnp.bfloat16)]
    another operation x44 -> x0, matrix products: 55.3 us -> none  [the longest x30 32.3 us: per_device(): jax.scipy.linalg.cho_solve((factor, True), jnp.eye(point_count, dtype=jnp...]
    all_gather x0 -> x1, blocking collectives: none -> 39.9 us  [per_device(): lax.all_gather(values_at_points(orbitals, points), ('gz', 'gy'), axis=0,...]
  transfers between devices with their start and end apart: 2 -> 3, of which waited for: 2 -> 2; matrix products, arithmetic and copies ran while one was open for 0% -> 3% of each run, Pallas kernels for 0% -> 48%
where the time goes in v1:
time: 273 us; the launch traced here: 270 us
  Pallas kernels  130 us (48%)
  blocking collectives  39.9 us (15%)
  waiting for transfers between devices  35.7 us (13%)
  matrix products  29 us (11%)
  local copies, waits for them, and re-layouts  17.2 us (6%)
  starting transfers between devices  17.2 us (6%)
    pallas_call x1, Pallas kernels, spd_inverse(): pl.pallas_call(functools.partial(inverse_kernel, 128), out_shape=jax.Shap...  129 us
    all_gather x1, blocking collectives, per_device(): lax.all_gather(values_at_points(orbitals, points), ('gz', 'gy'), axis=0,...  39.9 us
    all_to_all x1, waiting for transfers between devices, per_device(): lax.all_to_all(smoothed, 'gz', split_axis=1, concat_axis=0, tiled=True)  19.9 us
    dot_general x1, matrix products, per_device(): lax.dot_general(slab, inverse, (((2,), (0,)), ((), ())), precision=lax.Pr...  17.9 us
    all_to_all x1, waiting for transfers between devices, per_device(): lax.all_to_all(orbitals, 'gy', split_axis=2, concat_axis=0, tiled=True)  15.8 us
    dot_general x1, local copies, waits for them, and re-layouts, per_device(): lax.dot_general(circulants(kernel), sums * sums, (((2,), (1,)), ((0,), (0...  8.31 us
    all_to_all x1, starting transfers between devices, per_device(): lax.all_to_all(jnp.transpose(blocks, (2, 0, 1)), 'gz', split_axis=0, conc...  7.03 us
    unnamed x13, local copies, waits for them, and re-layouts  6.2 us
  transfers between devices with their start and end apart: 3, of which 2 were waited for; matrix products, arithmetic and copies ran while one was open for 3% of the time, Pallas kernels for 48%

profile of v1, /device:TPU:0, one launch (start us, length us, event | category | flops | bytes accessed | tf_op | source)
XLA Modules:
  0.0 270.5 jit_solution(14673273239043826524)
XLA Ops:
  0.0 0.0 copy-start
  0.0 3.7 %copy.29 = bf16[2,256,1024]{1,0,2:T(2,128)(2,1)} copy(bf16[2,256,1024]{2,1,0:T(8,128)(2,1)} %orbital_ref.1) | data formatting | bytes 2097152 | tf_op args[0]
  3.7 5.4 %all-to-all-start = ((bf16[2,256,1024]{1,0,2:T(2,128)(2,1)}), bf16[2,256,1024]{1,0,2:T(2,128)(2,1)S(1)}, u32[]{:S(2)}, u32[]{:S(2)}) async-start(bf16[2,256,1024]{1,0,2:T(2,128)(2,1)} %copy.29), calls=%async_computation | async-start | bytes 2097152 | tf_op jit(solution)/shard_map/all_to_all | solution.py:125
  9.1 0.0 copy-done
  9.1 0.1 constant_dynamic-slice_fusion
  9.2 0.1 copy.41
  9.3 15.8 %all-to-all-done = bf16[2,256,1024]{1,0,2:T(2,128)(2,1)S(1)} async-done(((bf16[2,256,1024]{1,0,2:T(2,128)(2,1)}), bf16[2,256,1024]{1,0,2:T(2,128)(2,1)S(1)}, u32[]{:S(2)}, u32[]{:S(2)}) %all-to-all-start) | async-done | bytes 1048608 | tf_op jit(solution)/shard_map/all_to_all | solution.py:125
  25.1 0.1 copy.30
  25.2 0.7 copy.31
  25.9 1.7 copy.32
  27.6 7.0 %all-to-all-start.1 = ((bf16[128,16,256]{2,1,0:T(8,128)(2,1)}), bf16[128,16,256]{2,1,0:T(8,128)(2,1)S(1)}, u32[]{:S(2)}, u32[]{:S(2)}) async-start(bf16[128,16,256]{2,1,0:T(8,128)(2,1)} %copy.32), calls=%async_computation.1 | async-start | bytes 2097152 | tf_op jit(solution)/shard_map/all_to_all | solution.py:126
  34.7 0.0 copy-done.1
  34.7 0.0 copy-done.2
  34.7 1.7 shard_map.37
  36.3 39.9 %all-gather = bf16[128,2,1024]{2,1,0:T(2,128)(2,1)S(1)} all-gather(bf16[1,2,1024]{2,1,0:T(2,128)(2,1)S(1)} %bitcast.39), channel_id=1, replica_groups=mesh['gz'=16,'gy'=8] {'gz','gy'}, dimensions={0}, use_global_device_ids=true | all-gather | bytes 528384 | tf_op jit(solution)/shard_map/all_gather | solution.py:122
  76.2 0.2 reshape.7
  76.4 1.0 fusion.24
  77.5 0.1 pad_maximum_fusion
  77.5 5.1 %fusion.7 = f32[8,256,256]{2,1,0:T(8,128)} fusion(f32[8,512]{1,0:T(8,128)S(1)} %fusion.26, f32[256,512]{1,0:T(8,128)S(1)} %pad_maximum_fusion), kind=kOutput, calls=%fused_computation.7 | convolution fusion | flops 3222274048 | bytes 2637824 | tf_op jit(solution)/shard_map/dot_general | solution.py:110
  82.7 0.0 all-to-all-done.1
  82.7 0.1 copy.33
  82.8 0.0 copy-start.4
  82.8 1.3 fusion.16
  84.1 0.3 copy-done.4
  84.3 4.0 %fusion.2 = f32[8,256,1024]{2,1,0:T(8,128)S(1)} fusion(f32[8,256,256]{2,1,0:T(8,128)S(1)} %copy-done.4, f32[1024,8,256]{2,0,1:T(8,128)S(1)} %fusion.16), kind=kOutput, calls=%fused_computation.2 | convolution fusion | flops 3223322624 | bytes 18874368 | tf_op jit(solution)/shard_map/dot_general | solution.py:137
  88.3 8.3 %copy.36 = f32[8,256,1024]{2,0,1:T(8,128)} copy(f32[8,256,1024]{2,1,0:T(8,128)S(1)} %fusion.2) | data formatting | bytes 16777216 | tf_op jit(solution)/shard_map/dot_general | solution.py:137
  96.7 4.7 %all-to-all-start.2 = ((f32[8,256,1024]{2,0,1:T(8,128)}), f32[8,256,1024]{2,0,1:T(8,128)}, u32[]{:S(2)}, u32[]{:S(2)}) async-start(f32[8,256,1024]{2,0,1:T(8,128)} %copy.36), calls=%async_computation.2 | async-start | bytes 16777216 | tf_op jit(solution)/shard_map/all_to_all | solution.py:144
  101.4 0.7 convolution_multiply_fusion.gram_ref
  102.1 128.5 %shard_map.38 = f32[1024,1024]{1,0:T(8,128)S(1)} custom-call(f32[1024,1024]{1,0:T(8,128)S(1)} %convolution_multiply_fusion.gram_ref), custom_call_target="tpu_custom_call" | custom-call | flops 64424509440 | bytes 8388608 | tf_op jit(solution)/shard_map/pallas_call | solution.py:92
  230.7 1.9 copy-done.3
  232.6 19.9 %all-to-all-done.2 = f32[8,256,1024]{2,0,1:T(8,128)} async-done(((f32[8,256,1024]{2,0,1:T(8,128)}), f32[8,256,1024]{2,0,1:T(8,128)}, u32[]{:S(2)}, u32[]{:S(2)}) %all-to-all-start.2) | async-done | bytes 8388640 | tf_op jit(solution)/shard_map/all_to_all | solution.py:144
  252.6 17.9 %fusion.9 = bf16[16,128,1024]{2,1,0:T(8,128)(2,1)} fusion(f32[1024,1024]{1,0:T(8,128)} %copy-done.3, f32[8,16,16,1024]{3,0,2,1:T(8,128)} %bitcast.12), kind=kOutput, calls=%fused_computation.9 | convolution fusion | flops 12886999040 | bytes 16777216 | tf_op jit(solution)/shard_map/dot_general | solution.py:146
  (4 shorter events, 0.0 us)
Async XLA Ops:
  0.0 9.1 %copy-start = (f32[256,128]{1,0:T(8,128)S(1)}, f32[256,128]{1,0:T(8,128)}, u32[]{:S(2)}) copy-start(f32[256,128]{1,0:T(8,128)} %param.5) | copy-start | bytes 393220
  3.7 21.4 %all-to-all-start = ((bf16[2,256,1024]{1,0,2:T(2,128)(2,1)}), bf16[2,256,1024]{1,0,2:T(2,128)(2,1)S(1)}, u32[]{:S(2)}, u32[]{:S(2)}) async-start(bf16[2,256,1024]{1,0,2:T(2,128)(2,1)} %copy.29), calls=%async_computation | async-start | bytes 2097152 | tf_op jit(solution)/shard_map/all_to_all | solution.py:125
  9.3 25.4 %copy-start.1 = (bf16[2,256,1024]{2,1,0:T(8,128)(2,1)S(1)}, bf16[2,256,1024]{2,1,0:T(8,128)(2,1)}, u32[]{:S(2)}) copy-start(bf16[2,256,1024]{2,1,0:T(8,128)(2,1)} %orbital_ref.1) | copy-start | bytes 3145732
  9.3 25.4 %copy-start.2 = (s32[1024]{0:T(1024)S(1)}, s32[1024]{0:T(1024)}, u32[]{:S(2)}) copy-start(s32[1024]{0:T(1024)} %param.4) | copy-start | bytes 12292
  27.6 55.0 %all-to-all-start.1 = ((bf16[128,16,256]{2,1,0:T(8,128)(2,1)}), bf16[128,16,256]{2,1,0:T(8,128)(2,1)S(1)}, u32[]{:S(2)}, u32[]{:S(2)}) async-start(bf16[128,16,256]{2,1,0:T(8,128)(2,1)} %copy.32), calls=%async_computation.1 | async-start | bytes 2097152 | tf_op jit(solution)/shard_map/all_to_all | solution.py:126
  82.8 1.6 copy-start.4
  96.7 155.9 %all-to-all-start.2 = ((f32[8,256,1024]{2,0,1:T(8,128)}), f32[8,256,1024]{2,0,1:T(8,128)}, u32[]{:S(2)}, u32[]{:S(2)}) async-start(f32[8,256,1024]{2,0,1:T(8,128)} %copy.36), calls=%async_computation.2 | async-start | bytes 16777216 | tf_op jit(solution)/shard_map/all_to_all | solution.py:144
  230.7 1.9 copy-start.3

commit v2 on v1

v2 whole, which is shorter than its diff:
```python
import functools

import jax
import jax.numpy as jnp
import numpy as np
from jax import lax
from jax.experimental import pallas as pl
from jax.experimental.pallas import tpu as pltpu
from jax.sharding import PartitionSpec as P

FULL = lax.Precision.HIGHEST
F32 = jnp.float32
BF16 = jnp.bfloat16
EARLY = 8


def point_kernel(orbital_ref, points_ref, out_ref):
    bands, planes, columns = orbital_ref.shape
    points = points_ref[...]
    point_planes = points // columns
    point_columns = points - point_planes * columns
    count = points.shape[1]
    column_pick = (
        lax.broadcasted_iota(jnp.int32, (columns, count), 0) == point_columns
    ).astype(jnp.bfloat16)
    plane_pick = lax.broadcasted_iota(jnp.int32, (planes, count), 0) == point_planes
    for band in range(bands):
        picked = jnp.dot(orbital_ref[band], column_pick, preferred_element_type=F32)
        out_ref[band : band + 1, :] = jnp.sum(
            jnp.where(plane_pick, picked, 0.0), axis=0, keepdims=True
        ).astype(jnp.bfloat16)


def values_at_points(orbitals, points):
    bands = orbitals.shape[0]
    count = points.shape[0]
    return pl.pallas_call(
        point_kernel,
        out_shape=jax.ShapeDtypeStruct((bands, count), jnp.bfloat16),
        compiler_params=pltpu.CompilerParams(vmem_limit_bytes=24 << 20),
        cost_estimate=pl.CostEstimate(
            flops=2 * bands * orbitals.shape[1] * orbitals.shape[2] * count,
            bytes_accessed=orbitals.size * 2,
            transcendentals=0,
        ),
    )(orbitals, points.reshape(1, count))


def split_parts(values, count):
    parts = []
    for _ in range(count):
        part = values.astype(BF16)
        parts.append(part)
        values = values - part.astype(F32)
    return parts


def full_dot(left, right):
    high, middle, low = split_parts(left, 3)
    wide = jnp.concatenate([high, high, middle, high, low, middle], axis=1)
    return jnp.dot(wide, full_stack(right), preferred_element_type=F32)


def full_stack(right):
    high, middle, low = split_parts(right, 3)
    return jnp.concatenate([high, middle, high, low, high, middle], axis=0)


def tree_sum(terms):
    while len(terms) > 1:
        terms = [sum(terms[i : i + 2][1:], terms[i]) for i in range(0, len(terms), 2)]
    return terms[0]


def eliminate_rows(rows, first, lane, sub):
    shape = rows.shape
    columns = [jnp.broadcast_to(rows[:, first + j : first + j + 1], shape) for j in range(8)]
    cell = {
        (i, j): jnp.broadcast_to(columns[j][i : i + 1, :], shape)
        for j in range(8)
        for i in range(j + 1)
    }
    for k in range(8):
        recip = 1.0 / cell[k, k]
        side = {i: cell[min(i, k), max(i, k)] for i in range(8) if i != k}
        scaled = {i: side[i] * recip for i in side}
        swept = {}
        for i, j in cell:
            if i == k and j == k:
                swept[i, j] = -recip
            elif i == k or j == k:
                swept[i, j] = scaled[j if i == k else i]
            else:
                swept[i, j] = cell[i, j] - side[i] * scaled[j]
        cell = swept
    inside = (lane >= first) & (lane < first + 8)
    source = [
        jnp.where(
            inside,
            jnp.where(lane == first + j, -1.0, 0.0),
            -jnp.broadcast_to(rows[j : j + 1, :], shape),
        )
        for j in range(8)
    ]
    results = [
        tree_sum([cell[min(i, j), max(i, j)] * source[j] for j in range(8)]) for i in range(8)
    ]
    panel = results[0]
    for i in range(1, 8):
        panel = jnp.where(sub == i, results[i], panel)
    return results, panel, inside


def small_inverse(block):
    size = block.shape[0]
    group_rows = 32
    tiles = [block[i : i + 8, :] for i in range(0, size, 8)]
    lane = lax.broadcasted_iota(jnp.int32, (8, size), 1)
    sub = lax.broadcasted_iota(jnp.int32, (8, size), 0)
    per_group = group_rows // 8
    for start in range(0, size, group_rows):
        group = list(range(start // 8, start // 8 + per_group))
        for at in group:
            results, panel, inside = eliminate_rows(tiles[at], at * 8, lane, sub)
            for step in range(1, per_group):
                other = group[(at - group[0] + step) % per_group]
                terms = [
                    jnp.broadcast_to(tiles[other][:, at * 8 + j : at * 8 + j + 1], (8, size))
                    * results[j]
                    for j in range(8)
                ]
                tiles[other] = jnp.where(inside, 0.0, tiles[other]) - tree_sum(terms)
            tiles[at] = panel
        rest = [i for i in range(len(tiles)) if i not in group]
        panel = jnp.concatenate([tiles[i] for i in group], axis=0)
        stack = jnp.concatenate([tiles[i] for i in rest], axis=0)
        change = full_dot(stack[:, start : start + group_rows], panel)
        wide_lane = lax.broadcasted_iota(jnp.int32, stack.shape, 1)
        in_group = (wide_lane >= start) & (wide_lane < start + group_rows)
        stack = jnp.where(in_group, 0.0, stack) - change
        for place, i in enumerate(rest):
            tiles[i] = stack[place * 8 : place * 8 + 8, :]
    return jnp.concatenate(tiles, axis=0)


def inverse_kernel(width, point_ref, high_ref, low_ref, work):
    size = work.shape[0]
    row_block = 256
    for first in range(0, size, row_block):
        base = lax.dot_general(
            point_ref[:, first : first + row_block],
            point_ref[...],
            (((0,), (0,)), ((), ())),
            preferred_element_type=F32,
        )
        work[first : first + row_block, :] = base * base

    def eliminate(k, carry):
        at = pl.ds(pl.multiple_of(k * width, width), width)
        pivot = small_inverse(work[at, at])
        work[at, :] = full_dot(pivot, work[at, :])
        work[at, at] = pivot
        panel = work[at, :]
        stacked = full_stack(panel)
        for first in range(0, size, row_block):
            rows = slice(first, first + row_block)
            high, middle, low = split_parts(work[rows, at], 3)
            wide = jnp.concatenate([high, high, middle, high, low, middle], axis=1)
            change = jnp.dot(wide, stacked, preferred_element_type=F32)
            work[rows, at] = jnp.zeros((row_block, width), F32)
            work[rows, :] = work[rows, :] - change
        work[at, :] = panel
        return carry

    lax.fori_loop(0, size // width, eliminate, 0)
    for first in range(0, size, row_block):
        rows = slice(first, first + row_block)
        high, low = split_parts(work[rows, :], 2)
        high_ref[rows, :] = high
        low_ref[rows, :] = low


def gram_inverse(at_points):
    size = at_points.shape[1]
    part = jax.ShapeDtypeStruct((size, size), BF16)
    return pl.pallas_call(
        functools.partial(inverse_kernel, 128),
        out_shape=(part, part),
        scratch_shapes=[pltpu.VMEM((size, size), F32)],
        compiler_params=pltpu.CompilerParams(vmem_limit_bytes=28 << 20),
        cost_estimate=pl.CostEstimate(
            flops=60 * size**3, bytes_accessed=8 * size * size, transcendentals=0
        ),
    )(at_points)


def filter_kernel(pencil_ref, point_ref, weight_ref, wave_ref, early_ref, late_ref, circulant):
    col_count, _, planes = pencil_ref.shape
    slabs, early, _, width = early_ref.shape
    late = late_ref.shape[1]

    @pl.when(pl.program_id(0) == 0)
    def _():
        rows = jnp.dot(
            weight_ref[...], wave_ref[...], precision=FULL, preferred_element_type=F32
        ) * (1.0 / planes)
        for c in range(col_count):
            turned = pltpu.roll(
                jnp.broadcast_to(rows[c : c + 1, :], (planes, planes)),
                0,
                1,
                stride=1,
                stride_axis=0,
            )
            high, low = split_parts(turned, 2)
            circulant[c] = jnp.concatenate([high, high, low], axis=1)

    for c in range(col_count):
        sums = lax.dot_general(
            pencil_ref[c], point_ref[...], (((0,), (0,)), ((), ())), preferred_element_type=F32
        )
        high, low = split_parts(sums * sums, 2)
        smooth = jnp.dot(
            circulant[c], jnp.concatenate([high, low, high], axis=0), preferred_element_type=F32
        ).reshape(slabs, early + late, width)
        early_ref[:, :, c, :] = smooth[:, :early]
        late_ref[:, :, c, :] = smooth[:, early:]


def filtered_products(pencils, at_points, weights, slabs, early):
    col_count, bands, planes = pencils.shape
    count = at_points.shape[1]
    late = planes // slabs - early
    angles = 2.0 * np.pi / planes * (np.arange(planes)[:, None] * np.arange(planes) % planes)
    waves = jnp.asarray(np.cos(angles), F32)
    chunk = 256
    return pl.pallas_call(
        filter_kernel,
        grid=(count // chunk,),
        in_specs=[
            pl.BlockSpec(pencils.shape, lambda i: (0, 0, 0)),
            pl.BlockSpec((bands, chunk), lambda i: (0, i)),
            pl.BlockSpec(weights.shape, lambda i: (0, 0)),
            pl.BlockSpec(waves.shape, lambda i: (0, 0)),
        ],
        out_specs=[
            pl.BlockSpec((slabs, early, col_count, chunk), lambda i: (0, 0, 0, i)),
            pl.BlockSpec((slabs, late, col_count, chunk), lambda i: (0, 0, 0, i)),
        ],
        out_shape=[
            jax.ShapeDtypeStruct((slabs, early, col_count, count), F32),
            jax.ShapeDtypeStruct((slabs, late, col_count, count), F32),
        ],
        scratch_shapes=[pltpu.VMEM((col_count, planes, 3 * planes), BF16)],
        compiler_params=pltpu.CompilerParams(vmem_limit_bytes=28 << 20),
        cost_estimate=pl.CostEstimate(
            flops=8 * col_count * planes * bands * count, bytes_accessed=10 << 20, transcendentals=0
        ),
    )(pencils, at_points, weights, waves)


def fit_rows(rows, high_ref, low_ref):
    high, low = split_parts(rows, 2)
    dot = functools.partial(jnp.dot, preferred_element_type=F32)
    return (
        dot(high, high_ref[...]) + (dot(low, high_ref[...]) + dot(high, low_ref[...]))
    ).astype(BF16)


def late_fit_kernel(rows_ref, high_ref, low_ref, out_ref):
    out_ref[...] = fit_rows(rows_ref[...], high_ref, low_ref)


def late_fit(rows, high, low):
    total, count = rows.shape
    block = 256
    whole = pl.BlockSpec((count, count), lambda i: (0, 0))
    return pl.pallas_call(
        late_fit_kernel,
        grid=(total // block,),
        in_specs=[pl.BlockSpec((block, count), lambda i: (i, 0)), whole, whole],
        out_specs=pl.BlockSpec((block, count), lambda i: (i, 0)),
        out_shape=jax.ShapeDtypeStruct(rows.shape, BF16),
        compiler_params=pltpu.CompilerParams(vmem_limit_bytes=24 << 20),
        cost_estimate=pl.CostEstimate(
            flops=6 * total * count * count, bytes_accessed=10 << 20, transcendentals=0
        ),
    )(rows, high, low)


def early_fit_kernel(rows_ref, high_ref, low_ref, out_ref):
    planes, cols, count = out_ref.shape
    rows = jnp.concatenate(
        [rows_ref[:, z].reshape(cols, count) for z in range(planes)], axis=0
    )
    out_ref[...] = fit_rows(rows, high_ref, low_ref).reshape(planes, cols, count)


def early_fit(slab, high, low, total_planes):
    sources, early, col_count, count = slab.shape
    block = 2
    whole = pl.BlockSpec((count, count), lambda i: (0, 0))
    return pl.pallas_call(
        early_fit_kernel,
        grid=(early // block,),
        in_specs=[
            pl.BlockSpec((sources, block, col_count, count), lambda i: (0, i, 0, 0)),
            whole,
            whole,
        ],
        out_specs=pl.BlockSpec((block, sources * col_count, count), lambda i: (i, 0, 0)),
        out_shape=jax.ShapeDtypeStruct((total_planes, sources * col_count, count), BF16),
        compiler_params=pltpu.CompilerParams(vmem_limit_bytes=24 << 20),
        cost_estimate=pl.CostEstimate(
            flops=6 * slab.size * count, bytes_accessed=10 << 20, transcendentals=0
        ),
    )(slab, high, low)


def place_late_kernel(late_ref, _, out_ref):
    planes, cols, count = out_ref.shape
    for z in range(planes):
        out_ref[z] = late_ref[:, z].astype(F32).reshape(cols, count).astype(BF16)


def place_late(late, fitted):
    sources, planes, col_count, count = late.shape
    block = 2
    first = (fitted.shape[0] - planes) // block
    return pl.pallas_call(
        place_late_kernel,
        grid=(planes // block,),
        in_specs=[
            pl.BlockSpec((sources, block, col_count, count), lambda i: (0, i, 0, 0)),
            pl.BlockSpec(memory_space=pl.ANY),
        ],
        out_specs=pl.BlockSpec((block, sources * col_count, count), lambda i: (first + i, 0, 0)),
        out_shape=jax.ShapeDtypeStruct(fitted.shape, BF16),
        input_output_aliases={1: 0},
        compiler_params=pltpu.CompilerParams(vmem_limit_bytes=12 << 20),
        cost_estimate=pl.CostEstimate(flops=0, bytes_accessed=2 * late.size * 2, transcendentals=0),
    )(late, fitted)


def per_device(orbitals, points, coulomb):
    gz_count = lax.axis_size("gz")
    planes, columns = coulomb.shape
    col_pencil = columns // gz_count
    count = points.shape[0]
    slab_planes = planes // gz_count
    early = EARLY
    blocks = lax.all_to_all(orbitals, "gy", split_axis=2, concat_axis=0, tiled=True)
    pencils = lax.all_to_all(
        jnp.transpose(blocks, (2, 0, 1)), "gz", split_axis=0, concat_axis=1, tiled=True
    )
    at_points = lax.all_gather(
        values_at_points(orbitals, points), ("gz", "gy"), axis=0, tiled=True
    )
    weights = lax.dynamic_slice_in_dim(
        coulomb, lax.axis_index("gz") * col_pencil, col_pencil, 1
    ).T
    first, second = filtered_products(pencils, at_points, weights, gz_count, early)
    swap = functools.partial(
        lax.all_to_all, axis_name="gz", split_axis=0, concat_axis=0, tiled=True
    )
    slab = swap(first)
    high, low = gram_inverse(at_points)
    late = late_fit(second.reshape(-1, count), high, low)
    late = swap(late.reshape(gz_count, slab_planes - early, col_pencil, count))
    return place_late(late, early_fit(slab, high, low, slab_planes))


def solution(mesh):
    return jax.shard_map(
        per_device,
        mesh=mesh,
        in_specs=(P(("gz", "gy"), None, None), P(), P(None, "gy")),
        out_specs=P("gz", "gy", None),
        check_vma=False,
    )
```

time: 273 us -> 208 us (0.76)
  Pallas kernels: 130 us -> 92.8 us
  matrix products: 29 us -> 0 us
  blocking collectives: 39.9 us -> 60.8 us
  waiting for transfers between devices: 35.7 us -> 18.5 us
    pallas_call x1 -> x5, Pallas kernels: 129 us -> 91.2 us  [the longest x1 62.4 us: gram_inverse(): pl.pallas_call(functools.partial(inverse_kernel, 128), out_shape=(part, p...]
    dot_general x5 -> x0, matrix products: 29 us -> none  [the longest x1 17.9 us: per_device(): lax.dot_general(slab, inverse, (((2,), (0,)), ((), ())), precision=lax.Pr...]
    all_to_all x0 -> x1, blocking collectives: none -> 21.3 us  [per_device(): lax.all_to_all(orbitals, 'gy', split_axis=2, concat_axis=0, tiled=True)]
    all_to_all x2, waiting for transfers between devices: 35.7 us -> 18.5 us  [the longest x1 18.5 us: per_device(): late = swap(late.reshape(gz_count, slab_planes - early, col_pencil, count))]
    dot_general x1 -> x0, local copies, waits for them, and re-layouts: 8.31 us -> none  [per_device(): lax.dot_general(circulants(kernel), sums * sums, (((2,), (1,)), ((0,), (0...]
    unnamed x13 -> x27, local copies, waits for them, and re-layouts: 6.2 us -> 14 us
  transfers between devices with their start and end apart: 3 -> 3, of which waited for: 2 -> 1; matrix products, arithmetic and copies ran while one was open for 3% -> 0% of each run, Pallas kernels for 48% -> 39%
where the time goes in v2:
time: 208 us
  Pallas kernels  92.8 us (45%)
  blocking collectives  60.8 us (29%)
  starting transfers between devices  18.7 us (9%)
  waiting for transfers between devices  18.5 us (9%)
  local copies, waits for them, and re-layouts  16.7 us (8%)
    pallas_call x1, Pallas kernels, gram_inverse(): pl.pallas_call(functools.partial(inverse_kernel, 128), out_shape=(part, p...  62.4 us
    all_gather x1, blocking collectives, per_device(): lax.all_gather(values_at_points(orbitals, points), ('gz', 'gy'), axis=0,...  39.5 us
    all_to_all x1, blocking collectives, per_device(): lax.all_to_all(orbitals, 'gy', split_axis=2, concat_axis=0, tiled=True)  21.3 us
    all_to_all x1, waiting for transfers between devices, per_device(): late = swap(late.reshape(gz_count, slab_planes - early, col_pencil, count))  18.5 us
    unnamed x27, local copies, waits for them, and re-layouts  14 us
    pallas_call x1, Pallas kernels, filtered_products(): pl.pallas_call(filter_kernel, grid=(count // chunk,), in_specs=[pl.BlockS...  10.3 us
    pallas_call x1, Pallas kernels, early_fit(): pl.pallas_call(early_fit_kernel, grid=(early // block,), in_specs=[pl.Blo...  9.23 us
    pallas_call x1, Pallas kernels, late_fit(): pl.pallas_call(late_fit_kernel, grid=(total // block,), in_specs=[pl.Bloc...  7.18 us
  transfers between devices with their start and end apart: 3, of which 1 were waited for; matrix products, arithmetic and copies ran while one was open for 0% of the time, Pallas kernels for 39%

profile of v2, /device:TPU:0, one launch (start us, length us, event | category | flops | bytes accessed | tf_op | source)
XLA Modules:
  0.0 207.7 jit_solution(18352183142302024206)
XLA Ops:
  0.0 2.5 %copy.15 = bf16[2,256,1024]{1,0,2:T(2,128)(2,1)S(1)} copy(bf16[2,256,1024]{2,1,0:T(8,128)(2,1)} %orbital_ref.1) | data formatting | bytes 2097152 | tf_op args[0]
  2.6 21.3 %all_to_all.46 = bf16[2,256,1024]{1,0,2:T(2,128)(2,1)S(1)} all-to-all(bf16[2,256,1024]{1,0,2:T(2,128)(2,1)S(1)} %copy.15), channel_id=1, replica_groups=mesh['gz'=16,'gy'=8] {'gy'}, dimensions={2} | all-to-all | bytes 2097152 | tf_op jit(solution)/shard_map/all_to_all | solution.py:352
  23.9 0.1 copy.16
  24.0 0.7 copy.17
  24.7 1.7 copy.18
  26.3 7.0 %all-to-all-start.1 = ((bf16[128,16,256]{2,1,0:T(8,128)(2,1)}), bf16[128,16,256]{2,1,0:T(8,128)(2,1)S(1)}, u32[]{:S(2)}, u32[]{:S(2)}) async-start(bf16[128,16,256]{2,1,0:T(8,128)(2,1)} %copy.18), calls=%async_computation.1 | async-start | bytes 2097152 | tf_op jit(solution)/shard_map/all_to_all | solution.py:353
  33.4 0.0 copy-start.7
  33.4 0.1 constant_dynamic-slice_fusion
  33.5 0.1 copy.21
  33.6 1.7 shard_map.46
  35.3 39.5 %all-gather = bf16[128,2,1024]{2,1,0:T(2,128)(2,1)S(1)} all-gather(bf16[1,2,1024]{2,1,0:T(2,128)(2,1)S(1)} %bitcast.18), channel_id=1, replica_groups=mesh['gz'=16,'gy'=8] {'gz','gy'}, dimensions={0}, use_global_device_ids=true | all-gather | bytes 528384 | tf_op jit(solution)/shard_map/all_gather | solution.py:356
  74.8 0.2 reshape.13.point_ref
  75.0 0.0 all-to-all-done.1
  75.0 0.1 copy.19
  75.1 10.3 %shard_map.47 = (f32[16,8,8,1024]{3,2,1,0:T(8,128)S(1)}, f32[16,8,8,1024]{3,2,1,0:T(8,128)S(1)}) custom-call(bf16[8,256,256]{2,1,0:T(8,128)(2,1)S(1)} %bitcast.16, bf16[256,1024]{1,0:T(8,128)(2,1)S(1)} %reshape.13.point_ref, f32[8,256]{1,0:T(8,128)S(1)} %bitcast.17, f32[256,256]{1,0:T(8,128)S(1)} %copy-done.7), custom_call_target="tpu_custom_call" | custom-call | flops 4294967296 | bytes 10485760 | tf_op jit(solution)/shard_map/pallas_call | solution.py:237
  85.5 2.0 copy-done.1
  87.5 2.0 copy-done.5
  89.5 4.7 %all-to-all-start.3 = ((f32[16,8,8,1024]{3,2,1,0:T(8,128)}), f32[16,8,8,1024]{3,2,1,0:T(8,128)}, u32[]{:S(2)}, u32[]{:S(2)}) async-start(f32[16,8,8,1024]{3,2,1,0:T(8,128)} %copy-done.1), calls=%async_computation.3 | async-start | bytes 8388608 | tf_op jit(solution)/shard_map/all_to_all | solution.py:366
  94.2 0.0 copy-start.6
  94.2 62.4 %shard_map.48 = (bf16[1024,1024]{1,0:T(8,128)(2,1)S(1)}, bf16[1024,1024]{1,0:T(8,128)(2,1)S(1)}) custom-call(bf16[256,1024]{1,0:T(8,128)(2,1)S(1)} %reshape.13.point_ref), custom_call_target="tpu_custom_call" | custom-call | flops 64424509440 | bytes 8388608 | tf_op jit(solution)/shard_map/pallas_call | solution.py:186
  156.7 7.2 %shard_map.49 = bf16[1024,1024]{1,0:T(8,128)(2,1)S(1)} custom-call(f32[1024,1024]{1,0:T(8,128)S(1)} %bitcast.20, bf16[1024,1024]{1,0:T(8,128)(2,1)S(1)} %get-tuple-element.10.high_ref, bf16[1024,1024]{1,0:T(8,128)(2,1)S(1)} %get-tuple-element.11.low_ref), custom_call_target="tpu_custom_call" | custom-call | flops 6442450944 | bytes 10485760 | tf_op jit(solution)/shard_map/pallas_call | solution.py:278
  163.9 1.4 copy-done.2
  165.2 1.3 copy-done.8
  166.6 1.3 copy-done.10
  167.9 0.0 all-to-all-done.3.rows_ref
  167.9 6.9 %all-to-all-start.2 = ((bf16[16,8,8,1024]{3,2,1,0:T(8,128)(2,1)}), bf16[16,8,8,1024]{3,2,1,0:T(8,128)(2,1)S(1)}, u32[]{:S(2)}, u32[]{:S(2)}) async-start(bf16[16,8,8,1024]{3,2,1,0:T(8,128)(2,1)} %bitcast.15), calls=%async_computation.2 | async-start | bytes 4194304 | tf_op jit(solution)/shard_map/all_to_all | solution.py:369
  174.8 0.0 copy-start.9
  174.8 1.6 copy-done.9
  176.4 1.6 copy-done.11
  178.0 9.2 %shard_map.50._ = bf16[16,128,1024]{2,1,0:T(8,128)(2,1)} custom-call(f32[16,8,8,1024]{3,2,1,0:T(8,128)} %all-to-all-done.3.rows_ref, bf16[1024,1024]{1,0:T(8,128)(2,1)S(1)} %copy-done.9, bf16[1024,1024]{1,0:T(8,128)(2,1)S(1)} %copy-done.11), custom_call_target="tpu_custom_call" | custom-call | flops 6442450944 | bytes 10485760 | tf_op jit(solution)/shard_map/pallas_call | solution.py:303
  187.2 18.5 %all-to-all-done.2.late_ref = bf16[16,8,8,1024]{3,2,1,0:T(8,128)(2,1)S(1)} async-done(((bf16[16,8,8,1024]{3,2,1,0:T(8,128)(2,1)}), bf16[16,8,8,1024]{3,2,1,0:T(8,128)(2,1)S(1)}, u32[]{:S(2)}, u32[]{:S(2)}) %all-to-all-start.2) | async-done | bytes 2097184 | tf_op jit(solution)/shard_map/all_to_all | solution.py:369
  205.7 1.9 shard_map.51
  (14 shorter events, 0.0 us)
Async XLA Ops:
  0.0 33.4 %copy-start = (f32[256,128]{1,0:T(8,128)S(1)}, f32[256,128]{1,0:T(8,128)}, u32[]{:S(2)}) copy-start(f32[256,128]{1,0:T(8,128)} %param.6) | copy-start | bytes 393220
  23.8 9.7 %copy-start.3 = (bf16[2,256,1024]{2,1,0:T(8,128)(2,1)S(1)}, bf16[2,256,1024]{2,1,0:T(8,128)(2,1)}, u32[]{:S(2)}) copy-start(bf16[2,256,1024]{2,1,0:T(8,128)(2,1)} %orbital_ref.1) | copy-start | bytes 3145732
  23.9 9.7 %copy-start.4 = (s32[1024]{0:T(1024)S(1)}, s32[1024]{0:T(1024)}, u32[]{:S(2)}) copy-start(s32[1024]{0:T(1024)} %param.5) | copy-start | bytes 12292
  26.3 48.7 %all-to-all-start.1 = ((bf16[128,16,256]{2,1,0:T(8,128)(2,1)}), bf16[128,16,256]{2,1,0:T(8,128)(2,1)S(1)}, u32[]{:S(2)}, u32[]{:S(2)}) async-start(bf16[128,16,256]{2,1,0:T(8,128)(2,1)} %copy.18), calls=%async_computation.1 | async-start | bytes 2097152 | tf_op jit(solution)/shard_map/all_to_all | solution.py:353
  33.4 41.7 %copy-start.7 = (f32[256,256]{1,0:T(8,128)S(1)}, f32[256,256]{1,0:T(8,128)}, u32[]{:S(2)}) copy-start(f32[256,256]{1,0:T(8,128)} %constant.14.clone.wave_ref) | copy-start | bytes 786436
  85.5 2.0 copy-start.1
  87.5 2.0 copy-start.5
  89.5 78.4 %all-to-all-start.3 = ((f32[16,8,8,1024]{3,2,1,0:T(8,128)}), f32[16,8,8,1024]{3,2,1,0:T(8,128)}, u32[]{:S(2)}, u32[]{:S(2)}) async-start(f32[16,8,8,1024]{3,2,1,0:T(8,128)} %copy-done.1), calls=%async_computation.3 | async-start | bytes 8388608 | tf_op jit(solution)/shard_map/all_to_all | solution.py:366
  94.2 62.5 %copy-start.6 = (f32[16,8,8,1024]{3,2,1,0:T(8,128)S(1)}, f32[16,8,8,1024]{3,2,1,0:T(8,128)}, u32[]{:S(2)}) copy-start(f32[16,8,8,1024]{3,2,1,0:T(8,128)} %copy-done.5) | copy-start | bytes 12582916
  163.9 1.4 copy-start.2
  165.2 1.3 copy-start.8
  166.6 1.3 copy-start.10
  167.9 37.8 %all-to-all-start.2 = ((bf16[16,8,8,1024]{3,2,1,0:T(8,128)(2,1)}), bf16[16,8,8,1024]{3,2,1,0:T(8,128)(2,1)S(1)}, u32[]{:S(2)}, u32[]{:S(2)}) async-start(bf16[16,8,8,1024]{3,2,1,0:T(8,128)(2,1)} %bitcast.15), calls=%async_computation.2 | async-start | bytes 4194304 | tf_op jit(solution)/shard_map/all_to_all | solution.py:369
  174.8 1.6 copy-start.9
  176.4 1.6 copy-start.11

commit v3 on v2

--- a/solution.py
+++ b/solution.py
@@ -14,7 +14,7 @@
 EARLY = 8
 
 
-def point_kernel(orbital_ref, points_ref, out_ref):
+def pick_points(orbital_ref, points_ref, out_ref):
     bands, planes, columns = orbital_ref.shape
     points = points_ref[...]
     point_planes = points // columns
@@ -22,26 +22,144 @@
     count = points.shape[1]
     column_pick = (
         lax.broadcasted_iota(jnp.int32, (columns, count), 0) == point_columns
-    ).astype(jnp.bfloat16)
+    ).astype(BF16)
     plane_pick = lax.broadcasted_iota(jnp.int32, (planes, count), 0) == point_planes
     for band in range(bands):
         picked = jnp.dot(orbital_ref[band], column_pick, preferred_element_type=F32)
         out_ref[band : band + 1, :] = jnp.sum(
             jnp.where(plane_pick, picked, 0.0), axis=0, keepdims=True
-        ).astype(jnp.bfloat16)
-
-
-def values_at_points(orbitals, points):
-    bands = orbitals.shape[0]
+        ).astype(BF16)
+
+
+def send(source, target, send_sem, recv_sem, device):
+    copy = pltpu.make_async_remote_copy(
+        src_ref=source,
+        dst_ref=target,
+        send_sem=send_sem,
+        recv_sem=recv_sem,
+        device_id=device,
+        device_id_type=pl.DeviceIdType.MESH,
+    )
+    copy.start()
+    return copy
+
+
+def exchange_kernel(
+    gz_count,
+    gy_count,
+    orbital_ref,
+    points_ref,
+    pencil_ref,
+    value_ref,
+    own_blocks,
+    row_blocks,
+    own_values,
+    gy_value_sems,
+    gz_value_sems,
+    gy_block_sems,
+    gz_block_sems,
+    local_sems,
+):
+    gz, gy = lax.axis_index("gz"), lax.axis_index("gy")
+    gy_peers = [lax.rem(gy + d, gy_count) for d in range(1, gy_count)]
+    gz_peers = [lax.rem(gz + d, gz_count) for d in range(1, gz_count)]
+    barrier = pltpu.get_barrier_semaphore()
+    for device in [(gz, peer) for peer in gy_peers] + [(peer, gy) for peer in gz_peers]:
+        pl.semaphore_signal(
+            barrier, inc=1, device_id=device, device_id_type=pl.DeviceIdType.MESH
+        )
+    pick_points(orbital_ref, points_ref, own_values)
+    pl.semaphore_wait(barrier, gy_count + gz_count - 2)
+
+    own_value_copy = pltpu.make_async_copy(own_values, value_ref.at[gz, gy], local_sems.at[0])
+    own_value_copy.start()
+    gy_values = [
+        send(
+            own_values, value_ref.at[gz, gy], gy_value_sems.at[0, i], gy_value_sems.at[1, i], (gz, peer)
+        )
+        for i, peer in enumerate(gy_peers)
+    ]
+
+    bands, planes, columns = orbital_ref.shape
+    _, _, cols, _ = own_blocks.shape
+    width = 256
+    for band in range(bands):
+        for first in range(0, columns, width):
+            turned = orbital_ref[band, :, first : first + width].astype(F32).T
+            own_blocks[first // cols : (first + width) // cols, band] = turned.reshape(
+                width // cols, cols, planes
+            ).astype(BF16)
+    own_rows = pltpu.make_async_copy(
+        own_blocks.at[pl.ds(gy * gz_count, gz_count)], row_blocks.at[gy], local_sems.at[1]
+    )
+    own_rows.start()
+    gy_blocks = [
+        send(
+            own_blocks.at[pl.ds(peer * gz_count, gz_count)],
+            row_blocks.at[gy],
+            gy_block_sems.at[0, i],
+            gy_block_sems.at[1, i],
+            (gz, peer),
+        )
+        for i, peer in enumerate(gy_peers)
+    ]
+
+    own_value_copy.wait()
+    for copy in gy_values:
+        copy.wait_recv()
+    gz_values = [
+        send(
+            value_ref.at[gz], value_ref.at[gz], gz_value_sems.at[0, i], gz_value_sems.at[1, i], (peer, gy)
+        )
+        for i, peer in enumerate(gz_peers)
+    ]
+    own_rows.wait()
+    for copy in gy_blocks:
+        copy.wait_recv()
+    gz_blocks = [
+        send(
+            row_blocks.at[:, peer],
+            pencil_ref.at[gz],
+            gz_block_sems.at[0, i],
+            gz_block_sems.at[1, i],
+            (peer, gy),
+        )
+        for i, peer in enumerate(gz_peers)
+    ]
+    own_pencil = pltpu.make_async_copy(row_blocks.at[:, gz], pencil_ref.at[gz], local_sems.at[2])
+    own_pencil.start()
+    own_pencil.wait()
+    for copy in gy_values + gy_blocks:
+        copy.wait_send()
+    for copy in gz_values + gz_blocks:
+        copy.wait()
+
+
+def exchange(orbitals, points, gz_count, gy_count, cols):
+    bands, planes, columns = orbitals.shape
     count = points.shape[0]
-    return pl.pallas_call(
-        point_kernel,
-        out_shape=jax.ShapeDtypeStruct((bands, count), jnp.bfloat16),
-        compiler_params=pltpu.CompilerParams(vmem_limit_bytes=24 << 20),
-        cost_estimate=pl.CostEstimate(
-            flops=2 * bands * orbitals.shape[1] * orbitals.shape[2] * count,
-            bytes_accessed=orbitals.size * 2,
-            transcendentals=0,
+    vmem = pl.BlockSpec(memory_space=pltpu.VMEM)
+    dma = pltpu.SemaphoreType.DMA
+    return pl.pallas_call(
+        functools.partial(exchange_kernel, gz_count, gy_count),
+        in_specs=[vmem, vmem],
+        out_specs=(vmem, vmem),
+        out_shape=(
+            jax.ShapeDtypeStruct((gz_count, gy_count, bands, cols, planes), BF16),
+            jax.ShapeDtypeStruct((gz_count, gy_count, bands, count), BF16),
+        ),
+        scratch_shapes=[
+            pltpu.VMEM((columns // cols, bands, cols, planes), BF16),
+            pltpu.VMEM((gy_count, gz_count, bands, cols, planes), BF16),
+            pltpu.VMEM((bands, count), BF16),
+            dma((2, gy_count - 1)),
+            dma((2, gz_count - 1)),
+            dma((2, gy_count - 1)),
+            dma((2, gz_count - 1)),
+            dma((3,)),
+        ],
+        compiler_params=pltpu.CompilerParams(
+            collective_id=0, has_side_effects=True, vmem_limit_bytes=24 << 20
         ),
     )(orbitals, points.reshape(1, count))
 
@@ -343,19 +461,15 @@
 
 
 def per_device(orbitals, points, coulomb):
-    gz_count = lax.axis_size("gz")
+    gz_count, gy_count = lax.axis_size("gz"), lax.axis_size("gy")
     planes, columns = coulomb.shape
     col_pencil = columns // gz_count
     count = points.shape[0]
     slab_planes = planes // gz_count
     early = EARLY
-    blocks = lax.all_to_all(orbitals, "gy", split_axis=2, concat_axis=0, tiled=True)
-    pencils = lax.all_to_all(
-        jnp.transpose(blocks, (2, 0, 1)), "gz", split_axis=0, concat_axis=1, tiled=True
-    )
-    at_points = lax.all_gather(
-        values_at_points(orbitals, points), ("gz", "gy"), axis=0, tiled=True
-    )
+    pencils, at_points = exchange(orbitals, points, gz_count, gy_count, col_pencil)
+    at_points = at_points.reshape(-1, count)
+    pencils = jnp.transpose(pencils.reshape(-1, col_pencil, planes), (1, 0, 2))
     weights = lax.dynamic_slice_in_dim(
         coulomb, lax.axis_index("gz") * col_pencil, col_pencil, 1
     ).T

time: 208 us -> 174 us (0.84)
  blocking collectives: 60.8 us -> 0 us
  Pallas kernels: 92.8 us -> 125 us
  starting transfers between devices: 18.7 us -> 14.7 us
  local copies, waits for them, and re-layouts: 16.7 us -> 14.6 us
    all_gather x1 -> x0, blocking collectives: 39.5 us -> none  [per_device(): lax.all_gather(values_at_points(orbitals, points), ('gz', 'gy'), axis=0,...]
    pallas_call x1, Pallas kernels: 1.68 us -> 34.3 us  [exchange(): pl.pallas_call(functools.partial(exchange_kernel, gz_count, gy_count), in...]
    all_to_all x1 -> x0, blocking collectives: 21.3 us -> none  [per_device(): lax.all_to_all(orbitals, 'gy', split_axis=2, concat_axis=0, tiled=True)]
    all_to_all x1 -> x0, starting transfers between devices: 7.03 us -> none  [per_device(): lax.all_to_all(jnp.transpose(blocks, (2, 0, 1)), 'gz', split_axis=0, conc...]
    all_to_all x1, starting transfers between devices: 4.71 us -> 7.6 us  [per_device(): slab = swap(first)]
    unnamed x27 -> x25, local copies, waits for them, and re-layouts: 14 us -> 14.1 us
  transfers between devices with their start and end apart: 3 -> 2, of which waited for: 1 -> 1; matrix products, arithmetic and copies ran while one was open for 0% -> 0% of each run, Pallas kernels for 39% -> 46%
where the time goes in v3:
time: 174 us; the launch traced here: 173 us
  Pallas kernels  125 us (72%)
  waiting for transfers between devices  18.3 us (11%)
  starting transfers between devices  14.7 us (8%)
  local copies, waits for them, and re-layouts  14.6 us (8%)
    pallas_call x1, Pallas kernels, gram_inverse(): pl.pallas_call(functools.partial(inverse_kernel, 128), out_shape=(part, p...  62.4 us
    pallas_call x1, Pallas kernels, exchange(): pl.pallas_call(functools.partial(exchange_kernel, gz_count, gy_count), in...  34.3 us
    all_to_all x1, waiting for transfers between devices, per_device(): late = swap(late.reshape(gz_count, slab_planes - early, col_pencil, count))  18.3 us
    unnamed x25, local copies, waits for them, and re-layouts  14.1 us
    pallas_call x1, Pallas kernels, filtered_products(): pl.pallas_call(filter_kernel, grid=(count // chunk,), in_specs=[pl.BlockS...  10.3 us
    pallas_call x1, Pallas kernels, early_fit(): pl.pallas_call(early_fit_kernel, grid=(early // block,), in_specs=[pl.Blo...  9.23 us
    all_to_all x1, starting transfers between devices, per_device(): slab = swap(first)  7.6 us
    pallas_call x1, Pallas kernels, late_fit(): pl.pallas_call(late_fit_kernel, grid=(total // block,), in_specs=[pl.Bloc...  7.18 us
  transfers between devices with their start and end apart: 2, of which 1 were waited for; matrix products, arithmetic and copies ran while one was open for 0% of the time, Pallas kernels for 46%

profile of v3, /device:TPU:0, one launch (start us, length us, event | category | flops | bytes accessed | tf_op | source)
XLA Modules:
  0.0 173.2 jit_solution(11441622459395663584)
XLA Ops:
  0.0 0.0 copy-start
  0.0 0.0 copy-start.7
  0.0 0.9 copy-done
  0.9 0.1 constant_dynamic-slice_fusion
  1.0 0.1 copy.9
  1.1 1.2 copy-done.3
  2.3 0.7 copy-done.4
  3.0 34.3 %shard_map.46 = (bf16[16,8,2,8,256]{4,3,2,1,0:T(8,128)(2,1)S(1)}, bf16[16,8,2,1024]{3,2,1,0:T(2,128)(2,1)S(1)}) custom-call(bf16[2,256,1024]{2,1,0:T(8,128)(2,1)S(1)} %copy-done.3, s32[1,1024]{1,0:T(1,128)S(1)} %bitcast.12), custom_call_target="tpu_custom_call" | custom-call | tf_op jit(solution)/shard_map/pallas_call | solution.py:143
  37.3 0.2 copy.11
  37.5 0.2 reshape.17.point_ref
  37.7 0.0 copy-done.7
  37.7 10.3 %shard_map.47 = (f32[16,8,8,1024]{3,2,1,0:T(8,128)S(1)}, f32[16,8,8,1024]{3,2,1,0:T(8,128)S(1)}) custom-call(bf16[8,256,256]{2,1,0:T(8,128)(2,1)S(1)} %bitcast.9, bf16[256,1024]{1,0:T(8,128)(2,1)S(1)} %reshape.17.point_ref, f32[8,256]{1,0:T(8,128)S(1)} %bitcast.11, f32[256,256]{1,0:T(8,128)S(1)} %copy-done.7), custom_call_target="tpu_custom_call" | custom-call | flops 4294967296 | bytes 10485760 | tf_op jit(solution)/shard_map/pallas_call | solution.py:355
  48.1 0.0 copy-start.1
  48.1 2.0 %copy-done.1 = f32[16,8,8,1024]{3,2,1,0:T(8,128)} copy-done((f32[16,8,8,1024]{3,2,1,0:T(8,128)}, f32[16,8,8,1024]{3,2,1,0:T(8,128)S(1)}, u32[]{:S(2)}) %copy-start.1) | copy-done | bytes 4194328
  50.1 2.0 %copy-done.5 = f32[16,8,8,1024]{3,2,1,0:T(8,128)} copy-done((f32[16,8,8,1024]{3,2,1,0:T(8,128)}, f32[16,8,8,1024]{3,2,1,0:T(8,128)S(1)}, u32[]{:S(2)}) %copy-start.5) | copy-done | bytes 4194328
  52.1 7.6 %all-to-all-start.1 = ((f32[16,8,8,1024]{3,2,1,0:T(8,128)}), f32[16,8,8,1024]{3,2,1,0:T(8,128)}, u32[]{:S(2)}, u32[]{:S(2)}) async-start(f32[16,8,8,1024]{3,2,1,0:T(8,128)} %copy-done.1), calls=%async_computation.1 | async-start | bytes 8388608 | tf_op jit(solution)/shard_map/all_to_all | solution.py:480
  59.7 0.0 copy-start.6
  59.7 62.4 %shard_map.48 = (bf16[1024,1024]{1,0:T(8,128)(2,1)S(1)}, bf16[1024,1024]{1,0:T(8,128)(2,1)S(1)}) custom-call(bf16[256,1024]{1,0:T(8,128)(2,1)S(1)} %reshape.17.point_ref), custom_call_target="tpu_custom_call" | custom-call | flops 64424509440 | bytes 8388608 | tf_op jit(solution)/shard_map/pallas_call | solution.py:304
  122.2 0.0 copy-done.6
  122.2 7.2 %shard_map.49 = bf16[1024,1024]{1,0:T(8,128)(2,1)S(1)} custom-call(f32[1024,1024]{1,0:T(8,128)S(1)} %bitcast.13, bf16[1024,1024]{1,0:T(8,128)(2,1)S(1)} %get-tuple-element.14.high_ref, bf16[1024,1024]{1,0:T(8,128)(2,1)S(1)} %get-tuple-element.15.low_ref), custom_call_target="tpu_custom_call" | custom-call | flops 6442450944 | bytes 10485760 | tf_op jit(solution)/shard_map/pallas_call | solution.py:396
  129.4 0.0 copy-start.2
  129.4 1.4 copy-done.2
  130.8 1.3 copy-done.8
  132.1 1.3 copy-done.10
  133.4 0.0 all-to-all-done.1.rows_ref
  133.4 7.2 %all-to-all-start = ((bf16[16,8,8,1024]{3,2,1,0:T(8,128)(2,1)}), bf16[16,8,8,1024]{3,2,1,0:T(8,128)(2,1)S(1)}, u32[]{:S(2)}, u32[]{:S(2)}) async-start(bf16[16,8,8,1024]{3,2,1,0:T(8,128)(2,1)} %bitcast.8), calls=%async_computation | async-start | bytes 4194304 | tf_op jit(solution)/shard_map/all_to_all | solution.py:483
  140.6 0.0 copy-start.9
  140.6 1.6 copy-done.9
  142.2 1.6 copy-done.11
  143.7 9.2 %shard_map.50._ = bf16[16,128,1024]{2,1,0:T(8,128)(2,1)} custom-call(f32[16,8,8,1024]{3,2,1,0:T(8,128)} %all-to-all-done.1.rows_ref, bf16[1024,1024]{1,0:T(8,128)(2,1)S(1)} %copy-done.9, bf16[1024,1024]{1,0:T(8,128)(2,1)S(1)} %copy-done.11), custom_call_target="tpu_custom_call" | custom-call | flops 6442450944 | bytes 10485760 | tf_op jit(solution)/shard_map/pallas_call | solution.py:421
  153.0 18.3 %all-to-all-done.late_ref = bf16[16,8,8,1024]{3,2,1,0:T(8,128)(2,1)S(1)} async-done(((bf16[16,8,8,1024]{3,2,1,0:T(8,128)(2,1)}), bf16[16,8,8,1024]{3,2,1,0:T(8,128)(2,1)S(1)}, u32[]{:S(2)}, u32[]{:S(2)}) %all-to-all-start) | async-done | bytes 2097184 | tf_op jit(solution)/shard_map/all_to_all | solution.py:483
  171.3 1.9 %shard_map.51 = bf16[16,128,1024]{2,1,0:T(8,128)(2,1)} custom-call(bf16[16,8,8,1024]{3,2,1,0:T(8,128)(2,1)S(1)} %all-to-all-done.late_ref, bf16[16,128,1024]{2,1,0:T(8,128)(2,1)} %shard_map.50._), custom_call_target="tpu_custom_call", output_to_operand_aliasing={{}: (1, {})} | custom-call | bytes 4194304 | tf_op jit(solution)/shard_map/pallas_call | solution.py:448
  (6 shorter events, 0.0 us)
Async XLA Ops:
  0.0 0.9 copy-start
  0.0 37.7 %copy-start.7 = (f32[256,256]{1,0:T(8,128)S(1)}, f32[256,256]{1,0:T(8,128)}, u32[]{:S(2)}) copy-start(f32[256,256]{1,0:T(8,128)} %constant.14.clone.wave_ref) | copy-start | bytes 786436
  1.1 1.2 copy-start.3
  2.3 0.7 copy-start.4
  48.1 2.0 %copy-start.1 = (f32[16,8,8,1024]{3,2,1,0:T(8,128)}, f32[16,8,8,1024]{3,2,1,0:T(8,128)S(1)}, u32[]{:S(2)}) copy-start(f32[16,8,8,1024]{3,2,1,0:T(8,128)S(1)} %get-tuple-element.16) | copy-start | bytes 12582916
  50.1 2.0 %copy-start.5 = (f32[16,8,8,1024]{3,2,1,0:T(8,128)}, f32[16,8,8,1024]{3,2,1,0:T(8,128)S(1)}, u32[]{:S(2)}) copy-start(f32[16,8,8,1024]{3,2,1,0:T(8,128)S(1)} %get-tuple-element.13) | copy-start | bytes 12582916
  52.1 81.3 %all-to-all-start.1 = ((f32[16,8,8,1024]{3,2,1,0:T(8,128)}), f32[16,8,8,1024]{3,2,1,0:T(8,128)}, u32[]{:S(2)}, u32[]{:S(2)}) async-start(f32[16,8,8,1024]{3,2,1,0:T(8,128)} %copy-done.1), calls=%async_computation.1 | async-start | bytes 8388608 | tf_op jit(solution)/shard_map/all_to_all | solution.py:480
  59.7 62.5 %copy-start.6 = (f32[16,8,8,1024]{3,2,1,0:T(8,128)S(1)}, f32[16,8,8,1024]{3,2,1,0:T(8,128)}, u32[]{:S(2)}) copy-start(f32[16,8,8,1024]{3,2,1,0:T(8,128)} %copy-done.5) | copy-start | bytes 12582916
  129.4 1.4 copy-start.2
  130.8 1.3 copy-start.8
  132.1 1.3 copy-start.10
  133.4 37.9 %all-to-all-start = ((bf16[16,8,8,1024]{3,2,1,0:T(8,128)(2,1)}), bf16[16,8,8,1024]{3,2,1,0:T(8,128)(2,1)S(1)}, u32[]{:S(2)}, u32[]{:S(2)}) async-start(bf16[16,8,8,1024]{3,2,1,0:T(8,128)(2,1)} %bitcast.8), calls=%async_computation | async-start | bytes 4194304 | tf_op jit(solution)/shard_map/all_to_all | solution.py:483
  140.6 1.6 copy-start.9
  142.2 1.6 copy-start.11

commit v4 on v3

--- a/solution.py
+++ b/solution.py
@@ -11,7 +11,7 @@
 FULL = lax.Precision.HIGHEST
 F32 = jnp.float32
 BF16 = jnp.bfloat16
-EARLY = 8
+EARLY = 10
 
 
 def pick_points(orbital_ref, points_ref, out_ref):
@@ -69,69 +69,82 @@
             barrier, inc=1, device_id=device, device_id_type=pl.DeviceIdType.MESH
         )
     pick_points(orbital_ref, points_ref, own_values)
-    pl.semaphore_wait(barrier, gy_count + gz_count - 2)
-
-    own_value_copy = pltpu.make_async_copy(own_values, value_ref.at[gz, gy], local_sems.at[0])
-    own_value_copy.start()
-    gy_values = [
-        send(
-            own_values, value_ref.at[gz, gy], gy_value_sems.at[0, i], gy_value_sems.at[1, i], (gz, peer)
-        )
-        for i, peer in enumerate(gy_peers)
-    ]
-
     bands, planes, columns = orbital_ref.shape
     _, _, cols, _ = own_blocks.shape
     width = 256
     for band in range(bands):
         for first in range(0, columns, width):
             turned = orbital_ref[band, :, first : first + width].astype(F32).T
-            own_blocks[first // cols : (first + width) // cols, band] = turned.reshape(
+            own_blocks[band, first // cols : (first + width) // cols] = turned.reshape(
                 width // cols, cols, planes
             ).astype(BF16)
-    own_rows = pltpu.make_async_copy(
-        own_blocks.at[pl.ds(gy * gz_count, gz_count)], row_blocks.at[gy], local_sems.at[1]
-    )
-    own_rows.start()
-    gy_blocks = [
+    pl.semaphore_wait(barrier, gy_count + gz_count - 2)
+
+    local = [pltpu.make_async_copy(own_values, value_ref.at[gz, gy], local_sems.at[0])]
+    for band in range(bands):
+        local.append(
+            pltpu.make_async_copy(
+                own_blocks.at[band, pl.ds(gy * gz_count, gz_count)],
+                row_blocks.at[band, gy],
+                local_sems.at[1 + band],
+            )
+        )
+    for copy in local:
+        copy.start()
+    gy_values = [
         send(
-            own_blocks.at[pl.ds(peer * gz_count, gz_count)],
-            row_blocks.at[gy],
-            gy_block_sems.at[0, i],
-            gy_block_sems.at[1, i],
-            (gz, peer),
+            own_values, value_ref.at[gz, gy], gy_value_sems.at[0, i], gy_value_sems.at[1, i], (gz, peer)
         )
         for i, peer in enumerate(gy_peers)
     ]
-
-    own_value_copy.wait()
+    gy_blocks = [
+        [
+            send(
+                own_blocks.at[band, pl.ds(peer * gz_count, gz_count)],
+                row_blocks.at[band, gy],
+                gy_block_sems.at[0, band, i],
+                gy_block_sems.at[1, band, i],
+                (gz, peer),
+            )
+            for i, peer in enumerate(gy_peers)
+        ]
+        for band in range(bands)
+    ]
+    for copy in local:
+        copy.wait()
     for copy in gy_values:
         copy.wait_recv()
-    gz_values = [
+    second = [
         send(
             value_ref.at[gz], value_ref.at[gz], gz_value_sems.at[0, i], gz_value_sems.at[1, i], (peer, gy)
         )
         for i, peer in enumerate(gz_peers)
     ]
-    own_rows.wait()
-    for copy in gy_blocks:
-        copy.wait_recv()
-    gz_blocks = [
-        send(
-            row_blocks.at[:, peer],
-            pencil_ref.at[gz],
-            gz_block_sems.at[0, i],
-            gz_block_sems.at[1, i],
-            (peer, gy),
-        )
-        for i, peer in enumerate(gz_peers)
-    ]
-    own_pencil = pltpu.make_async_copy(row_blocks.at[:, gz], pencil_ref.at[gz], local_sems.at[2])
-    own_pencil.start()
-    own_pencil.wait()
-    for copy in gy_values + gy_blocks:
+    own = []
+    for band in range(bands):
+        for copy in gy_blocks[band]:
+            copy.wait_recv()
+        second += [
+            send(
+                row_blocks.at[band, :, peer],
+                pencil_ref.at[band, gz],
+                gz_block_sems.at[0, band, i],
+                gz_block_sems.at[1, band, i],
+                (peer, gy),
+            )
+            for i, peer in enumerate(gz_peers)
+        ]
+        own.append(
+            pltpu.make_async_copy(
+                row_blocks.at[band, :, gz], pencil_ref.at[band, gz], local_sems.at[1 + bands + band]
+            )
+        )
+        own[band].start()
+    for copy in own:
+        copy.wait()
+    for copy in gy_values + sum(gy_blocks, []):
         copy.wait_send()
-    for copy in gz_values + gz_blocks:
+    for copy in second:
         copy.wait()
 
 
@@ -145,18 +158,18 @@
         in_specs=[vmem, vmem],
         out_specs=(vmem, vmem),
         out_shape=(
-            jax.ShapeDtypeStruct((gz_count, gy_count, bands, cols, planes), BF16),
+            jax.ShapeDtypeStruct((bands, gz_count, gy_count, cols, planes), BF16),
             jax.ShapeDtypeStruct((gz_count, gy_count, bands, count), BF16),
         ),
         scratch_shapes=[
-            pltpu.VMEM((columns // cols, bands, cols, planes), BF16),
-            pltpu.VMEM((gy_count, gz_count, bands, cols, planes), BF16),
+            pltpu.VMEM((bands, columns // cols, cols, planes), BF16),
+            pltpu.VMEM((bands, gy_count, gz_count, cols, planes), BF16),
             pltpu.VMEM((bands, count), BF16),
             dma((2, gy_count - 1)),
             dma((2, gz_count - 1)),
-            dma((2, gy_count - 1)),
-            dma((2, gz_count - 1)),
-            dma((3,)),
+            dma((2, bands, gy_count - 1)),
+            dma((2, bands, gz_count - 1)),
+            dma((1 + 2 * bands,)),
         ],
         compiler_params=pltpu.CompilerParams(
             collective_id=0, has_side_effects=True, vmem_limit_bytes=24 << 20
@@ -261,17 +274,17 @@
     return jnp.concatenate(tiles, axis=0)
 
 
-def inverse_kernel(width, point_ref, high_ref, low_ref, work):
+def inverse_kernel(width, point_ref, late_ref, fitted_ref, high_ref, low_ref, work):
     size = work.shape[0]
-    row_block = 256
-    for first in range(0, size, row_block):
+    block = 256
+    for first in range(0, size, block):
         base = lax.dot_general(
-            point_ref[:, first : first + row_block],
+            point_ref[:, first : first + block],
             point_ref[...],
             (((0,), (0,)), ((), ())),
             preferred_element_type=F32,
         )
-        work[first : first + row_block, :] = base * base
+        work[first : first + block, :] = base * base
 
     def eliminate(k, carry):
         at = pl.ds(pl.multiple_of(k * width, width), width)
@@ -280,42 +293,56 @@
         work[at, at] = pivot
         panel = work[at, :]
         stacked = full_stack(panel)
-        for first in range(0, size, row_block):
-            rows = slice(first, first + row_block)
-            high, middle, low = split_parts(work[rows, at], 3)
-            wide = jnp.concatenate([high, high, middle, high, low, middle], axis=1)
-            change = jnp.dot(wide, stacked, preferred_element_type=F32)
-            work[rows, at] = jnp.zeros((row_block, width), F32)
-            work[rows, :] = work[rows, :] - change
+        high, middle, low = split_parts(work[:, at], 3)
+        wide = jnp.concatenate([high, high, middle, high, low, middle], axis=1)
+        work[:, at] = jnp.zeros((size, width), F32)
+        for first in range(0, size, block):
+            columns = slice(first, first + block)
+            change = jnp.dot(wide, stacked[:, columns], preferred_element_type=F32)
+            work[:, columns] = work[:, columns] - change
         work[at, :] = panel
         return carry
 
     lax.fori_loop(0, size // width, eliminate, 0)
-    for first in range(0, size, row_block):
-        rows = slice(first, first + row_block)
+    for first in range(0, size, block):
+        rows = slice(first, first + block)
         high, low = split_parts(work[rows, :], 2)
         high_ref[rows, :] = high
         low_ref[rows, :] = low
-
-
-def gram_inverse(at_points):
+    for first in range(0, late_ref.shape[0], block):
+        rows = slice(first, first + block)
+        fitted_ref[rows, :] = fit_rows(late_ref[rows, :], high_ref, low_ref)
+
+
+def inverse_and_late_fit(at_points, late):
     size = at_points.shape[1]
-    part = jax.ShapeDtypeStruct((size, size), BF16)
+    whole = pl.BlockSpec((size, size), lambda i: (0, 0))
+    rows = pl.BlockSpec(late.shape, lambda i: (0, 0))
     return pl.pallas_call(
         functools.partial(inverse_kernel, 128),
-        out_shape=(part, part),
+        grid=(1,),
+        in_specs=[pl.BlockSpec(at_points.shape, lambda i: (0, 0)), rows],
+        out_specs=(rows, whole, whole),
+        out_shape=(
+            pltpu.HBM(late.shape, BF16),
+            pltpu.HBM((size, size), BF16),
+            pltpu.HBM((size, size), BF16),
+        ),
         scratch_shapes=[pltpu.VMEM((size, size), F32)],
-        compiler_params=pltpu.CompilerParams(vmem_limit_bytes=28 << 20),
+        compiler_params=pltpu.CompilerParams(vmem_limit_bytes=44 << 20),
         cost_estimate=pl.CostEstimate(
             flops=60 * size**3, bytes_accessed=8 * size * size, transcendentals=0
         ),
-    )(at_points)
-
-
-def filter_kernel(pencil_ref, point_ref, weight_ref, wave_ref, early_ref, late_ref, circulant):
+    )(at_points, late)
+
+
+def filter_kernel(
+    slabs, pencil_ref, point_ref, weight_ref, wave_ref, early_ref, late_ref, circulant, natural, ordered
+):
     col_count, _, planes = pencil_ref.shape
-    slabs, early, _, width = early_ref.shape
-    late = late_ref.shape[1]
+    early_rows = early_ref.shape[0]
+    slab_planes, early = planes // slabs, early_rows // slabs
+    late = slab_planes - early
 
     @pl.when(pl.program_id(0) == 0)
     def _():
@@ -323,14 +350,19 @@
             weight_ref[...], wave_ref[...], precision=FULL, preferred_element_type=F32
         ) * (1.0 / planes)
         for c in range(col_count):
-            turned = pltpu.roll(
+            natural[...] = pltpu.roll(
                 jnp.broadcast_to(rows[c : c + 1, :], (planes, planes)),
                 0,
                 1,
                 stride=1,
                 stride_axis=0,
             )
-            high, low = split_parts(turned, 2)
+            for slab in range(slabs):
+                start = slab * slab_planes
+                ordered[slab * early : (slab + 1) * early, :] = natural[start : start + early, :]
+                place = early_rows + slab * late
+                ordered[place : place + late, :] = natural[start + early : start + slab_planes, :]
+            high, low = split_parts(ordered[...], 2)
             circulant[c] = jnp.concatenate([high, high, low], axis=1)
 
     for c in range(col_count):
@@ -340,20 +372,21 @@
         high, low = split_parts(sums * sums, 2)
         smooth = jnp.dot(
             circulant[c], jnp.concatenate([high, low, high], axis=0), preferred_element_type=F32
-        ).reshape(slabs, early + late, width)
-        early_ref[:, :, c, :] = smooth[:, :early]
-        late_ref[:, :, c, :] = smooth[:, early:]
+        )
+        early_ref[:, c, :] = smooth[:early_rows]
+        late_ref[:, c, :] = smooth[early_rows:]
 
 
 def filtered_products(pencils, at_points, weights, slabs, early):
     col_count, bands, planes = pencils.shape
     count = at_points.shape[1]
     late = planes // slabs - early
+    early, late = slabs * early, slabs * late
     angles = 2.0 * np.pi / planes * (np.arange(planes)[:, None] * np.arange(planes) % planes)
     waves = jnp.asarray(np.cos(angles), F32)
     chunk = 256
     return pl.pallas_call(
-        filter_kernel,
+        functools.partial(filter_kernel, slabs),
         grid=(count // chunk,),
         in_specs=[
             pl.BlockSpec(pencils.shape, lambda i: (0, 0, 0)),
@@ -362,14 +395,18 @@
             pl.BlockSpec(waves.shape, lambda i: (0, 0)),
         ],
         out_specs=[
-            pl.BlockSpec((slabs, early, col_count, chunk), lambda i: (0, 0, 0, i)),
-            pl.BlockSpec((slabs, late, col_count, chunk), lambda i: (0, 0, 0, i)),
+            pl.BlockSpec((early, col_count, chunk), lambda i: (0, 0, i)),
+            pl.BlockSpec((late, col_count, chunk), lambda i: (0, 0, i)),
         ],
         out_shape=[
-            jax.ShapeDtypeStruct((slabs, early, col_count, count), F32),
-            jax.ShapeDtypeStruct((slabs, late, col_count, count), F32),
-        ],
-        scratch_shapes=[pltpu.VMEM((col_count, planes, 3 * planes), BF16)],
+            pltpu.HBM((early, col_count, count), F32),
+            pltpu.HBM((late, col_count, count), F32),
+        ],
+        scratch_shapes=[
+            pltpu.VMEM((col_count, planes, 3 * planes), BF16),
+            pltpu.VMEM((planes, planes), F32),
+            pltpu.VMEM((planes, planes), F32),
+        ],
         compiler_params=pltpu.CompilerParams(vmem_limit_bytes=28 << 20),
         cost_estimate=pl.CostEstimate(
             flops=8 * col_count * planes * bands * count, bytes_accessed=10 << 20, transcendentals=0
@@ -383,27 +420,6 @@
     return (
         dot(high, high_ref[...]) + (dot(low, high_ref[...]) + dot(high, low_ref[...]))
     ).astype(BF16)
-
-
-def late_fit_kernel(rows_ref, high_ref, low_ref, out_ref):
-    out_ref[...] = fit_rows(rows_ref[...], high_ref, low_ref)
-
-
-def late_fit(rows, high, low):
-    total, count = rows.shape
-    block = 256
-    whole = pl.BlockSpec((count, count), lambda i: (0, 0))
-    return pl.pallas_call(
-        late_fit_kernel,
-        grid=(total // block,),
-        in_specs=[pl.BlockSpec((block, count), lambda i: (i, 0)), whole, whole],
-        out_specs=pl.BlockSpec((block, count), lambda i: (i, 0)),
-        out_shape=jax.ShapeDtypeStruct(rows.shape, BF16),
-        compiler_params=pltpu.CompilerParams(vmem_limit_bytes=24 << 20),
-        cost_estimate=pl.CostEstimate(
-            flops=6 * total * count * count, bytes_accessed=10 << 20, transcendentals=0
-        ),
-    )(rows, high, low)
 
 
 def early_fit_kernel(rows_ref, high_ref, low_ref, out_ref):
@@ -468,7 +484,7 @@
     slab_planes = planes // gz_count
     early = EARLY
     pencils, at_points = exchange(orbitals, points, gz_count, gy_count, col_pencil)
-    at_points = at_points.reshape(-1, count)
+    at_points = jnp.transpose(at_points, (2, 0, 1, 3)).reshape(-1, count)
     pencils = jnp.transpose(pencils.reshape(-1, col_pencil, planes), (1, 0, 2))
     weights = lax.dynamic_slice_in_dim(
         coulomb, lax.axis_index("gz") * col_pencil, col_pencil, 1
@@ -477,9 +493,8 @@
     swap = functools.partial(
         lax.all_to_all, axis_name="gz", split_axis=0, concat_axis=0, tiled=True
     )
-    slab = swap(first)
-    high, low = gram_inverse(at_points)
-    late = late_fit(second.reshape(-1, count), high, low)
+    slab = swap(first.reshape(gz_count, early, col_pencil, count))
+    late, high, low = inverse_and_late_fit(at_points, second.reshape(-1, count))
     late = swap(late.reshape(gz_count, slab_planes - early, col_pencil, count))
     return place_late(late, early_fit(slab, high, low, slab_planes))
 

time: 174 us -> 174 us (level); the launches traced: 173 us -> 171 us
  local copies, waits for them, and re-layouts: 14.6 us -> 8.38 us
  waiting for transfers between devices: 18.3 us -> 23 us
  Pallas kernels: 125 us -> 122 us
  starting transfers between devices: 14.7 us -> 17.7 us
    all_to_all x1, waiting for transfers between devices: 0.01 us -> 15 us  [per_device(): slab = swap(first.reshape(gz_count, early, col_pencil, count))]
    all_to_all x1, waiting for transfers between devices: 18.3 us -> 7.98 us  [per_device(): late = swap(late.reshape(gz_count, slab_planes - early, col_pencil, count))]
    unnamed x25 -> x15, local copies, waits for them, and re-layouts: 14.1 us -> 7.95 us
    all_to_all x1, starting transfers between devices: 7.15 us -> 10.9 us  [per_device(): late = swap(late.reshape(gz_count, slab_planes - early, col_pencil, count))]
    pallas_call x3 -> x2, Pallas kernels: 80 us -> 76.8 us  [the longest x1 65.4 us: inverse_and_late_fit(): pl.pallas_call(functools.partial(inverse_kernel, 128), grid=(1,), in_spec...]
    pallas_call x1, Pallas kernels: 34.3 us -> 32.1 us  [exchange(): pl.pallas_call(functools.partial(exchange_kernel, gz_count, gy_count), in...]
    pallas_call x1, Pallas kernels: 9.23 us -> 11 us  [early_fit(): pl.pallas_call(early_fit_kernel, grid=(early // block,), in_specs=[pl.Blo...]
  transfers between devices with their start and end apart: 2 -> 2, of which waited for: 1 -> 2; matrix products, arithmetic and copies ran while one was open for 0% -> 0% of each run, Pallas kernels for 46% -> 45%
where the time goes in v4:
time: 174 us; the launch traced here: 171 us
  Pallas kernels  122 us (70%)
  waiting for transfers between devices  23 us (13%)
  starting transfers between devices  17.7 us (10%)
  local copies, waits for them, and re-layouts  8.38 us (5%)
    pallas_call x1, Pallas kernels, inverse_and_late_fit(): pl.pallas_call(functools.partial(inverse_kernel, 128), grid=(1,), in_spec...  65.4 us
    pallas_call x1, Pallas kernels, exchange(): pl.pallas_call(functools.partial(exchange_kernel, gz_count, gy_count), in...  32.1 us
    all_to_all x1, waiting for transfers between devices, per_device(): slab = swap(first.reshape(gz_count, early, col_pencil, count))  15 us
    pallas_call x1, Pallas kernels, filtered_products(): pl.pallas_call(functools.partial(filter_kernel, slabs), grid=(count // ch...  11.4 us
    pallas_call x1, Pallas kernels, early_fit(): pl.pallas_call(early_fit_kernel, grid=(early // block,), in_specs=[pl.Blo...  11 us
    all_to_all x1, starting transfers between devices, per_device(): late = swap(late.reshape(gz_count, slab_planes - early, col_pencil, count))  10.9 us
    all_to_all x1, waiting for transfers between devices, per_device(): late = swap(late.reshape(gz_count, slab_planes - early, col_pencil, count))  7.98 us
    unnamed x15, local copies, waits for them, and re-layouts  7.95 us
  transfers between devices with their start and end apart: 2, of which 2 were waited for; matrix products, arithmetic and copies ran while one was open for 0% of the time, Pallas kernels for 45%

profile of v4, /device:TPU:0, one launch (start us, length us, event | category | flops | bytes accessed | tf_op | source)
XLA Modules:
  0.0 171.0 jit_solution(1934411533548022671)
XLA Ops:
  0.0 0.0 copy-start
  0.0 0.0 copy-start.4
  0.0 0.9 copy-done
  0.9 0.1 constant_dynamic-slice_fusion
  1.0 0.1 copy.9
  1.1 0.0 copy-start.1
  1.1 1.2 copy-done.1
  2.3 0.0 copy-start.2
  2.3 0.7 copy-done.2
  3.0 32.1 %shard_map.46 = (bf16[2,16,8,8,256]{4,3,2,1,0:T(8,128)(2,1)S(1)}, bf16[16,8,2,1024]{3,2,1,0:T(2,128)(2,1)S(1)}) custom-call(bf16[2,256,1024]{2,1,0:T(8,128)(2,1)S(1)} %copy-done.1, s32[1,1024]{1,0:T(1,128)S(1)} %bitcast.15), custom_call_target="tpu_custom_call" | custom-call | tf_op jit(solution)/shard_map/pallas_call | solution.py:156
  35.1 0.1 copy.6
  35.3 0.2 copy.7
  35.5 0.0 copy-done.4
  35.5 11.4 %shard_map.47 = (f32[160,8,1024]{2,1,0:T(8,128)}, f32[96,8,1024]{2,1,0:T(8,128)}) custom-call(bf16[8,256,256]{2,1,0:T(8,128)(2,1)S(1)} %bitcast.10, bf16[256,1024]{1,0:T(8,128)(2,1)S(1)} %bitcast.11, f32[8,256]{1,0:T(8,128)S(1)} %bitcast.14, f32[256,256]{1,0:T(8,128)S(1)} %copy-done.4), custom_call_target="tpu_custom_call" | custom-call | flops 4294967296 | bytes 10485760 | tf_op jit(solution)/shard_map/pallas_call | solution.py:388
  46.9 6.8 %all-to-all-start.1 = ((f32[16,10,8,1024]{3,2,1,0:T(8,128)}), f32[16,10,8,1024]{3,2,1,0:T(8,128)}, u32[]{:S(2)}, u32[]{:S(2)}) async-start(f32[16,10,8,1024]{3,2,1,0:T(8,128)} %bitcast.17), calls=%async_computation.1 | async-start | bytes 10485760 | tf_op jit(solution)/shard_map/all_to_all | solution.py:496
  53.8 0.0 copy-start.3
  53.8 1.9 %copy-done.3 = f32[96,8,1024]{2,1,0:T(8,128)S(1)} copy-done((f32[96,8,1024]{2,1,0:T(8,128)S(1)}, f32[96,8,1024]{2,1,0:T(8,128)}, u32[]{:S(2)}) %copy-start.3) | copy-done | bytes 3145752
  55.7 65.4 %shard_map.48 = (bf16[768,1024]{1,0:T(8,128)(2,1)}, bf16[1024,1024]{1,0:T(8,128)(2,1)}, bf16[1024,1024]{1,0:T(8,128)(2,1)}) custom-call(bf16[256,1024]{1,0:T(8,128)(2,1)S(1)} %bitcast.12, f32[768,1024]{1,0:T(8,128)S(1)} %bitcast.16), custom_call_target="tpu_custom_call" | custom-call | flops 64424509440 | bytes 8388608 | tf_op jit(solution)/shard_map/pallas_call | solution.py:321
  121.1 15.0 %all-to-all-done.1.rows_ref = f32[16,10,8,1024]{3,2,1,0:T(8,128)} async-done(((f32[16,10,8,1024]{3,2,1,0:T(8,128)}), f32[16,10,8,1024]{3,2,1,0:T(8,128)}, u32[]{:S(2)}, u32[]{:S(2)}) %all-to-all-start.1) | async-done | bytes 5242912 | tf_op jit(solution)/shard_map/all_to_all | solution.py:496
  136.1 10.9 %all-to-all-start = ((bf16[16,6,8,1024]{3,2,1,0:T(8,128)(2,1)}), bf16[16,6,8,1024]{3,2,1,0:T(8,128)(2,1)S(1)}, u32[]{:S(2)}, u32[]{:S(2)}) async-start(bf16[16,6,8,1024]{3,2,1,0:T(8,128)(2,1)} %bitcast.18), calls=%async_computation | async-start | bytes 3145728 | tf_op jit(solution)/shard_map/all_to_all | solution.py:498
  147.0 0.0 copy-start.5
  147.0 1.6 copy-done.5
  148.6 0.0 copy-start.6
  148.6 1.6 copy-done.6
  150.2 11.0 %shard_map.49._ = bf16[16,128,1024]{2,1,0:T(8,128)(2,1)} custom-call(f32[16,10,8,1024]{3,2,1,0:T(8,128)} %all-to-all-done.1.rows_ref, bf16[1024,1024]{1,0:T(8,128)(2,1)S(1)} %copy-done.5, bf16[1024,1024]{1,0:T(8,128)(2,1)S(1)} %copy-done.6), custom_call_target="tpu_custom_call" | custom-call | flops 8053063680 | bytes 10485760 | tf_op jit(solution)/shard_map/pallas_call | solution.py:437
  161.2 8.0 %all-to-all-done.late_ref = bf16[16,6,8,1024]{3,2,1,0:T(8,128)(2,1)S(1)} async-done(((bf16[16,6,8,1024]{3,2,1,0:T(8,128)(2,1)}), bf16[16,6,8,1024]{3,2,1,0:T(8,128)(2,1)S(1)}, u32[]{:S(2)}, u32[]{:S(2)}) %all-to-all-start) | async-done | bytes 1572896 | tf_op jit(solution)/shard_map/all_to_all | solution.py:498
  169.2 1.7 %shard_map.50 = bf16[16,128,1024]{2,1,0:T(8,128)(2,1)} custom-call(bf16[16,6,8,1024]{3,2,1,0:T(8,128)(2,1)S(1)} %all-to-all-done.late_ref, bf16[16,128,1024]{2,1,0:T(8,128)(2,1)} %shard_map.49._), custom_call_target="tpu_custom_call", output_to_operand_aliasing={{}: (1, {})} | custom-call | bytes 3145728 | tf_op jit(solution)/shard_map/pallas_call | solution.py:464
Async XLA Ops:
  0.0 0.9 copy-start
  0.0 35.5 %copy-start.4 = (f32[256,256]{1,0:T(8,128)S(1)}, f32[256,256]{1,0:T(8,128)}, u32[]{:S(2)}) copy-start(f32[256,256]{1,0:T(8,128)} %constant.14.clone.wave_ref) | copy-start | bytes 786436
  1.1 1.2 copy-start.1
  2.3 0.7 copy-start.2
  46.9 89.2 %all-to-all-start.1 = ((f32[16,10,8,1024]{3,2,1,0:T(8,128)}), f32[16,10,8,1024]{3,2,1,0:T(8,128)}, u32[]{:S(2)}, u32[]{:S(2)}) async-start(f32[16,10,8,1024]{3,2,1,0:T(8,128)} %bitcast.17), calls=%async_computation.1 | async-start | bytes 10485760 | tf_op jit(solution)/shard_map/all_to_all | solution.py:496
  53.8 1.9 %copy-start.3 = (f32[96,8,1024]{2,1,0:T(8,128)S(1)}, f32[96,8,1024]{2,1,0:T(8,128)}, u32[]{:S(2)}) copy-start(f32[96,8,1024]{2,1,0:T(8,128)} %get-tuple-element.14) | copy-start | bytes 9437188
  136.1 33.1 %all-to-all-start = ((bf16[16,6,8,1024]{3,2,1,0:T(8,128)(2,1)}), bf16[16,6,8,1024]{3,2,1,0:T(8,128)(2,1)S(1)}, u32[]{:S(2)}, u32[]{:S(2)}) async-start(bf16[16,6,8,1024]{3,2,1,0:T(8,128)(2,1)} %bitcast.18), calls=%async_computation | async-start | bytes 3145728 | tf_op jit(solution)/shard_map/all_to_all | solution.py:498
  147.0 1.6 copy-start.5
  148.6 1.6 copy-start.6

commit v5 on v4

--- a/solution.py
+++ b/solution.py
@@ -11,7 +11,7 @@
 FULL = lax.Precision.HIGHEST
 F32 = jnp.float32
 BF16 = jnp.bfloat16
-EARLY = 10
+EARLY = 8
 
 
 def pick_points(orbital_ref, points_ref, out_ref):
@@ -47,17 +47,28 @@
 def exchange_kernel(
     gz_count,
     gy_count,
-    orbital_ref,
+    orbital_hbm,
     points_ref,
+    weight_ref,
+    left_wave_hbm,
+    right_wave_hbm,
     pencil_ref,
     value_ref,
+    circulant_ref,
+    orbital_ref,
+    left_wave_ref,
+    right_wave_ref,
     own_blocks,
-    row_blocks,
+    plane_stage,
+    row_stage,
+    value_stage,
     own_values,
+    gz_value_sems,
     gy_value_sems,
-    gz_value_sems,
-    gy_block_sems,
-    gz_block_sems,
+    gy_first_sems,
+    gz_first_sems,
+    gz_second_sems,
+    gy_second_sems,
     local_sems,
 ):
     gz, gy = lax.axis_index("gz"), lax.axis_index("gy")
@@ -68,113 +79,173 @@
         pl.semaphore_signal(
             barrier, inc=1, device_id=device, device_id_type=pl.DeviceIdType.MESH
         )
+    load = pltpu.make_async_copy(orbital_hbm, orbital_ref, local_sems.at[0])
+    load.start()
+    load_waves = [
+        pltpu.make_async_copy(left_wave_hbm, left_wave_ref, local_sems.at[7]),
+        pltpu.make_async_copy(right_wave_hbm, right_wave_ref, local_sems.at[8]),
+    ]
+    for copy in load_waves:
+        copy.start()
+    load.wait()
     pick_points(orbital_ref, points_ref, own_values)
     bands, planes, columns = orbital_ref.shape
-    _, _, cols, _ = own_blocks.shape
+    half = bands // 2
+    cols = own_blocks.shape[3]
     width = 256
     for band in range(bands):
         for first in range(0, columns, width):
             turned = orbital_ref[band, :, first : first + width].astype(F32).T
-            own_blocks[band, first // cols : (first + width) // cols] = turned.reshape(
-                width // cols, cols, planes
-            ).astype(BF16)
+            at = first // cols
+            own_blocks[band, at // gz_count : (at + width // cols) // gz_count] = (
+                turned.reshape(width // cols // gz_count, gz_count, cols, planes).astype(BF16)
+            )
     pl.semaphore_wait(barrier, gy_count + gz_count - 2)
 
-    local = [pltpu.make_async_copy(own_values, value_ref.at[gz, gy], local_sems.at[0])]
-    for band in range(bands):
-        local.append(
-            pltpu.make_async_copy(
-                own_blocks.at[band, pl.ds(gy * gz_count, gz_count)],
-                row_blocks.at[band, gy],
-                local_sems.at[1 + band],
-            )
-        )
-    for copy in local:
+    own = [
+        pltpu.make_async_copy(own_values, value_stage.at[gz], local_sems.at[1]),
+        pltpu.make_async_copy(
+            own_blocks.at[pl.ds(0, half), gy], plane_stage.at[gy], local_sems.at[2]
+        ),
+        pltpu.make_async_copy(
+            own_blocks.at[pl.ds(half, half), :, gz], row_stage.at[gz], local_sems.at[3]
+        ),
+    ]
+    for copy in own:
         copy.start()
-    gy_values = [
+    values = [
+        send(own_values, value_stage.at[gz], gz_value_sems.at[0, i], gz_value_sems.at[1, i], (peer, gy))
+        for i, peer in enumerate(gz_peers)
+    ]
+    lower = [
         send(
-            own_values, value_ref.at[gz, gy], gy_value_sems.at[0, i], gy_value_sems.at[1, i], (gz, peer)
+            own_blocks.at[pl.ds(0, half), peer],
+            plane_stage.at[gy],
+            gy_first_sems.at[0, i],
+            gy_first_sems.at[1, i],
+            (gz, peer),
         )
         for i, peer in enumerate(gy_peers)
     ]
-    gy_blocks = [
-        [
-            send(
-                own_blocks.at[band, pl.ds(peer * gz_count, gz_count)],
-                row_blocks.at[band, gy],
-                gy_block_sems.at[0, band, i],
-                gy_block_sems.at[1, band, i],
-                (gz, peer),
-            )
-            for i, peer in enumerate(gy_peers)
-        ]
-        for band in range(bands)
-    ]
-    for copy in local:
-        copy.wait()
-    for copy in gy_values:
-        copy.wait_recv()
-    second = [
+    upper = [
         send(
-            value_ref.at[gz], value_ref.at[gz], gz_value_sems.at[0, i], gz_value_sems.at[1, i], (peer, gy)
+            own_blocks.at[pl.ds(half, half), :, peer],
+            row_stage.at[gz],
+            gz_first_sems.at[0, i],
+            gz_first_sems.at[1, i],
+            (peer, gy),
         )
         for i, peer in enumerate(gz_peers)
     ]
-    own = []
-    for band in range(bands):
-        for copy in gy_blocks[band]:
-            copy.wait_recv()
-        second += [
-            send(
-                row_blocks.at[band, :, peer],
-                pencil_ref.at[band, gz],
-                gz_block_sems.at[0, band, i],
-                gz_block_sems.at[1, band, i],
-                (peer, gy),
-            )
-            for i, peer in enumerate(gz_peers)
-        ]
-        own.append(
-            pltpu.make_async_copy(
-                row_blocks.at[band, :, gz], pencil_ref.at[band, gz], local_sems.at[1 + bands + band]
-            )
-        )
-        own[band].start()
     for copy in own:
         copy.wait()
-    for copy in gy_values + sum(gy_blocks, []):
+    for copy in values:
+        copy.wait_recv()
+    values_on = [
+        send(value_stage, value_ref.at[gy], gy_value_sems.at[0, i], gy_value_sems.at[1, i], (gz, peer))
+        for i, peer in enumerate(gy_peers)
+    ]
+    for copy in lower:
+        copy.wait_recv()
+    lower_on = [
+        send(
+            plane_stage.at[:, :, peer],
+            pencil_ref.at[0, gz],
+            gz_second_sems.at[0, i],
+            gz_second_sems.at[1, i],
+            (peer, gy),
+        )
+        for i, peer in enumerate(gz_peers)
+    ]
+    for copy in upper:
+        copy.wait_recv()
+    upper_on = [
+        send(
+            row_stage.at[:, :, peer],
+            pencil_ref.at[1, :, gy],
+            gy_second_sems.at[0, i],
+            gy_second_sems.at[1, i],
+            (gz, peer),
+        )
+        for i, peer in enumerate(gy_peers)
+    ]
+    own_on = [
+        pltpu.make_async_copy(value_stage, value_ref.at[gy], local_sems.at[4]),
+        pltpu.make_async_copy(plane_stage.at[:, :, gz], pencil_ref.at[0, gz], local_sems.at[5]),
+        pltpu.make_async_copy(row_stage.at[:, :, gy], pencil_ref.at[1, :, gy], local_sems.at[6]),
+    ]
+    for copy in own_on:
+        copy.start()
+    for copy in load_waves:
+        copy.wait()
+    for c in range(cols):
+        high, low = split_parts(
+            jnp.dot(
+                left_wave_ref[...] * weight_ref[c : c + 1, :],
+                right_wave_ref[...],
+                precision=FULL,
+                preferred_element_type=F32,
+            ),
+            2,
+        )
+        circulant_ref[c] = jnp.concatenate([high, high, low], axis=1)
+    for copy in own_on:
+        copy.wait()
+    for copy in values + lower + upper:
         copy.wait_send()
-    for copy in second:
+    for copy in values_on + lower_on + upper_on:
         copy.wait()
 
 
-def exchange(orbitals, points, gz_count, gy_count, cols):
+def exchange(orbitals, points, weights, gz_count, gy_count, early):
     bands, planes, columns = orbitals.shape
     count = points.shape[0]
-    vmem = pl.BlockSpec(memory_space=pltpu.VMEM)
+    cols = weights.shape[0]
+    half = bands // 2
+    slab = planes // gz_count
+    z = np.arange(planes)
+    order = z.reshape(gz_count, slab)
+    order = np.concatenate([order[:, :early].ravel(), order[:, early:].ravel()])
+    angles = 2.0 * np.pi / planes * (z[:, None] * z % planes)
+    waves = np.concatenate([np.cos(angles), np.sin(angles)], axis=1)
+    vmem, hbm = (pl.BlockSpec(memory_space=space) for space in (pltpu.VMEM, pltpu.HBM))
     dma = pltpu.SemaphoreType.DMA
     return pl.pallas_call(
         functools.partial(exchange_kernel, gz_count, gy_count),
-        in_specs=[vmem, vmem],
-        out_specs=(vmem, vmem),
+        in_specs=[hbm, vmem, vmem, hbm, hbm],
+        out_specs=(vmem, vmem, vmem),
         out_shape=(
-            jax.ShapeDtypeStruct((bands, gz_count, gy_count, cols, planes), BF16),
-            jax.ShapeDtypeStruct((gz_count, gy_count, bands, count), BF16),
+            jax.ShapeDtypeStruct((2, gz_count, gy_count, half, cols, planes), BF16),
+            jax.ShapeDtypeStruct((gy_count, gz_count, bands, count), BF16),
+            jax.ShapeDtypeStruct((cols, planes, 3 * planes), BF16),
         ),
         scratch_shapes=[
-            pltpu.VMEM((bands, columns // cols, cols, planes), BF16),
+            pltpu.VMEM((bands, planes, columns), BF16),
+            pltpu.VMEM((planes, 2 * planes), F32),
+            pltpu.VMEM((2 * planes, planes), F32),
             pltpu.VMEM((bands, gy_count, gz_count, cols, planes), BF16),
+            pltpu.VMEM((gy_count, half, gz_count, cols, planes), BF16),
+            pltpu.VMEM((gz_count, half, gy_count, cols, planes), BF16),
+            pltpu.VMEM((gz_count, bands, count), BF16),
             pltpu.VMEM((bands, count), BF16),
+            dma((2, gz_count - 1)),
+            dma((2, gy_count - 1)),
             dma((2, gy_count - 1)),
             dma((2, gz_count - 1)),
-            dma((2, bands, gy_count - 1)),
-            dma((2, bands, gz_count - 1)),
-            dma((1 + 2 * bands,)),
+            dma((2, gz_count - 1)),
+            dma((2, gy_count - 1)),
+            dma((9,)),
         ],
         compiler_params=pltpu.CompilerParams(
-            collective_id=0, has_side_effects=True, vmem_limit_bytes=24 << 20
-        ),
-    )(orbitals, points.reshape(1, count))
+            collective_id=0, has_side_effects=True, vmem_limit_bytes=28 << 20
+        ),
+    )(
+        orbitals,
+        points.reshape(1, count),
+        jnp.concatenate([weights, weights], axis=1) * (1.0 / planes),
+        jnp.asarray(waves[order], F32),
+        jnp.asarray(waves.T, F32),
+    )
 
 
 def split_parts(values, count):
@@ -336,63 +407,34 @@
     )(at_points, late)
 
 
-def filter_kernel(
-    slabs, pencil_ref, point_ref, weight_ref, wave_ref, early_ref, late_ref, circulant, natural, ordered
-):
-    col_count, _, planes = pencil_ref.shape
-    early_rows = early_ref.shape[0]
-    slab_planes, early = planes // slabs, early_rows // slabs
-    late = slab_planes - early
-
-    @pl.when(pl.program_id(0) == 0)
-    def _():
-        rows = jnp.dot(
-            weight_ref[...], wave_ref[...], precision=FULL, preferred_element_type=F32
-        ) * (1.0 / planes)
-        for c in range(col_count):
-            natural[...] = pltpu.roll(
-                jnp.broadcast_to(rows[c : c + 1, :], (planes, planes)),
-                0,
-                1,
-                stride=1,
-                stride_axis=0,
-            )
-            for slab in range(slabs):
-                start = slab * slab_planes
-                ordered[slab * early : (slab + 1) * early, :] = natural[start : start + early, :]
-                place = early_rows + slab * late
-                ordered[place : place + late, :] = natural[start + early : start + slab_planes, :]
-            high, low = split_parts(ordered[...], 2)
-            circulant[c] = jnp.concatenate([high, high, low], axis=1)
-
-    for c in range(col_count):
+def filter_kernel(pencil_ref, point_ref, circulant_ref, early_ref, late_ref):
+    early = early_ref.shape[0]
+    for c in range(pencil_ref.shape[0]):
         sums = lax.dot_general(
             pencil_ref[c], point_ref[...], (((0,), (0,)), ((), ())), preferred_element_type=F32
         )
         high, low = split_parts(sums * sums, 2)
         smooth = jnp.dot(
-            circulant[c], jnp.concatenate([high, low, high], axis=0), preferred_element_type=F32
-        )
-        early_ref[:, c, :] = smooth[:early_rows]
-        late_ref[:, c, :] = smooth[early_rows:]
-
-
-def filtered_products(pencils, at_points, weights, slabs, early):
+            circulant_ref[c],
+            jnp.concatenate([high, low, high], axis=0),
+            preferred_element_type=F32,
+        )
+        early_ref[:, c, :] = smooth[:early]
+        late_ref[:, c, :] = smooth[early:]
+
+
+def filtered_products(pencils, at_points, circulant, early):
     col_count, bands, planes = pencils.shape
     count = at_points.shape[1]
-    late = planes // slabs - early
-    early, late = slabs * early, slabs * late
-    angles = 2.0 * np.pi / planes * (np.arange(planes)[:, None] * np.arange(planes) % planes)
-    waves = jnp.asarray(np.cos(angles), F32)
+    late = planes - early
     chunk = 256
     return pl.pallas_call(
-        functools.partial(filter_kernel, slabs),
+        filter_kernel,
         grid=(count // chunk,),
         in_specs=[
             pl.BlockSpec(pencils.shape, lambda i: (0, 0, 0)),
             pl.BlockSpec((bands, chunk), lambda i: (0, i)),
-            pl.BlockSpec(weights.shape, lambda i: (0, 0)),
-            pl.BlockSpec(waves.shape, lambda i: (0, 0)),
+            pl.BlockSpec(circulant.shape, lambda i: (0, 0, 0)),
         ],
         out_specs=[
             pl.BlockSpec((early, col_count, chunk), lambda i: (0, 0, i)),
@@ -402,16 +444,11 @@
             pltpu.HBM((early, col_count, count), F32),
             pltpu.HBM((late, col_count, count), F32),
         ],
-        scratch_shapes=[
-            pltpu.VMEM((col_count, planes, 3 * planes), BF16),
-            pltpu.VMEM((planes, planes), F32),
-            pltpu.VMEM((planes, planes), F32),
-        ],
         compiler_params=pltpu.CompilerParams(vmem_limit_bytes=28 << 20),
         cost_estimate=pl.CostEstimate(
             flops=8 * col_count * planes * bands * count, bytes_accessed=10 << 20, transcendentals=0
         ),
-    )(pencils, at_points, weights, waves)
+    )(pencils, at_points, circulant)
 
 
 def fit_rows(rows, high_ref, low_ref):
@@ -483,13 +520,18 @@
     count = points.shape[0]
     slab_planes = planes // gz_count
     early = EARLY
-    pencils, at_points = exchange(orbitals, points, gz_count, gy_count, col_pencil)
-    at_points = jnp.transpose(at_points, (2, 0, 1, 3)).reshape(-1, count)
-    pencils = jnp.transpose(pencils.reshape(-1, col_pencil, planes), (1, 0, 2))
     weights = lax.dynamic_slice_in_dim(
         coulomb, lax.axis_index("gz") * col_pencil, col_pencil, 1
     ).T
-    first, second = filtered_products(pencils, at_points, weights, gz_count, early)
+    pencils, at_points, circulant = exchange(
+        orbitals, points, weights, gz_count, gy_count, early
+    )
+    bands = orbitals.shape[0]
+    at_points = jnp.transpose(
+        at_points.reshape(gy_count, gz_count, 2, bands // 2, count), (2, 1, 0, 3, 4)
+    ).reshape(-1, count)
+    pencils = jnp.transpose(pencils.reshape(-1, col_pencil, planes), (1, 0, 2))
+    first, second = filtered_products(pencils, at_points, circulant, gz_count * early)
     swap = functools.partial(
         lax.all_to_all, axis_name="gz", split_axis=0, concat_axis=0, tiled=True
     )

time: 174 us -> 158 us (0.908); the launches traced: 171 us -> 158 us
  starting transfers between devices: 17.7 us -> 11.6 us
  Pallas kernels: 122 us -> 117 us
  waiting for transfers between devices: 23 us -> 18.4 us
  local copies, waits for them, and re-layouts: 8.38 us -> 10.9 us
    all_to_all x1, waiting for transfers between devices: 15 us -> 0.01 us  [per_device(): slab = swap(first.reshape(gz_count, early, col_pencil, count))]
    all_to_all x1, waiting for transfers between devices: 7.98 us -> 18.4 us  [per_device(): late = swap(late.reshape(gz_count, slab_planes - early, col_pencil, count))]
    pallas_call x1, Pallas kernels: 32.1 us -> 27.7 us  [exchange(): pl.pallas_call(functools.partial(exchange_kernel, gz_count, gy_count), in...]
    all_to_all x1, starting transfers between devices: 10.9 us -> 6.92 us  [per_device(): late = swap(late.reshape(gz_count, slab_planes - early, col_pencil, count))]
    unnamed x15 -> x17, local copies, waits for them, and re-layouts: 7.95 us -> 10.3 us
    all_to_all x1, starting transfers between devices: 6.84 us -> 4.73 us  [per_device(): slab = swap(first.reshape(gz_count, early, col_pencil, count))]
    pallas_call x1, Pallas kernels: 11 us -> 9.23 us  [early_fit(): pl.pallas_call(early_fit_kernel, grid=(early // block,), in_specs=[pl.Blo...]
    pallas_call x1, Pallas kernels: 65.4 us -> 67.2 us  [inverse_and_late_fit(): pl.pallas_call(functools.partial(inverse_kernel, 128), grid=(1,), in_spec...]
  transfers between devices with their start and end apart: 2 -> 2, of which waited for: 2 -> 1; matrix products, arithmetic and copies ran while one was open for 0% -> 0% of each run, Pallas kernels for 45% -> 49%
where the time goes in v5:
time: 158 us
  Pallas kernels  117 us (74%)
  waiting for transfers between devices  18.4 us (12%)
  starting transfers between devices  11.6 us (7%)
  local copies, waits for them, and re-layouts  10.9 us (7%)
    pallas_call x1, Pallas kernels, inverse_and_late_fit(): pl.pallas_call(functools.partial(inverse_kernel, 128), grid=(1,), in_spec...  67.2 us
    pallas_call x1, Pallas kernels, exchange(): pl.pallas_call(functools.partial(exchange_kernel, gz_count, gy_count), in...  27.7 us
    all_to_all x1, waiting for transfers between devices, per_device(): late = swap(late.reshape(gz_count, slab_planes - early, col_pencil, count))  18.4 us
    pallas_call x1, Pallas kernels, filtered_products(): pl.pallas_call(filter_kernel, grid=(count // chunk,), in_specs=[pl.BlockS...  10.5 us
    unnamed x17, local copies, waits for them, and re-layouts  10.3 us
    pallas_call x1, Pallas kernels, early_fit(): pl.pallas_call(early_fit_kernel, grid=(early // block,), in_specs=[pl.Blo...  9.23 us
    all_to_all x1, starting transfers between devices, per_device(): late = swap(late.reshape(gz_count, slab_planes - early, col_pencil, count))  6.92 us
    all_to_all x1, starting transfers between devices, per_device(): slab = swap(first.reshape(gz_count, early, col_pencil, count))  4.73 us
  transfers between devices with their start and end apart: 2, of which 1 were waited for; matrix products, arithmetic and copies ran while one was open for 0% of the time, Pallas kernels for 49%

profile of v5, /device:TPU:0, one launch (start us, length us, event | category | flops | bytes accessed | tf_op | source)
XLA Modules:
  0.0 157.6 jit_solution(15112651446276479680)
XLA Ops:
  0.0 0.0 copy-start
  0.0 0.9 copy-done
  0.9 0.1 constant_dynamic-slice_fusion
  1.0 0.1 copy.10
  1.1 0.0 copy-start.1
  1.1 1.2 copy-done.1
  2.3 0.0 copy-start.2
  2.3 1.0 copy-done.2
  3.4 0.0 copy-start.3
  3.4 1.0 copy-done.3
  4.4 0.0 copy-start.4
  4.4 0.7 copy-done.4
  5.1 27.7 %shard_map.55 = (bf16[2,16,8,1,8,256]{5,4,3,2,1,0:T(8,128)(2,1)S(1)}, bf16[8,16,2,1024]{3,2,1,0:T(2,128)(2,1)S(1)}, bf16[8,256,768]{2,1,0:T(8,128)(2,1)S(1)}) custom-call(bf16[2,256,1024]{2,1,0:T(8,128)(2,1)S(1)} %copy-done.1, s32[1,1024]{1,0:T(1,128)S(1)} %bitcast.16, f32[8,512]{1,0:T(8,128)S(1)} %maximum_multiply_fusion.weight_ref, ...), custom_call_target="tpu_custom_call" | custom-call | tf_op jit(solution)/shard_map/pallas_call | solution.py:213
  32.8 0.3 copy.8
  33.1 0.2 copy.9
  33.3 10.5 %shard_map.56 = (f32[128,8,1024]{2,1,0:T(8,128)}, f32[128,8,1024]{2,1,0:T(8,128)}) custom-call(bf16[8,256,256]{2,1,0:T(8,128)(2,1)S(1)} %bitcast.12, bf16[256,1024]{1,0:T(8,128)(2,1)S(1)} %bitcast.13, bf16[8,256,768]{2,1,0:T(8,128)(2,1)S(1)} %get-tuple-element.15.circulant_ref), custom_call_target="tpu_custom_call" | custom-call | flops 4294967296 | bytes 10485760 | tf_op jit(solution)/shard_map/pallas_call | solution.py:431
  43.8 4.7 %all-to-all-start.1 = ((f32[16,8,8,1024]{3,2,1,0:T(8,128)}), f32[16,8,8,1024]{3,2,1,0:T(8,128)}, u32[]{:S(2)}, u32[]{:S(2)}) async-start(f32[16,8,8,1024]{3,2,1,0:T(8,128)} %bitcast.18), calls=%async_computation.1 | async-start | bytes 8388608 | tf_op jit(solution)/shard_map/all_to_all | solution.py:538
  48.5 0.0 copy-start.5
  48.5 2.2 %copy-done.5 = f32[128,8,1024]{2,1,0:T(8,128)S(1)} copy-done((f32[128,8,1024]{2,1,0:T(8,128)S(1)}, f32[128,8,1024]{2,1,0:T(8,128)}, u32[]{:S(2)}) %copy-start.5) | copy-done | bytes 4194328
  50.7 67.2 %shard_map.57 = (bf16[1024,1024]{1,0:T(8,128)(2,1)}, bf16[1024,1024]{1,0:T(8,128)(2,1)}, bf16[1024,1024]{1,0:T(8,128)(2,1)}) custom-call(bf16[256,1024]{1,0:T(8,128)(2,1)S(1)} %bitcast.14, f32[1024,1024]{1,0:T(8,128)S(1)} %bitcast.17), custom_call_target="tpu_custom_call" | custom-call | flops 64424509440 | bytes 8388608 | tf_op jit(solution)/shard_map/pallas_call | solution.py:392
  118.0 0.0 all-to-all-done.1.rows_ref
  118.0 6.9 %all-to-all-start = ((bf16[16,8,8,1024]{3,2,1,0:T(8,128)(2,1)}), bf16[16,8,8,1024]{3,2,1,0:T(8,128)(2,1)S(1)}, u32[]{:S(2)}, u32[]{:S(2)}) async-start(bf16[16,8,8,1024]{3,2,1,0:T(8,128)(2,1)} %bitcast.19), calls=%async_computation | async-start | bytes 4194304 | tf_op jit(solution)/shard_map/all_to_all | solution.py:540
  124.9 0.0 copy-start.6
  124.9 1.6 %copy-done.6 = bf16[1024,1024]{1,0:T(8,128)(2,1)S(1)} copy-done((bf16[1024,1024]{1,0:T(8,128)(2,1)S(1)}, bf16[1024,1024]{1,0:T(8,128)(2,1)}, u32[]{:S(2)}) %copy-start.6) | copy-done | bytes 2097176
  126.5 0.0 copy-start.7
  126.5 1.6 %copy-done.7 = bf16[1024,1024]{1,0:T(8,128)(2,1)S(1)} copy-done((bf16[1024,1024]{1,0:T(8,128)(2,1)S(1)}, bf16[1024,1024]{1,0:T(8,128)(2,1)}, u32[]{:S(2)}) %copy-start.7) | copy-done | bytes 2097176
  128.1 9.2 %shard_map.58._ = bf16[16,128,1024]{2,1,0:T(8,128)(2,1)} custom-call(f32[16,8,8,1024]{3,2,1,0:T(8,128)} %all-to-all-done.1.rows_ref, bf16[1024,1024]{1,0:T(8,128)(2,1)S(1)} %copy-done.6, bf16[1024,1024]{1,0:T(8,128)(2,1)S(1)} %copy-done.7), custom_call_target="tpu_custom_call" | custom-call | flops 6442450944 | bytes 10485760 | tf_op jit(solution)/shard_map/pallas_call | solution.py:474
  137.3 18.4 %all-to-all-done.late_ref = bf16[16,8,8,1024]{3,2,1,0:T(8,128)(2,1)S(1)} async-done(((bf16[16,8,8,1024]{3,2,1,0:T(8,128)(2,1)}), bf16[16,8,8,1024]{3,2,1,0:T(8,128)(2,1)S(1)}, u32[]{:S(2)}, u32[]{:S(2)}) %all-to-all-start) | async-done | bytes 2097184 | tf_op jit(solution)/shard_map/all_to_all | solution.py:540
  155.7 1.9 %shard_map.59 = bf16[16,128,1024]{2,1,0:T(8,128)(2,1)} custom-call(bf16[16,8,8,1024]{3,2,1,0:T(8,128)(2,1)S(1)} %all-to-all-done.late_ref, bf16[16,128,1024]{2,1,0:T(8,128)(2,1)} %shard_map.58._), custom_call_target="tpu_custom_call", output_to_operand_aliasing={{}: (1, {})} | custom-call | bytes 4194304 | tf_op jit(solution)/shard_map/pallas_call | solution.py:501
  (1 shorter events, 0.0 us)
Async XLA Ops:
  0.0 0.9 copy-start
  1.1 1.2 copy-start.1
  2.3 1.0 copy-start.2
  3.4 1.0 copy-start.3
  4.4 0.7 copy-start.4
  43.8 74.2 %all-to-all-start.1 = ((f32[16,8,8,1024]{3,2,1,0:T(8,128)}), f32[16,8,8,1024]{3,2,1,0:T(8,128)}, u32[]{:S(2)}, u32[]{:S(2)}) async-start(f32[16,8,8,1024]{3,2,1,0:T(8,128)} %bitcast.18), calls=%async_computation.1 | async-start | bytes 8388608 | tf_op jit(solution)/shard_map/all_to_all | solution.py:538
  48.5 2.2 %copy-start.5 = (f32[128,8,1024]{2,1,0:T(8,128)S(1)}, f32[128,8,1024]{2,1,0:T(8,128)}, u32[]{:S(2)}) copy-start(f32[128,8,1024]{2,1,0:T(8,128)} %get-tuple-element.16) | copy-start | bytes 12582916
  118.0 37.7 %all-to-all-start = ((bf16[16,8,8,1024]{3,2,1,0:T(8,128)(2,1)}), bf16[16,8,8,1024]{3,2,1,0:T(8,128)(2,1)S(1)}, u32[]{:S(2)}, u32[]{:S(2)}) async-start(bf16[16,8,8,1024]{3,2,1,0:T(8,128)(2,1)} %bitcast.19), calls=%async_computation | async-start | bytes 4194304 | tf_op jit(solution)/shard_map/all_to_all | solution.py:540
  124.9 1.6 %copy-start.6 = (bf16[1024,1024]{1,0:T(8,128)(2,1)S(1)}, bf16[1024,1024]{1,0:T(8,128)(2,1)}, u32[]{:S(2)}) copy-start(bf16[1024,1024]{1,0:T(8,128)(2,1)} %get-tuple-element.19.high_ref) | copy-start | bytes 6291460
  126.5 1.6 %copy-start.7 = (bf16[1024,1024]{1,0:T(8,128)(2,1)S(1)}, bf16[1024,1024]{1,0:T(8,128)(2,1)}, u32[]{:S(2)}) copy-start(bf16[1024,1024]{1,0:T(8,128)(2,1)} %get-tuple-element.20.low_ref) | copy-start | bytes 6291460

commit v6 on v5

--- a/solution.py
+++ b/solution.py
@@ -12,6 +12,10 @@
 F32 = jnp.float32
 BF16 = jnp.bfloat16
 EARLY = 8
+
+
+def in_hbm(array):
+    return pltpu.with_memory_space_constraint(array, pltpu.HBM)
 
 
 def pick_points(orbital_ref, points_ref, out_ref):
@@ -240,11 +244,11 @@
             collective_id=0, has_side_effects=True, vmem_limit_bytes=28 << 20
         ),
     )(
-        orbitals,
+        in_hbm(orbitals),
         points.reshape(1, count),
         jnp.concatenate([weights, weights], axis=1) * (1.0 / planes),
-        jnp.asarray(waves[order], F32),
-        jnp.asarray(waves.T, F32),
+        in_hbm(jnp.asarray(waves[order], F32)),
+        in_hbm(jnp.asarray(waves.T, F32)),
     )
 
 
@@ -348,50 +352,55 @@
 def inverse_kernel(width, point_ref, late_ref, fitted_ref, high_ref, low_ref, work):
     size = work.shape[0]
     block = 256
-    for first in range(0, size, block):
-        base = lax.dot_general(
-            point_ref[:, first : first + block],
-            point_ref[...],
-            (((0,), (0,)), ((), ())),
-            preferred_element_type=F32,
-        )
-        work[first : first + block, :] = base * base
-
-    def eliminate(k, carry):
-        at = pl.ds(pl.multiple_of(k * width, width), width)
-        pivot = small_inverse(work[at, at])
-        work[at, :] = full_dot(pivot, work[at, :])
-        work[at, at] = pivot
-        panel = work[at, :]
-        stacked = full_stack(panel)
-        high, middle, low = split_parts(work[:, at], 3)
-        wide = jnp.concatenate([high, high, middle, high, low, middle], axis=1)
-        work[:, at] = jnp.zeros((size, width), F32)
+
+    @pl.when(pl.program_id(0) == 0)
+    def _():
         for first in range(0, size, block):
-            columns = slice(first, first + block)
-            change = jnp.dot(wide, stacked[:, columns], preferred_element_type=F32)
-            work[:, columns] = work[:, columns] - change
-        work[at, :] = panel
-        return carry
-
-    lax.fori_loop(0, size // width, eliminate, 0)
-    for first in range(0, size, block):
-        rows = slice(first, first + block)
-        high, low = split_parts(work[rows, :], 2)
-        high_ref[rows, :] = high
-        low_ref[rows, :] = low
-    for first in range(0, late_ref.shape[0], block):
-        rows = slice(first, first + block)
-        fitted_ref[rows, :] = fit_rows(late_ref[rows, :], high_ref, low_ref)
+            base = lax.dot_general(
+                point_ref[:, first : first + block],
+                point_ref[...],
+                (((0,), (0,)), ((), ())),
+                preferred_element_type=F32,
+            )
+            work[first : first + block, :] = base * base
+
+        def eliminate(k, carry):
+            at = pl.ds(pl.multiple_of(k * width, width), width)
+            pivot = small_inverse(work[at, at])
+            work[at, :] = full_dot(pivot, work[at, :])
+            work[at, at] = pivot
+            panel = work[at, :]
+            stacked = full_stack(panel)
+            high, middle, low = split_parts(work[:, at], 3)
+            wide = jnp.concatenate([high, high, middle, high, low, middle], axis=1)
+            work[:, at] = jnp.zeros((size, width), F32)
+            for first in range(0, size, block):
+                columns = slice(first, first + block)
+                change = jnp.dot(wide, stacked[:, columns], preferred_element_type=F32)
+                work[:, columns] = work[:, columns] - change
+            work[at, :] = panel
+            return carry
+
+        lax.fori_loop(0, size // width, eliminate, 0)
+        for first in range(0, size, block):
+            rows = slice(first, first + block)
+            high, low = split_parts(work[rows, :], 2)
+            high_ref[rows, :] = high
+            low_ref[rows, :] = low
+
+    @pl.when(pl.program_id(0) > 0)
+    def _():
+        fitted_ref[...] = fit_rows(late_ref[...], high_ref, low_ref)
 
 
 def inverse_and_late_fit(at_points, late):
     size = at_points.shape[1]
+    block = 256
     whole = pl.BlockSpec((size, size), lambda i: (0, 0))
-    rows = pl.BlockSpec(late.shape, lambda i: (0, 0))
+    rows = pl.BlockSpec((block, size), lambda i: (jnp.maximum(i - 1, 0), 0))
     return pl.pallas_call(
         functools.partial(inverse_kernel, 128),
-        grid=(1,),
+        grid=(1 + late.shape[0] // block,),
         in_specs=[pl.BlockSpec(at_points.shape, lambda i: (0, 0)), rows],
         out_specs=(rows, whole, whole),
         out_shape=(
@@ -400,20 +409,28 @@
             pltpu.HBM((size, size), BF16),
         ),
         scratch_shapes=[pltpu.VMEM((size, size), F32)],
-        compiler_params=pltpu.CompilerParams(vmem_limit_bytes=44 << 20),
+        compiler_params=pltpu.CompilerParams(vmem_limit_bytes=36 << 20),
         cost_estimate=pl.CostEstimate(
             flops=60 * size**3, bytes_accessed=8 * size * size, transcendentals=0
         ),
-    )(at_points, late)
+    )(at_points, in_hbm(late))
 
 
 def filter_kernel(pencil_ref, point_ref, circulant_ref, early_ref, late_ref):
     early = early_ref.shape[0]
-    for c in range(pencil_ref.shape[0]):
+    col_count = pencil_ref.shape[0]
+
+    def products(c):
         sums = lax.dot_general(
             pencil_ref[c], point_ref[...], (((0,), (0,)), ((), ())), preferred_element_type=F32
         )
-        high, low = split_parts(sums * sums, 2)
+        return split_parts(sums * sums, 2)
+
+    following = products(0)
+    for c in range(col_count):
+        high, low = following
+        if c + 1 < col_count:
+            following = products(c + 1)
         smooth = jnp.dot(
             circulant_ref[c],
             jnp.concatenate([high, low, high], axis=0),

time: 158 us -> 153 us (0.968)
  local copies, waits for them, and re-layouts: 10.9 us -> 5.45 us
    unnamed x17 -> x9, local copies, waits for them, and re-layouts: 10.3 us -> 4.84 us
    pallas_call x1, Pallas kernels: 67.2 us -> 70.1 us  [inverse_and_late_fit(): pl.pallas_call(functools.partial(inverse_kernel, 128), grid=(1 + late.sha...]
    pallas_call x1, Pallas kernels: 10.5 us -> 8.2 us  [filtered_products(): pl.pallas_call(filter_kernel, grid=(count // chunk,), in_specs=[pl.BlockS...]
  transfers between devices with their start and end apart: 2 -> 2, of which waited for: 1 -> 1; matrix products, arithmetic and copies ran while one was open for 0% -> 0% of each run, Pallas kernels for 49% -> 52%
where the time goes in v6:
time: 153 us
  Pallas kernels  117 us (76%)
  waiting for transfers between devices  18.2 us (12%)
  starting transfers between devices  12 us (8%)
  local copies, waits for them, and re-layouts  5.45 us (4%)
    pallas_call x1, Pallas kernels, inverse_and_late_fit(): pl.pallas_call(functools.partial(inverse_kernel, 128), grid=(1 + late.sha...  70.1 us
    pallas_call x1, Pallas kernels, exchange(): pl.pallas_call(functools.partial(exchange_kernel, gz_count, gy_count), in...  27.7 us
    all_to_all x1, waiting for transfers between devices, per_device(): late = swap(late.reshape(gz_count, slab_planes - early, col_pencil, count))  18.2 us
    pallas_call x1, Pallas kernels, early_fit(): pl.pallas_call(early_fit_kernel, grid=(early // block,), in_specs=[pl.Blo...  9.23 us
    pallas_call x1, Pallas kernels, filtered_products(): pl.pallas_call(filter_kernel, grid=(count // chunk,), in_specs=[pl.BlockS...  8.2 us
    all_to_all x1, starting transfers between devices, per_device(): late = swap(late.reshape(gz_count, slab_planes - early, col_pencil, count))  7.16 us
    all_to_all x1, starting transfers between devices, per_device(): slab = swap(first.reshape(gz_count, early, col_pencil, count))  4.88 us
    unnamed x9, local copies, waits for them, and re-layouts  4.84 us
  transfers between devices with their start and end apart: 2, of which 1 were waited for; matrix products, arithmetic and copies ran while one was open for 0% of the time, Pallas kernels for 52%

profile of v6, /device:TPU:0, one launch (start us, length us, event | category | flops | bytes accessed | tf_op | source)
XLA Modules:
  0.0 152.9 jit_solution(3624799554984499047)
XLA Ops:
  0.0 0.0 copy-start
  0.0 0.9 copy-done
  0.9 0.1 constant_dynamic-slice_fusion
  1.0 0.1 copy.10
  1.1 0.0 copy-start.1
  1.1 0.7 copy-done.1
  1.8 27.7 %shard_map.55 = (bf16[2,16,8,1,8,256]{5,4,3,2,1,0:T(8,128)(2,1)S(1)}, bf16[8,16,2,1024]{3,2,1,0:T(2,128)(2,1)S(1)}, bf16[8,256,768]{2,1,0:T(8,128)(2,1)S(1)}) custom-call(bf16[2,256,1024]{2,1,0:T(8,128)(2,1)} %orbital_hbm.1, s32[1,1024]{1,0:T(1,128)S(1)} %bitcast.16, f32[8,512]{1,0:T(8,128)S(1)} %maximum_multiply_fusion.weight_ref, ...), custom_call_target="tpu_custom_call" | custom-call | tf_op jit(solution)/shard_map/pallas_call | solution.py:217
  29.4 0.3 copy.8
  29.7 0.2 copy.9
  30.0 8.2 %shard_map.56 = (f32[128,8,1024]{2,1,0:T(8,128)}, f32[128,8,1024]{2,1,0:T(8,128)}) custom-call(bf16[8,256,256]{2,1,0:T(8,128)(2,1)S(1)} %bitcast.12, bf16[256,1024]{1,0:T(8,128)(2,1)S(1)} %bitcast.13, bf16[8,256,768]{2,1,0:T(8,128)(2,1)S(1)} %get-tuple-element.15.circulant_ref), custom_call_target="tpu_custom_call" | custom-call | flops 4294967296 | bytes 10485760 | tf_op jit(solution)/shard_map/pallas_call | solution.py:448
  38.2 4.9 %all-to-all-start.1 = ((f32[16,8,8,1024]{3,2,1,0:T(8,128)}), f32[16,8,8,1024]{3,2,1,0:T(8,128)}, u32[]{:S(2)}, u32[]{:S(2)}) async-start(f32[16,8,8,1024]{3,2,1,0:T(8,128)} %bitcast.17), calls=%async_computation.1 | async-start | bytes 8388608 | tf_op jit(solution)/shard_map/all_to_all | solution.py:555
  43.1 70.1 %shard_map.57 = (bf16[1024,1024]{1,0:T(8,128)(2,1)}, bf16[1024,1024]{1,0:T(8,128)(2,1)}, bf16[1024,1024]{1,0:T(8,128)(2,1)}) custom-call(bf16[256,1024]{1,0:T(8,128)(2,1)S(1)} %bitcast.14, f32[1024,1024]{1,0:T(8,128)} %bitcast.20), custom_call_target="tpu_custom_call" | custom-call | flops 64424509440 | bytes 8388608 | tf_op jit(solution)/shard_map/pallas_call | solution.py:401
  113.2 0.0 all-to-all-done.1.rows_ref
  113.2 7.2 %all-to-all-start = ((bf16[16,8,8,1024]{3,2,1,0:T(8,128)(2,1)}), bf16[16,8,8,1024]{3,2,1,0:T(8,128)(2,1)S(1)}, u32[]{:S(2)}, u32[]{:S(2)}) async-start(bf16[16,8,8,1024]{3,2,1,0:T(8,128)(2,1)} %bitcast.18), calls=%async_computation | async-start | bytes 4194304 | tf_op jit(solution)/shard_map/all_to_all | solution.py:557
  120.3 0.0 copy-start.2
  120.3 1.6 %copy-done.2 = bf16[1024,1024]{1,0:T(8,128)(2,1)S(1)} copy-done((bf16[1024,1024]{1,0:T(8,128)(2,1)S(1)}, bf16[1024,1024]{1,0:T(8,128)(2,1)}, u32[]{:S(2)}) %copy-start.2) | copy-done | bytes 2097176
  121.9 0.0 copy-start.3
  121.9 1.6 %copy-done.3 = bf16[1024,1024]{1,0:T(8,128)(2,1)S(1)} copy-done((bf16[1024,1024]{1,0:T(8,128)(2,1)S(1)}, bf16[1024,1024]{1,0:T(8,128)(2,1)}, u32[]{:S(2)}) %copy-start.3) | copy-done | bytes 2097176
  123.5 9.2 %shard_map.58._ = bf16[16,128,1024]{2,1,0:T(8,128)(2,1)} custom-call(f32[16,8,8,1024]{3,2,1,0:T(8,128)} %all-to-all-done.1.rows_ref, bf16[1024,1024]{1,0:T(8,128)(2,1)S(1)} %copy-done.2, bf16[1024,1024]{1,0:T(8,128)(2,1)S(1)} %copy-done.3), custom_call_target="tpu_custom_call" | custom-call | flops 6442450944 | bytes 10485760 | tf_op jit(solution)/shard_map/pallas_call | solution.py:491
  132.7 18.2 %all-to-all-done.late_ref = bf16[16,8,8,1024]{3,2,1,0:T(8,128)(2,1)S(1)} async-done(((bf16[16,8,8,1024]{3,2,1,0:T(8,128)(2,1)}), bf16[16,8,8,1024]{3,2,1,0:T(8,128)(2,1)S(1)}, u32[]{:S(2)}, u32[]{:S(2)}) %all-to-all-start) | async-done | bytes 2097184 | tf_op jit(solution)/shard_map/all_to_all | solution.py:557
  150.9 1.9 %shard_map.59 = bf16[16,128,1024]{2,1,0:T(8,128)(2,1)} custom-call(bf16[16,8,8,1024]{3,2,1,0:T(8,128)(2,1)S(1)} %all-to-all-done.late_ref, bf16[16,128,1024]{2,1,0:T(8,128)(2,1)} %shard_map.58._), custom_call_target="tpu_custom_call", output_to_operand_aliasing={{}: (1, {})} | custom-call | bytes 4194304 | tf_op jit(solution)/shard_map/pallas_call | solution.py:518
  (1 shorter events, 0.0 us)
Async XLA Ops:
  0.0 0.9 copy-start
  1.1 0.7 copy-start.1
  38.2 75.0 %all-to-all-start.1 = ((f32[16,8,8,1024]{3,2,1,0:T(8,128)}), f32[16,8,8,1024]{3,2,1,0:T(8,128)}, u32[]{:S(2)}, u32[]{:S(2)}) async-start(f32[16,8,8,1024]{3,2,1,0:T(8,128)} %bitcast.17), calls=%async_computation.1 | async-start | bytes 8388608 | tf_op jit(solution)/shard_map/all_to_all | solution.py:555
  113.2 37.8 %all-to-all-start = ((bf16[16,8,8,1024]{3,2,1,0:T(8,128)(2,1)}), bf16[16,8,8,1024]{3,2,1,0:T(8,128)(2,1)S(1)}, u32[]{:S(2)}, u32[]{:S(2)}) async-start(bf16[16,8,8,1024]{3,2,1,0:T(8,128)(2,1)} %bitcast.18), calls=%async_computation | async-start | bytes 4194304 | tf_op jit(solution)/shard_map/all_to_all | solution.py:557
  120.3 1.6 %copy-start.2 = (bf16[1024,1024]{1,0:T(8,128)(2,1)S(1)}, bf16[1024,1024]{1,0:T(8,128)(2,1)}, u32[]{:S(2)}) copy-start(bf16[1024,1024]{1,0:T(8,128)(2,1)} %get-tuple-element.19.high_ref) | copy-start | bytes 6291460
  121.9 1.6 %copy-start.3 = (bf16[1024,1024]{1,0:T(8,128)(2,1)S(1)}, bf16[1024,1024]{1,0:T(8,128)(2,1)}, u32[]{:S(2)}) copy-start(bf16[1024,1024]{1,0:T(8,128)(2,1)} %get-tuple-element.20.low_ref) | copy-start | bytes 6291460

commit v7 on v6

--- a/solution.py
+++ b/solution.py
@@ -30,9 +30,9 @@
     plane_pick = lax.broadcasted_iota(jnp.int32, (planes, count), 0) == point_planes
     for band in range(bands):
         picked = jnp.dot(orbital_ref[band], column_pick, preferred_element_type=F32)
-        out_ref[band : band + 1, :] = jnp.sum(
-            jnp.where(plane_pick, picked, 0.0), axis=0, keepdims=True
-        ).astype(BF16)
+        values = jnp.sum(jnp.where(plane_pick, picked, 0.0), axis=0, keepdims=True).astype(BF16)
+        out_ref[0, band : band + 1, :] = values[:, : count // 2]
+        out_ref[1, band : band + 1, :] = values[:, count // 2 :]
 
 
 def send(source, target, send_sem, recv_sem, device):
@@ -52,23 +52,27 @@
     gz_count,
     gy_count,
     orbital_hbm,
-    points_ref,
-    weight_ref,
+    points_hbm,
+    coulomb_hbm,
     left_wave_hbm,
     right_wave_hbm,
     pencil_ref,
-    value_ref,
+    first_value_ref,
+    second_value_ref,
     circulant_ref,
     orbital_ref,
+    points_ref,
+    coulomb_ref,
     left_wave_ref,
     right_wave_ref,
     own_blocks,
     plane_stage,
     row_stage,
-    value_stage,
+    gz_value_stage,
+    gy_value_stage,
     own_values,
-    gz_value_sems,
-    gy_value_sems,
+    first_value_sems,
+    second_value_sems,
     gy_first_sems,
     gz_first_sems,
     gz_second_sems,
@@ -83,15 +87,21 @@
         pl.semaphore_signal(
             barrier, inc=1, device_id=device, device_id_type=pl.DeviceIdType.MESH
         )
-    load = pltpu.make_async_copy(orbital_hbm, orbital_ref, local_sems.at[0])
-    load.start()
+    load = [
+        pltpu.make_async_copy(points_hbm, points_ref, local_sems.at[9]),
+        pltpu.make_async_copy(orbital_hbm, orbital_ref, local_sems.at[0]),
+    ]
+    for copy in load:
+        copy.start()
     load_waves = [
+        pltpu.make_async_copy(coulomb_hbm, coulomb_ref, local_sems.at[10]),
         pltpu.make_async_copy(left_wave_hbm, left_wave_ref, local_sems.at[7]),
         pltpu.make_async_copy(right_wave_hbm, right_wave_ref, local_sems.at[8]),
     ]
     for copy in load_waves:
         copy.start()
-    load.wait()
+    for copy in load:
+        copy.wait()
     pick_points(orbital_ref, points_ref, own_values)
     bands, planes, columns = orbital_ref.shape
     half = bands // 2
@@ -107,7 +117,8 @@
     pl.semaphore_wait(barrier, gy_count + gz_count - 2)
 
     own = [
-        pltpu.make_async_copy(own_values, value_stage.at[gz], local_sems.at[1]),
+        pltpu.make_async_copy(own_values.at[0], gz_value_stage.at[gz], local_sems.at[1]),
+        pltpu.make_async_copy(own_values.at[1], gy_value_stage.at[gy], local_sems.at[11]),
         pltpu.make_async_copy(
             own_blocks.at[pl.ds(0, half), gy], plane_stage.at[gy], local_sems.at[2]
         ),
@@ -118,8 +129,23 @@
     for copy in own:
         copy.start()
     values = [
-        send(own_values, value_stage.at[gz], gz_value_sems.at[0, i], gz_value_sems.at[1, i], (peer, gy))
+        send(
+            own_values.at[0],
+            gz_value_stage.at[gz],
+            first_value_sems.at[0, 0, i],
+            first_value_sems.at[0, 1, i],
+            (peer, gy),
+        )
         for i, peer in enumerate(gz_peers)
+    ] + [
+        send(
+            own_values.at[1],
+            gy_value_stage.at[gy],
+            first_value_sems.at[1, 0, i],
+            first_value_sems.at[1, 1, i],
+            (gz, peer),
+        )
+        for i, peer in enumerate(gy_peers)
     ]
     lower = [
         send(
@@ -146,8 +172,23 @@
     for copy in values:
         copy.wait_recv()
     values_on = [
-        send(value_stage, value_ref.at[gy], gy_value_sems.at[0, i], gy_value_sems.at[1, i], (gz, peer))
+        send(
+            gz_value_stage,
+            first_value_ref.at[gy],
+            second_value_sems.at[0, 0, i],
+            second_value_sems.at[0, 1, i],
+            (gz, peer),
+        )
         for i, peer in enumerate(gy_peers)
+    ] + [
+        send(
+            gy_value_stage,
+            second_value_ref.at[gz],
+            second_value_sems.at[1, 0, i],
+            second_value_sems.at[1, 1, i],
+            (peer, gy),
+        )
+        for i, peer in enumerate(gz_peers)
     ]
     for copy in lower:
         copy.wait_recv()
@@ -174,7 +215,8 @@
         for i, peer in enumerate(gy_peers)
     ]
     own_on = [
-        pltpu.make_async_copy(value_stage, value_ref.at[gy], local_sems.at[4]),
+        pltpu.make_async_copy(gz_value_stage, first_value_ref.at[gy], local_sems.at[4]),
+        pltpu.make_async_copy(gy_value_stage, second_value_ref.at[gz], local_sems.at[12]),
         pltpu.make_async_copy(plane_stage.at[:, :, gz], pencil_ref.at[0, gz], local_sems.at[5]),
         pltpu.make_async_copy(row_stage.at[:, :, gy], pencil_ref.at[1, :, gy], local_sems.at[6]),
     ]
@@ -182,10 +224,21 @@
         copy.start()
     for copy in load_waves:
         copy.wait()
+    all_cols = coulomb_ref.shape[1]
+    own_cols = lax.broadcasted_iota(jnp.int32, (cols, all_cols), 0) + gz * cols
+    pick = (lax.broadcasted_iota(jnp.int32, (cols, all_cols), 1) == own_cols).astype(F32)
+    weights = lax.dot_general(
+        pick,
+        coulomb_ref[...],
+        (((1,), (1,)), ((), ())),
+        precision=FULL,
+        preferred_element_type=F32,
+    ) * (1.0 / planes)
+    weights = jnp.concatenate([weights, weights], axis=1)
     for c in range(cols):
         high, low = split_parts(
             jnp.dot(
-                left_wave_ref[...] * weight_ref[c : c + 1, :],
+                left_wave_ref[...] * weights[c : c + 1, :],
                 right_wave_ref[...],
                 precision=FULL,
                 preferred_element_type=F32,
@@ -201,10 +254,10 @@
         copy.wait()
 
 
-def exchange(orbitals, points, weights, gz_count, gy_count, early):
+def exchange(orbitals, points, coulomb, gz_count, gy_count, early):
     bands, planes, columns = orbitals.shape
     count = points.shape[0]
-    cols = weights.shape[0]
+    cols = coulomb.shape[1] // gz_count
     half = bands // 2
     slab = planes // gz_count
     z = np.arange(planes)
@@ -216,37 +269,41 @@
     dma = pltpu.SemaphoreType.DMA
     return pl.pallas_call(
         functools.partial(exchange_kernel, gz_count, gy_count),
-        in_specs=[hbm, vmem, vmem, hbm, hbm],
-        out_specs=(vmem, vmem, vmem),
+        in_specs=[hbm, hbm, hbm, hbm, hbm],
+        out_specs=(vmem, vmem, vmem, vmem),
         out_shape=(
             jax.ShapeDtypeStruct((2, gz_count, gy_count, half, cols, planes), BF16),
-            jax.ShapeDtypeStruct((gy_count, gz_count, bands, count), BF16),
+            jax.ShapeDtypeStruct((gy_count, gz_count, bands, count // 2), BF16),
+            jax.ShapeDtypeStruct((gz_count, gy_count, bands, count // 2), BF16),
             jax.ShapeDtypeStruct((cols, planes, 3 * planes), BF16),
         ),
         scratch_shapes=[
             pltpu.VMEM((bands, planes, columns), BF16),
+            pltpu.VMEM((1, count), jnp.int32),
+            pltpu.VMEM(coulomb.shape, F32),
             pltpu.VMEM((planes, 2 * planes), F32),
             pltpu.VMEM((2 * planes, planes), F32),
             pltpu.VMEM((bands, gy_count, gz_count, cols, planes), BF16),
             pltpu.VMEM((gy_count, half, gz_count, cols, planes), BF16),
             pltpu.VMEM((gz_count, half, gy_count, cols, planes), BF16),
-            pltpu.VMEM((gz_count, bands, count), BF16),
-            pltpu.VMEM((bands, count), BF16),
-            dma((2, gz_count - 1)),
-            dma((2, gy_count - 1)),
+            pltpu.VMEM((gz_count, bands, count // 2), BF16),
+            pltpu.VMEM((gy_count, bands, count // 2), BF16),
+            pltpu.VMEM((2, bands, count // 2), BF16),
+            dma((2, 2, gz_count - 1)),
+            dma((2, 2, gz_count - 1)),
             dma((2, gy_count - 1)),
             dma((2, gz_count - 1)),
             dma((2, gz_count - 1)),
             dma((2, gy_count - 1)),
-            dma((9,)),
+            dma((13,)),
         ],
         compiler_params=pltpu.CompilerParams(
             collective_id=0, has_side_effects=True, vmem_limit_bytes=28 << 20
         ),
     )(
         in_hbm(orbitals),
-        points.reshape(1, count),
-        jnp.concatenate([weights, weights], axis=1) * (1.0 / planes),
+        in_hbm(points.reshape(1, count)),
+        in_hbm(coulomb),
         in_hbm(jnp.asarray(waves[order], F32)),
         in_hbm(jnp.asarray(waves.T, F32)),
     )
@@ -349,7 +406,9 @@
     return jnp.concatenate(tiles, axis=0)
 
 
-def inverse_kernel(width, point_ref, late_ref, fitted_ref, high_ref, low_ref, work):
+def inverse_kernel(
+    width, point_ref, late_ref, fitted_ref, high_out, low_out, work, high_ref, low_ref
+):
     size = work.shape[0]
     block = 256
 
@@ -390,25 +449,33 @@
 
     @pl.when(pl.program_id(0) > 0)
     def _():
+        rows = pl.ds(pl.multiple_of((pl.program_id(0) - 1) * block, block), block)
+        high_out[...] = high_ref[rows, :]
+        low_out[...] = low_ref[rows, :]
         fitted_ref[...] = fit_rows(late_ref[...], high_ref, low_ref)
 
 
 def inverse_and_late_fit(at_points, late):
     size = at_points.shape[1]
     block = 256
-    whole = pl.BlockSpec((size, size), lambda i: (0, 0))
+    steps = late.shape[0] // block
+    assert steps == size // block
     rows = pl.BlockSpec((block, size), lambda i: (jnp.maximum(i - 1, 0), 0))
     return pl.pallas_call(
         functools.partial(inverse_kernel, 128),
-        grid=(1 + late.shape[0] // block,),
+        grid=(1 + steps,),
         in_specs=[pl.BlockSpec(at_points.shape, lambda i: (0, 0)), rows],
-        out_specs=(rows, whole, whole),
+        out_specs=(rows, rows, rows),
         out_shape=(
             pltpu.HBM(late.shape, BF16),
             pltpu.HBM((size, size), BF16),
             pltpu.HBM((size, size), BF16),
         ),
-        scratch_shapes=[pltpu.VMEM((size, size), F32)],
+        scratch_shapes=[
+            pltpu.VMEM((size, size), F32),
+            pltpu.VMEM((size, size), BF16),
+            pltpu.VMEM((size, size), BF16),
+        ],
         compiler_params=pltpu.CompilerParams(vmem_limit_bytes=36 << 20),
         cost_estimate=pl.CostEstimate(
             flops=60 * size**3, bytes_accessed=8 * size * size, transcendentals=0
@@ -537,15 +604,16 @@
     count = points.shape[0]
     slab_planes = planes // gz_count
     early = EARLY
-    weights = lax.dynamic_slice_in_dim(
-        coulomb, lax.axis_index("gz") * col_pencil, col_pencil, 1
-    ).T
-    pencils, at_points, circulant = exchange(
-        orbitals, points, weights, gz_count, gy_count, early
+    pencils, first_values, second_values, circulant = exchange(
+        orbitals, points, coulomb, gz_count, gy_count, early
     )
-    bands = orbitals.shape[0]
-    at_points = jnp.transpose(
-        at_points.reshape(gy_count, gz_count, 2, bands // 2, count), (2, 1, 0, 3, 4)
+    split = (2, orbitals.shape[0] // 2, count // 2)
+    at_points = jnp.concatenate(
+        [
+            jnp.transpose(first_values.reshape(gy_count, gz_count, *split), (2, 1, 0, 3, 4)),
+            jnp.transpose(second_values.reshape(gz_count, gy_count, *split), (2, 0, 1, 3, 4)),
+        ],
+        axis=4,
     ).reshape(-1, count)
     pencils = jnp.transpose(pencils.reshape(-1, col_pencil, planes), (1, 0, 2))
     first, second = filtered_products(pencils, at_points, circulant, gz_count * early)

time: 153 us -> 151 us (0.987)
  Pallas kernels: 117 us -> 115 us
  local copies, waits for them, and re-layouts: 5.45 us -> 3.75 us
  starting transfers between devices: 12 us -> 13.6 us
    unnamed x9 -> x4, local copies, waits for them, and re-layouts: 4.84 us -> 3.17 us
    all_to_all x1, starting transfers between devices: 4.88 us -> 6.46 us  [per_device(): slab = swap(first.reshape(gz_count, early, col_pencil, count))]
    pallas_call x1, Pallas kernels: 27.7 us -> 26.1 us  [exchange(): pl.pallas_call(functools.partial(exchange_kernel, gz_count, gy_count), in...]
where the time goes in v7:
time: 151 us
  Pallas kernels  115 us (76%)
  waiting for transfers between devices  17.8 us (12%)
  starting transfers between devices  13.6 us (9%)
  local copies, waits for them, and re-layouts  3.75 us (2%)
    pallas_call x1, Pallas kernels, inverse_and_late_fit(): pl.pallas_call(functools.partial(inverse_kernel, 128), grid=(1 + steps,),...  69.2 us
    pallas_call x1, Pallas kernels, exchange(): pl.pallas_call(functools.partial(exchange_kernel, gz_count, gy_count), in...  26.1 us
    all_to_all x1, waiting for transfers between devices, per_device(): late = swap(late.reshape(gz_count, slab_planes - early, col_pencil, count))  17.8 us
    pallas_call x1, Pallas kernels, early_fit(): pl.pallas_call(early_fit_kernel, grid=(early // block,), in_specs=[pl.Blo...  9.23 us
    pallas_call x1, Pallas kernels, filtered_products(): pl.pallas_call(filter_kernel, grid=(count // chunk,), in_specs=[pl.BlockS...  8.22 us
    all_to_all x1, starting transfers between devices, per_device(): late = swap(late.reshape(gz_count, slab_planes - early, col_pencil, count))  7.15 us
    all_to_all x1, starting transfers between devices, per_device(): slab = swap(first.reshape(gz_count, early, col_pencil, count))  6.46 us
    unnamed x4, local copies, waits for them, and re-layouts  3.17 us
  transfers between devices with their start and end apart: 2, of which 1 were waited for; matrix products, arithmetic and copies ran while one was open for 0% of the time, Pallas kernels for 52%

profile of v7, /device:TPU:0, one launch (start us, length us, event | category | flops | bytes accessed | tf_op | source)
XLA Modules:
  0.0 150.5 jit_solution(874997711856524657)
XLA Ops:
  0.0 26.1 %shard_map.55 = (bf16[2,16,8,1,8,256]{5,4,3,2,1,0:T(8,128)(2,1)S(1)}, bf16[8,16,2,512]{3,2,1,0:T(2,128)(2,1)S(1)}, bf16[16,8,2,512]{3,2,1,0:T(2,128)(2,1)S(1)}, bf16[8,256,768]{2,1,0:T(8,128)(2,1)S(1)}) custom-call(bf16[2,256,1024]{2,1,0:T(8,128)(2,1)} %orbital_hbm.1, s32[1,1024]{1,0:T(1,128)} %bitcast.23, f32[256,128]{1,0:T(8,128)} %coulomb_hbm.1, ...), custom_call_target="tpu_custom_call" | custom-call | tf_op jit(solution)/shard_map/pallas_call | solution.py:270
  26.1 0.2 copy.11
  26.4 0.6 pad_maximum_fusion
  27.0 0.1 copy.8
  27.1 0.2 copy.9
  27.3 8.2 %shard_map.56 = (f32[128,8,1024]{2,1,0:T(8,128)}, f32[128,8,1024]{2,1,0:T(8,128)}) custom-call(bf16[8,256,256]{2,1,0:T(8,128)(2,1)S(1)} %bitcast.16, bf16[256,1024]{1,0:T(8,128)(2,1)S(1)} %bitcast.17, bf16[8,256,768]{2,1,0:T(8,128)(2,1)S(1)} %get-tuple-element.17.circulant_ref), custom_call_target="tpu_custom_call" | custom-call | flops 4294967296 | bytes 10485760 | tf_op jit(solution)/shard_map/pallas_call | solution.py:515
  35.6 6.5 %all-to-all-start.1 = ((f32[16,8,8,1024]{3,2,1,0:T(8,128)}), f32[16,8,8,1024]{3,2,1,0:T(8,128)}, u32[]{:S(2)}, u32[]{:S(2)}) async-start(f32[16,8,8,1024]{3,2,1,0:T(8,128)} %bitcast.20), calls=%async_computation.1 | async-start | bytes 8388608 | tf_op jit(solution)/shard_map/all_to_all | solution.py:623
  42.0 69.2 %shard_map.57 = (bf16[1024,1024]{1,0:T(8,128)(2,1)}, bf16[1024,1024]{1,0:T(8,128)(2,1)}, bf16[1024,1024]{1,0:T(8,128)(2,1)}) custom-call(bf16[256,1024]{1,0:T(8,128)(2,1)S(1)} %bitcast.18, f32[1024,1024]{1,0:T(8,128)} %bitcast.24), custom_call_target="tpu_custom_call" | custom-call | flops 64424509440 | bytes 8388608 | tf_op jit(solution)/shard_map/pallas_call | solution.py:464
  111.2 0.0 all-to-all-done.1.rows_ref
  111.3 7.2 %all-to-all-start = ((bf16[16,8,8,1024]{3,2,1,0:T(8,128)(2,1)}), bf16[16,8,8,1024]{3,2,1,0:T(8,128)(2,1)S(1)}, u32[]{:S(2)}, u32[]{:S(2)}) async-start(bf16[16,8,8,1024]{3,2,1,0:T(8,128)(2,1)} %bitcast.21), calls=%async_computation | async-start | bytes 4194304 | tf_op jit(solution)/shard_map/all_to_all | solution.py:625
  118.4 0.0 copy-start
  118.4 1.6 %copy-done = bf16[1024,1024]{1,0:T(8,128)(2,1)S(1)} copy-done((bf16[1024,1024]{1,0:T(8,128)(2,1)S(1)}, bf16[1024,1024]{1,0:T(8,128)(2,1)}, u32[]{:S(2)}) %copy-start) | copy-done | bytes 2097176
  120.0 0.0 copy-start.1
  120.0 1.6 %copy-done.1 = bf16[1024,1024]{1,0:T(8,128)(2,1)S(1)} copy-done((bf16[1024,1024]{1,0:T(8,128)(2,1)S(1)}, bf16[1024,1024]{1,0:T(8,128)(2,1)}, u32[]{:S(2)}) %copy-start.1) | copy-done | bytes 2097176
  121.6 9.2 %shard_map.58._ = bf16[16,128,1024]{2,1,0:T(8,128)(2,1)} custom-call(f32[16,8,8,1024]{3,2,1,0:T(8,128)} %all-to-all-done.1.rows_ref, bf16[1024,1024]{1,0:T(8,128)(2,1)S(1)} %copy-done, bf16[1024,1024]{1,0:T(8,128)(2,1)S(1)} %copy-done.1), custom_call_target="tpu_custom_call" | custom-call | flops 6442450944 | bytes 10485760 | tf_op jit(solution)/shard_map/pallas_call | solution.py:558
  130.8 17.8 %all-to-all-done.late_ref = bf16[16,8,8,1024]{3,2,1,0:T(8,128)(2,1)S(1)} async-done(((bf16[16,8,8,1024]{3,2,1,0:T(8,128)(2,1)}), bf16[16,8,8,1024]{3,2,1,0:T(8,128)(2,1)S(1)}, u32[]{:S(2)}, u32[]{:S(2)}) %all-to-all-start) | async-done | bytes 2097184 | tf_op jit(solution)/shard_map/all_to_all | solution.py:625
  148.6 1.9 %shard_map.59 = bf16[16,128,1024]{2,1,0:T(8,128)(2,1)} custom-call(bf16[16,8,8,1024]{3,2,1,0:T(8,128)(2,1)S(1)} %all-to-all-done.late_ref, bf16[16,128,1024]{2,1,0:T(8,128)(2,1)} %shard_map.58._), custom_call_target="tpu_custom_call", output_to_operand_aliasing={{}: (1, {})} | custom-call | bytes 4194304 | tf_op jit(solution)/shard_map/pallas_call | solution.py:585
Async XLA Ops:
  35.6 75.7 %all-to-all-start.1 = ((f32[16,8,8,1024]{3,2,1,0:T(8,128)}), f32[16,8,8,1024]{3,2,1,0:T(8,128)}, u32[]{:S(2)}, u32[]{:S(2)}) async-start(f32[16,8,8,1024]{3,2,1,0:T(8,128)} %bitcast.20), calls=%async_computation.1 | async-start | bytes 8388608 | tf_op jit(solution)/shard_map/all_to_all | solution.py:623
  111.3 37.3 %all-to-all-start = ((bf16[16,8,8,1024]{3,2,1,0:T(8,128)(2,1)}), bf16[16,8,8,1024]{3,2,1,0:T(8,128)(2,1)S(1)}, u32[]{:S(2)}, u32[]{:S(2)}) async-start(bf16[16,8,8,1024]{3,2,1,0:T(8,128)(2,1)} %bitcast.21), calls=%async_computation | async-start | bytes 4194304 | tf_op jit(solution)/shard_map/all_to_all | solution.py:625
  118.4 1.6 %copy-start = (bf16[1024,1024]{1,0:T(8,128)(2,1)S(1)}, bf16[1024,1024]{1,0:T(8,128)(2,1)}, u32[]{:S(2)}) copy-start(bf16[1024,1024]{1,0:T(8,128)(2,1)} %get-tuple-element.21.high_ref) | copy-start | bytes 6291460
  120.0 1.6 %copy-start.1 = (bf16[1024,1024]{1,0:T(8,128)(2,1)S(1)}, bf16[1024,1024]{1,0:T(8,128)(2,1)}, u32[]{:S(2)}) copy-start(bf16[1024,1024]{1,0:T(8,128)(2,1)} %get-tuple-element.22.low_ref) | copy-start | bytes 6291460

commit v8 on v7

--- a/solution.py
+++ b/solution.py
@@ -319,12 +319,15 @@
 
 
 def full_dot(left, right):
+    return jnp.dot(left_stack(left), right_stack(right), preferred_element_type=F32)
+
+
+def left_stack(left):
     high, middle, low = split_parts(left, 3)
-    wide = jnp.concatenate([high, high, middle, high, low, middle], axis=1)
-    return jnp.dot(wide, full_stack(right), preferred_element_type=F32)
-
-
-def full_stack(right):
+    return jnp.concatenate([high, high, middle, high, low, middle], axis=1)
+
+
+def right_stack(right):
     high, middle, low = split_parts(right, 3)
     return jnp.concatenate([high, middle, high, low, high, middle], axis=0)
 
@@ -376,33 +379,28 @@
 
 def small_inverse(block):
     size = block.shape[0]
-    group_rows = 32
     tiles = [block[i : i + 8, :] for i in range(0, size, 8)]
     lane = lax.broadcasted_iota(jnp.int32, (8, size), 1)
     sub = lax.broadcasted_iota(jnp.int32, (8, size), 0)
-    per_group = group_rows // 8
-    for start in range(0, size, group_rows):
-        group = list(range(start // 8, start // 8 + per_group))
-        for at in group:
-            results, panel, inside = eliminate_rows(tiles[at], at * 8, lane, sub)
-            for step in range(1, per_group):
-                other = group[(at - group[0] + step) % per_group]
-                terms = [
-                    jnp.broadcast_to(tiles[other][:, at * 8 + j : at * 8 + j + 1], (8, size))
-                    * results[j]
-                    for j in range(8)
-                ]
-                tiles[other] = jnp.where(inside, 0.0, tiles[other]) - tree_sum(terms)
-            tiles[at] = panel
-        rest = [i for i in range(len(tiles)) if i not in group]
-        panel = jnp.concatenate([tiles[i] for i in group], axis=0)
+    for at in range(len(tiles)):
+        first = at * 8
+        following = [at + 1] if at + 1 < len(tiles) else []
+        rest = [i for i in range(len(tiles)) if i != at and i not in following]
         stack = jnp.concatenate([tiles[i] for i in rest], axis=0)
-        change = full_dot(stack[:, start : start + group_rows], panel)
         wide_lane = lax.broadcasted_iota(jnp.int32, stack.shape, 1)
-        in_group = (wide_lane >= start) & (wide_lane < start + group_rows)
-        stack = jnp.where(in_group, 0.0, stack) - change
+        kept = jnp.where((wide_lane >= first) & (wide_lane < first + 8), 0.0, stack)
+        wide = left_stack(stack[:, first : first + 8])
+        results, panel, inside = eliminate_rows(tiles[at], first, lane, sub)
+        for other in following:
+            terms = [
+                jnp.broadcast_to(tiles[other][:, first + j : first + j + 1], (8, size)) * results[j]
+                for j in range(8)
+            ]
+            tiles[other] = jnp.where(inside, 0.0, tiles[other]) - tree_sum(terms)
+        stack = kept - jnp.dot(wide, right_stack(panel), preferred_element_type=F32)
         for place, i in enumerate(rest):
             tiles[i] = stack[place * 8 : place * 8 + 8, :]
+        tiles[at] = panel
     return jnp.concatenate(tiles, axis=0)
 
 
@@ -429,9 +427,8 @@
             work[at, :] = full_dot(pivot, work[at, :])
             work[at, at] = pivot
             panel = work[at, :]
-            stacked = full_stack(panel)
-            high, middle, low = split_parts(work[:, at], 3)
-            wide = jnp.concatenate([high, high, middle, high, low, middle], axis=1)
+            stacked = right_stack(panel)
+            wide = left_stack(work[:, at])
             work[:, at] = jnp.zeros((size, width), F32)
             for first in range(0, size, block):
                 columns = slice(first, first + block)

time: 151 us -> 144 us (0.954)
  Pallas kernels: 115 us -> 107 us
    pallas_call x1, Pallas kernels: 69.2 us -> 61.6 us  [inverse_and_late_fit(): pl.pallas_call(functools.partial(inverse_kernel, 128), grid=(1 + steps,),...]
  transfers between devices with their start and end apart: 2 -> 2, of which waited for: 1 -> 1; matrix products, arithmetic and copies ran while one was open for 0% -> 0% of each run, Pallas kernels for 52% -> 50%
where the time goes in v8:
time: 144 us; the launch traced here: 143 us
  Pallas kernels  107 us (74%)
  waiting for transfers between devices  16.6 us (12%)
  starting transfers between devices  14.9 us (10%)
  local copies, waits for them, and re-layouts  3.75 us (3%)
    pallas_call x1, Pallas kernels, inverse_and_late_fit(): pl.pallas_call(functools.partial(inverse_kernel, 128), grid=(1 + steps,),...  61.6 us
    pallas_call x1, Pallas kernels, exchange(): pl.pallas_call(functools.partial(exchange_kernel, gz_count, gy_count), in...  26.1 us
    all_to_all x1, waiting for transfers between devices, per_device(): late = swap(late.reshape(gz_count, slab_planes - early, col_pencil, count))  16.6 us
    pallas_call x1, Pallas kernels, early_fit(): pl.pallas_call(early_fit_kernel, grid=(early // block,), in_specs=[pl.Blo...  9.23 us
    all_to_all x1, starting transfers between devices, per_device(): late = swap(late.reshape(gz_count, slab_planes - early, col_pencil, count))  8.42 us
    pallas_call x1, Pallas kernels, filtered_products(): pl.pallas_call(filter_kernel, grid=(count // chunk,), in_specs=[pl.BlockS...  8.22 us
    all_to_all x1, starting transfers between devices, per_device(): slab = swap(first.reshape(gz_count, early, col_pencil, count))  6.46 us
    unnamed x4, local copies, waits for them, and re-layouts  3.17 us
  transfers between devices with their start and end apart: 2, of which 1 were waited for; matrix products, arithmetic and copies ran while one was open for 0% of the time, Pallas kernels for 50%

profile of v8, /device:TPU:0, one launch (start us, length us, event | category | flops | bytes accessed | tf_op | source)
XLA Modules:
  0.0 143.0 jit_solution(17889892854513824731)
XLA Ops:
  0.0 26.1 %shard_map.55 = (bf16[2,16,8,1,8,256]{5,4,3,2,1,0:T(8,128)(2,1)S(1)}, bf16[8,16,2,512]{3,2,1,0:T(2,128)(2,1)S(1)}, bf16[16,8,2,512]{3,2,1,0:T(2,128)(2,1)S(1)}, bf16[8,256,768]{2,1,0:T(8,128)(2,1)S(1)}) custom-call(bf16[2,256,1024]{2,1,0:T(8,128)(2,1)} %orbital_hbm.1, s32[1,1024]{1,0:T(1,128)} %bitcast.23, f32[256,128]{1,0:T(8,128)} %coulomb_hbm.1, ...), custom_call_target="tpu_custom_call" | custom-call | tf_op jit(solution)/shard_map/pallas_call | solution.py:270
  26.1 0.2 copy.11
  26.4 0.6 pad_maximum_fusion
  27.0 0.1 copy.8
  27.1 0.2 copy.9
  27.3 8.2 %shard_map.56 = (f32[128,8,1024]{2,1,0:T(8,128)}, f32[128,8,1024]{2,1,0:T(8,128)}) custom-call(bf16[8,256,256]{2,1,0:T(8,128)(2,1)S(1)} %bitcast.16, bf16[256,1024]{1,0:T(8,128)(2,1)S(1)} %bitcast.17, bf16[8,256,768]{2,1,0:T(8,128)(2,1)S(1)} %get-tuple-element.17.circulant_ref), custom_call_target="tpu_custom_call" | custom-call | flops 4294967296 | bytes 10485760 | tf_op jit(solution)/shard_map/pallas_call | solution.py:512
  35.6 6.5 %all-to-all-start.1 = ((f32[16,8,8,1024]{3,2,1,0:T(8,128)}), f32[16,8,8,1024]{3,2,1,0:T(8,128)}, u32[]{:S(2)}, u32[]{:S(2)}) async-start(f32[16,8,8,1024]{3,2,1,0:T(8,128)} %bitcast.20), calls=%async_computation.1 | async-start | bytes 8388608 | tf_op jit(solution)/shard_map/all_to_all | solution.py:620
  42.0 61.6 %shard_map.57 = (bf16[1024,1024]{1,0:T(8,128)(2,1)}, bf16[1024,1024]{1,0:T(8,128)(2,1)}, bf16[1024,1024]{1,0:T(8,128)(2,1)}) custom-call(bf16[256,1024]{1,0:T(8,128)(2,1)S(1)} %bitcast.18, f32[1024,1024]{1,0:T(8,128)} %bitcast.24), custom_call_target="tpu_custom_call" | custom-call | flops 64424509440 | bytes 8388608 | tf_op jit(solution)/shard_map/pallas_call | solution.py:461
  103.6 0.0 all-to-all-done.1.rows_ref
  103.6 8.4 %all-to-all-start = ((bf16[16,8,8,1024]{3,2,1,0:T(8,128)(2,1)}), bf16[16,8,8,1024]{3,2,1,0:T(8,128)(2,1)S(1)}, u32[]{:S(2)}, u32[]{:S(2)}) async-start(bf16[16,8,8,1024]{3,2,1,0:T(8,128)(2,1)} %bitcast.21), calls=%async_computation | async-start | bytes 4194304 | tf_op jit(solution)/shard_map/all_to_all | solution.py:622
  112.0 0.0 copy-start
  112.0 1.6 %copy-done = bf16[1024,1024]{1,0:T(8,128)(2,1)S(1)} copy-done((bf16[1024,1024]{1,0:T(8,128)(2,1)S(1)}, bf16[1024,1024]{1,0:T(8,128)(2,1)}, u32[]{:S(2)}) %copy-start) | copy-done | bytes 2097176
  113.6 0.0 copy-start.1
  113.6 1.6 %copy-done.1 = bf16[1024,1024]{1,0:T(8,128)(2,1)S(1)} copy-done((bf16[1024,1024]{1,0:T(8,128)(2,1)S(1)}, bf16[1024,1024]{1,0:T(8,128)(2,1)}, u32[]{:S(2)}) %copy-start.1) | copy-done | bytes 2097176
  115.2 9.2 %shard_map.58._ = bf16[16,128,1024]{2,1,0:T(8,128)(2,1)} custom-call(f32[16,8,8,1024]{3,2,1,0:T(8,128)} %all-to-all-done.1.rows_ref, bf16[1024,1024]{1,0:T(8,128)(2,1)S(1)} %copy-done, bf16[1024,1024]{1,0:T(8,128)(2,1)S(1)} %copy-done.1), custom_call_target="tpu_custom_call" | custom-call | flops 6442450944 | bytes 10485760 | tf_op jit(solution)/shard_map/pallas_call | solution.py:555
  124.4 16.6 %all-to-all-done.late_ref = bf16[16,8,8,1024]{3,2,1,0:T(8,128)(2,1)S(1)} async-done(((bf16[16,8,8,1024]{3,2,1,0:T(8,128)(2,1)}), bf16[16,8,8,1024]{3,2,1,0:T(8,128)(2,1)S(1)}, u32[]{:S(2)}, u32[]{:S(2)}) %all-to-all-start) | async-done | bytes 2097184 | tf_op jit(solution)/shard_map/all_to_all | solution.py:622
  141.0 1.9 %shard_map.59 = bf16[16,128,1024]{2,1,0:T(8,128)(2,1)} custom-call(bf16[16,8,8,1024]{3,2,1,0:T(8,128)(2,1)S(1)} %all-to-all-done.late_ref, bf16[16,128,1024]{2,1,0:T(8,128)(2,1)} %shard_map.58._), custom_call_target="tpu_custom_call", output_to_operand_aliasing={{}: (1, {})} | custom-call | bytes 4194304 | tf_op jit(solution)/shard_map/pallas_call | solution.py:582
Async XLA Ops:
  35.6 68.0 %all-to-all-start.1 = ((f32[16,8,8,1024]{3,2,1,0:T(8,128)}), f32[16,8,8,1024]{3,2,1,0:T(8,128)}, u32[]{:S(2)}, u32[]{:S(2)}) async-start(f32[16,8,8,1024]{3,2,1,0:T(8,128)} %bitcast.20), calls=%async_computation.1 | async-start | bytes 8388608 | tf_op jit(solution)/shard_map/all_to_all | solution.py:620
  103.6 37.5 %all-to-all-start = ((bf16[16,8,8,1024]{3,2,1,0:T(8,128)(2,1)}), bf16[16,8,8,1024]{3,2,1,0:T(8,128)(2,1)S(1)}, u32[]{:S(2)}, u32[]{:S(2)}) async-start(bf16[16,8,8,1024]{3,2,1,0:T(8,128)(2,1)} %bitcast.21), calls=%async_computation | async-start | bytes 4194304 | tf_op jit(solution)/shard_map/all_to_all | solution.py:622
  112.0 1.6 %copy-start = (bf16[1024,1024]{1,0:T(8,128)(2,1)S(1)}, bf16[1024,1024]{1,0:T(8,128)(2,1)}, u32[]{:S(2)}) copy-start(bf16[1024,1024]{1,0:T(8,128)(2,1)} %get-tuple-element.21.high_ref) | copy-start | bytes 6291460
  113.6 1.6 %copy-start.1 = (bf16[1024,1024]{1,0:T(8,128)(2,1)S(1)}, bf16[1024,1024]{1,0:T(8,128)(2,1)}, u32[]{:S(2)}) copy-start(bf16[1024,1024]{1,0:T(8,128)(2,1)} %get-tuple-element.22.low_ref) | copy-start | bytes 6291460

commit v9 on v8

--- a/solution.py
+++ b/solution.py
@@ -461,7 +461,7 @@
     return pl.pallas_call(
         functools.partial(inverse_kernel, 128),
         grid=(1 + steps,),
-        in_specs=[pl.BlockSpec(at_points.shape, lambda i: (0, 0)), rows],
+        in_specs=[pl.BlockSpec(memory_space=pltpu.VMEM), rows],
         out_specs=(rows, rows, rows),
         out_shape=(
             pltpu.HBM(late.shape, BF16),
@@ -513,9 +513,9 @@
         filter_kernel,
         grid=(count // chunk,),
         in_specs=[
-            pl.BlockSpec(pencils.shape, lambda i: (0, 0, 0)),
+            pl.BlockSpec(memory_space=pltpu.VMEM),
             pl.BlockSpec((bands, chunk), lambda i: (0, i)),
-            pl.BlockSpec(circulant.shape, lambda i: (0, 0, 0)),
+            pl.BlockSpec(memory_space=pltpu.VMEM),
         ],
         out_specs=[
             pl.BlockSpec((early, col_count, chunk), lambda i: (0, 0, i)),
@@ -571,8 +571,9 @@
 
 def place_late_kernel(late_ref, _, out_ref):
     planes, cols, count = out_ref.shape
+    first = pl.program_id(0) * planes
     for z in range(planes):
-        out_ref[z] = late_ref[:, z].astype(F32).reshape(cols, count).astype(BF16)
+        out_ref[z] = late_ref[:, first + z].astype(F32).reshape(cols, count).astype(BF16)
 
 
 def place_late(late, fitted):
@@ -583,7 +584,7 @@
         place_late_kernel,
         grid=(planes // block,),
         in_specs=[
-            pl.BlockSpec((sources, block, col_count, count), lambda i: (0, i, 0, 0)),
+            pl.BlockSpec(memory_space=pltpu.VMEM),
             pl.BlockSpec(memory_space=pl.ANY),
         ],
         out_specs=pl.BlockSpec((block, sources * col_count, count), lambda i: (first + i, 0, 0)),

time: 144 us -> 144 us (level)
  no operation moved by 1% of the time
where the time goes in v9:
time: 144 us; the launch traced here: 143 us
  Pallas kernels  107 us (74%)
  waiting for transfers between devices  16.6 us (12%)
  starting transfers between devices  14.9 us (10%)
  local copies, waits for them, and re-layouts  3.75 us (3%)
    pallas_call x1, Pallas kernels, inverse_and_late_fit(): pl.pallas_call(functools.partial(inverse_kernel, 128), grid=(1 + steps,),...  61.6 us
    pallas_call x1, Pallas kernels, exchange(): pl.pallas_call(functools.partial(exchange_kernel, gz_count, gy_count), in...  26.1 us
    all_to_all x1, waiting for transfers between devices, per_device(): late = swap(late.reshape(gz_count, slab_planes - early, col_pencil, count))  16.6 us
    pallas_call x1, Pallas kernels, early_fit(): pl.pallas_call(early_fit_kernel, grid=(early // block,), in_specs=[pl.Blo...  9.23 us
    all_to_all x1, starting transfers between devices, per_device(): late = swap(late.reshape(gz_count, slab_planes - early, col_pencil, count))  8.42 us
    pallas_call x1, Pallas kernels, filtered_products(): pl.pallas_call(filter_kernel, grid=(count // chunk,), in_specs=[pl.BlockS...  8.22 us
    all_to_all x1, starting transfers between devices, per_device(): slab = swap(first.reshape(gz_count, early, col_pencil, count))  6.46 us
    unnamed x4, local copies, waits for them, and re-layouts  3.17 us
  transfers between devices with their start and end apart: 2, of which 1 were waited for; matrix products, arithmetic and copies ran while one was open for 0% of the time, Pallas kernels for 50%

profile of v9, /device:TPU:0, one launch (start us, length us, event | category | flops | bytes accessed | tf_op | source)
XLA Modules:
  0.0 142.9 jit_solution(8571230619261897084)
XLA Ops:
  0.0 26.1 %shard_map.55 = (bf16[2,16,8,1,8,256]{5,4,3,2,1,0:T(8,128)(2,1)S(1)}, bf16[8,16,2,512]{3,2,1,0:T(2,128)(2,1)S(1)}, bf16[16,8,2,512]{3,2,1,0:T(2,128)(2,1)S(1)}, bf16[8,256,768]{2,1,0:T(8,128)(2,1)S(1)}) custom-call(bf16[2,256,1024]{2,1,0:T(8,128)(2,1)} %orbital_hbm.1, s32[1,1024]{1,0:T(1,128)} %bitcast.23, f32[256,128]{1,0:T(8,128)} %coulomb_hbm.1, ...), custom_call_target="tpu_custom_call" | custom-call | tf_op jit(solution)/shard_map/pallas_call | solution.py:270
  26.1 0.2 copy.11
  26.4 0.6 pad_maximum_fusion
  27.0 0.1 copy.8
  27.1 0.2 copy.9
  27.3 8.2 %shard_map.56 = (f32[128,8,1024]{2,1,0:T(8,128)}, f32[128,8,1024]{2,1,0:T(8,128)}) custom-call(bf16[8,256,256]{2,1,0:T(8,128)(2,1)S(1)} %bitcast.16, bf16[256,1024]{1,0:T(8,128)(2,1)S(1)} %bitcast.17, bf16[8,256,768]{2,1,0:T(8,128)(2,1)S(1)} %get-tuple-element.17.circulant_ref), custom_call_target="tpu_custom_call" | custom-call | flops 4294967296 | bytes 10485760 | tf_op jit(solution)/shard_map/pallas_call | solution.py:512
  35.6 6.5 %all-to-all-start.1 = ((f32[16,8,8,1024]{3,2,1,0:T(8,128)}), f32[16,8,8,1024]{3,2,1,0:T(8,128)}, u32[]{:S(2)}, u32[]{:S(2)}) async-start(f32[16,8,8,1024]{3,2,1,0:T(8,128)} %bitcast.20), calls=%async_computation.1 | async-start | bytes 8388608 | tf_op jit(solution)/shard_map/all_to_all | solution.py:621
  42.0 61.6 %shard_map.57 = (bf16[1024,1024]{1,0:T(8,128)(2,1)}, bf16[1024,1024]{1,0:T(8,128)(2,1)}, bf16[1024,1024]{1,0:T(8,128)(2,1)}) custom-call(bf16[256,1024]{1,0:T(8,128)(2,1)S(1)} %bitcast.18, f32[1024,1024]{1,0:T(8,128)} %bitcast.24), custom_call_target="tpu_custom_call" | custom-call | flops 64424509440 | bytes 8388608 | tf_op jit(solution)/shard_map/pallas_call | solution.py:461
  103.6 0.0 all-to-all-done.1.rows_ref
  103.6 8.4 %all-to-all-start = ((bf16[16,8,8,1024]{3,2,1,0:T(8,128)(2,1)}), bf16[16,8,8,1024]{3,2,1,0:T(8,128)(2,1)S(1)}, u32[]{:S(2)}, u32[]{:S(2)}) async-start(bf16[16,8,8,1024]{3,2,1,0:T(8,128)(2,1)} %bitcast.21), calls=%async_computation | async-start | bytes 4194304 | tf_op jit(solution)/shard_map/all_to_all | solution.py:623
  112.0 0.0 copy-start
  112.0 1.6 %copy-done = bf16[1024,1024]{1,0:T(8,128)(2,1)S(1)} copy-done((bf16[1024,1024]{1,0:T(8,128)(2,1)S(1)}, bf16[1024,1024]{1,0:T(8,128)(2,1)}, u32[]{:S(2)}) %copy-start) | copy-done | bytes 2097176
  113.6 0.0 copy-start.1
  113.6 1.6 %copy-done.1 = bf16[1024,1024]{1,0:T(8,128)(2,1)S(1)} copy-done((bf16[1024,1024]{1,0:T(8,128)(2,1)S(1)}, bf16[1024,1024]{1,0:T(8,128)(2,1)}, u32[]{:S(2)}) %copy-start.1) | copy-done | bytes 2097176
  115.2 9.2 %shard_map.58._ = bf16[16,128,1024]{2,1,0:T(8,128)(2,1)} custom-call(f32[16,8,8,1024]{3,2,1,0:T(8,128)} %all-to-all-done.1.rows_ref, bf16[1024,1024]{1,0:T(8,128)(2,1)S(1)} %copy-done, bf16[1024,1024]{1,0:T(8,128)(2,1)S(1)} %copy-done.1), custom_call_target="tpu_custom_call" | custom-call | flops 6442450944 | bytes 10485760 | tf_op jit(solution)/shard_map/pallas_call | solution.py:555
  124.4 16.6 %all-to-all-done.late_ref = bf16[16,8,8,1024]{3,2,1,0:T(8,128)(2,1)S(1)} async-done(((bf16[16,8,8,1024]{3,2,1,0:T(8,128)(2,1)}), bf16[16,8,8,1024]{3,2,1,0:T(8,128)(2,1)S(1)}, u32[]{:S(2)}, u32[]{:S(2)}) %all-to-all-start) | async-done | bytes 2097184 | tf_op jit(solution)/shard_map/all_to_all | solution.py:623
  141.0 1.8 %shard_map.59 = bf16[16,128,1024]{2,1,0:T(8,128)(2,1)} custom-call(bf16[16,8,8,1024]{3,2,1,0:T(8,128)(2,1)S(1)} %all-to-all-done.late_ref, bf16[16,128,1024]{2,1,0:T(8,128)(2,1)} %shard_map.58._), custom_call_target="tpu_custom_call", output_to_operand_aliasing={{}: (1, {})} | custom-call | bytes 4194304 | tf_op jit(solution)/shard_map/pallas_call | solution.py:583
Async XLA Ops:
  35.6 68.0 %all-to-all-start.1 = ((f32[16,8,8,1024]{3,2,1,0:T(8,128)}), f32[16,8,8,1024]{3,2,1,0:T(8,128)}, u32[]{:S(2)}, u32[]{:S(2)}) async-start(f32[16,8,8,1024]{3,2,1,0:T(8,128)} %bitcast.20), calls=%async_computation.1 | async-start | bytes 8388608 | tf_op jit(solution)/shard_map/all_to_all | solution.py:621
  103.6 37.5 %all-to-all-start = ((bf16[16,8,8,1024]{3,2,1,0:T(8,128)(2,1)}), bf16[16,8,8,1024]{3,2,1,0:T(8,128)(2,1)S(1)}, u32[]{:S(2)}, u32[]{:S(2)}) async-start(bf16[16,8,8,1024]{3,2,1,0:T(8,128)(2,1)} %bitcast.21), calls=%async_computation | async-start | bytes 4194304 | tf_op jit(solution)/shard_map/all_to_all | solution.py:623
  112.0 1.6 %copy-start = (bf16[1024,1024]{1,0:T(8,128)(2,1)S(1)}, bf16[1024,1024]{1,0:T(8,128)(2,1)}, u32[]{:S(2)}) copy-start(bf16[1024,1024]{1,0:T(8,128)(2,1)} %get-tuple-element.21.high_ref) | copy-start | bytes 6291460
  113.6 1.6 %copy-start.1 = (bf16[1024,1024]{1,0:T(8,128)(2,1)S(1)}, bf16[1024,1024]{1,0:T(8,128)(2,1)}, u32[]{:S(2)}) copy-start(bf16[1024,1024]{1,0:T(8,128)(2,1)} %get-tuple-element.22.low_ref) | copy-start | bytes 6291460

commit v10 on v9

--- a/solution.py
+++ b/solution.py
@@ -384,7 +384,7 @@
     sub = lax.broadcasted_iota(jnp.int32, (8, size), 0)
     for at in range(len(tiles)):
         first = at * 8
-        following = [at + 1] if at + 1 < len(tiles) else []
+        following = [i for i in (at + 1, at + 2) if i < len(tiles)]
         rest = [i for i in range(len(tiles)) if i != at and i not in following]
         stack = jnp.concatenate([tiles[i] for i in rest], axis=0)
         wide_lane = lax.broadcasted_iota(jnp.int32, stack.shape, 1)
@@ -490,11 +490,11 @@
         )
         return split_parts(sums * sums, 2)
 
-    following = products(0)
+    ahead = [products(0), products(1)]
     for c in range(col_count):
-        high, low = following
-        if c + 1 < col_count:
-            following = products(c + 1)
+        high, low = ahead.pop(0)
+        if c + 2 < col_count:
+            ahead.append(products(c + 2))
         smooth = jnp.dot(
             circulant_ref[c],
             jnp.concatenate([high, low, high], axis=0),

time: 144 us -> 144 us (level)
  transfers between devices with their start and end apart: 2 -> 2, of which waited for: 1 -> 1; matrix products, arithmetic and copies ran while one was open for 0% -> 0% of each run, Pallas kernels for 50% -> 49%
where the time goes in v10:
time: 144 us; the launch traced here: 143 us
  Pallas kernels  106 us (74%)
  waiting for transfers between devices  16.6 us (12%)
  starting transfers between devices  15.4 us (11%)
  local copies, waits for them, and re-layouts  3.75 us (3%)
    pallas_call x1, Pallas kernels, inverse_and_late_fit(): pl.pallas_call(functools.partial(inverse_kernel, 128), grid=(1 + steps,),...  61.1 us
    pallas_call x1, Pallas kernels, exchange(): pl.pallas_call(functools.partial(exchange_kernel, gz_count, gy_count), in...  26.1 us
    all_to_all x1, waiting for transfers between devices, per_device(): late = swap(late.reshape(gz_count, slab_planes - early, col_pencil, count))  16.6 us
    pallas_call x1, Pallas kernels, early_fit(): pl.pallas_call(early_fit_kernel, grid=(early // block,), in_specs=[pl.Blo...  9.23 us
    all_to_all x1, starting transfers between devices, per_device(): late = swap(late.reshape(gz_count, slab_planes - early, col_pencil, count))  8.89 us
    pallas_call x1, Pallas kernels, filtered_products(): pl.pallas_call(filter_kernel, grid=(count // chunk,), in_specs=[pl.BlockS...  7.87 us
    all_to_all x1, starting transfers between devices, per_device(): slab = swap(first.reshape(gz_count, early, col_pencil, count))  6.46 us
    unnamed x4, local copies, waits for them, and re-layouts  3.17 us
  transfers between devices with their start and end apart: 2, of which 1 were waited for; matrix products, arithmetic and copies ran while one was open for 0% of the time, Pallas kernels for 49%

profile of v10, /device:TPU:0, one launch (start us, length us, event | category | flops | bytes accessed | tf_op | source)
XLA Modules:
  0.0 142.5 jit_solution(13315013897964615911)
XLA Ops:
  0.0 26.1 %shard_map.55 = (bf16[2,16,8,1,8,256]{5,4,3,2,1,0:T(8,128)(2,1)S(1)}, bf16[8,16,2,512]{3,2,1,0:T(2,128)(2,1)S(1)}, bf16[16,8,2,512]{3,2,1,0:T(2,128)(2,1)S(1)}, bf16[8,256,768]{2,1,0:T(8,128)(2,1)S(1)}) custom-call(bf16[2,256,1024]{2,1,0:T(8,128)(2,1)} %orbital_hbm.1, s32[1,1024]{1,0:T(1,128)} %bitcast.23, f32[256,128]{1,0:T(8,128)} %coulomb_hbm.1, ...), custom_call_target="tpu_custom_call" | custom-call | tf_op jit(solution)/shard_map/pallas_call | solution.py:270
  26.1 0.2 copy.11
  26.4 0.6 pad_maximum_fusion
  27.0 0.1 copy.8
  27.1 0.2 copy.9
  27.3 7.9 %shard_map.56 = (f32[128,8,1024]{2,1,0:T(8,128)}, f32[128,8,1024]{2,1,0:T(8,128)}) custom-call(bf16[8,256,256]{2,1,0:T(8,128)(2,1)S(1)} %bitcast.16, bf16[256,1024]{1,0:T(8,128)(2,1)S(1)} %bitcast.17, bf16[8,256,768]{2,1,0:T(8,128)(2,1)S(1)} %get-tuple-element.17.circulant_ref), custom_call_target="tpu_custom_call" | custom-call | flops 4294967296 | bytes 10485760 | tf_op jit(solution)/shard_map/pallas_call | solution.py:512
  35.2 6.5 %all-to-all-start.1 = ((f32[16,8,8,1024]{3,2,1,0:T(8,128)}), f32[16,8,8,1024]{3,2,1,0:T(8,128)}, u32[]{:S(2)}, u32[]{:S(2)}) async-start(f32[16,8,8,1024]{3,2,1,0:T(8,128)} %bitcast.20), calls=%async_computation.1 | async-start | bytes 8388608 | tf_op jit(solution)/shard_map/all_to_all | solution.py:621
  41.7 61.1 %shard_map.57 = (bf16[1024,1024]{1,0:T(8,128)(2,1)}, bf16[1024,1024]{1,0:T(8,128)(2,1)}, bf16[1024,1024]{1,0:T(8,128)(2,1)}) custom-call(bf16[256,1024]{1,0:T(8,128)(2,1)S(1)} %bitcast.18, f32[1024,1024]{1,0:T(8,128)} %bitcast.24), custom_call_target="tpu_custom_call" | custom-call | flops 64424509440 | bytes 8388608 | tf_op jit(solution)/shard_map/pallas_call | solution.py:461
  102.8 0.0 all-to-all-done.1.rows_ref
  102.8 8.9 %all-to-all-start = ((bf16[16,8,8,1024]{3,2,1,0:T(8,128)(2,1)}), bf16[16,8,8,1024]{3,2,1,0:T(8,128)(2,1)S(1)}, u32[]{:S(2)}, u32[]{:S(2)}) async-start(bf16[16,8,8,1024]{3,2,1,0:T(8,128)(2,1)} %bitcast.21), calls=%async_computation | async-start | bytes 4194304 | tf_op jit(solution)/shard_map/all_to_all | solution.py:623
  111.7 0.0 copy-start
  111.7 1.6 %copy-done = bf16[1024,1024]{1,0:T(8,128)(2,1)S(1)} copy-done((bf16[1024,1024]{1,0:T(8,128)(2,1)S(1)}, bf16[1024,1024]{1,0:T(8,128)(2,1)}, u32[]{:S(2)}) %copy-start) | copy-done | bytes 2097176
  113.3 0.0 copy-start.1
  113.3 1.6 %copy-done.1 = bf16[1024,1024]{1,0:T(8,128)(2,1)S(1)} copy-done((bf16[1024,1024]{1,0:T(8,128)(2,1)S(1)}, bf16[1024,1024]{1,0:T(8,128)(2,1)}, u32[]{:S(2)}) %copy-start.1) | copy-done | bytes 2097176
  114.9 9.2 %shard_map.58._ = bf16[16,128,1024]{2,1,0:T(8,128)(2,1)} custom-call(f32[16,8,8,1024]{3,2,1,0:T(8,128)} %all-to-all-done.1.rows_ref, bf16[1024,1024]{1,0:T(8,128)(2,1)S(1)} %copy-done, bf16[1024,1024]{1,0:T(8,128)(2,1)S(1)} %copy-done.1), custom_call_target="tpu_custom_call" | custom-call | flops 6442450944 | bytes 10485760 | tf_op jit(solution)/shard_map/pallas_call | solution.py:555
  124.1 16.6 %all-to-all-done.late_ref = bf16[16,8,8,1024]{3,2,1,0:T(8,128)(2,1)S(1)} async-done(((bf16[16,8,8,1024]{3,2,1,0:T(8,128)(2,1)}), bf16[16,8,8,1024]{3,2,1,0:T(8,128)(2,1)S(1)}, u32[]{:S(2)}, u32[]{:S(2)}) %all-to-all-start) | async-done | bytes 2097184 | tf_op jit(solution)/shard_map/all_to_all | solution.py:623
  140.7 1.8 %shard_map.59 = bf16[16,128,1024]{2,1,0:T(8,128)(2,1)} custom-call(bf16[16,8,8,1024]{3,2,1,0:T(8,128)(2,1)S(1)} %all-to-all-done.late_ref, bf16[16,128,1024]{2,1,0:T(8,128)(2,1)} %shard_map.58._), custom_call_target="tpu_custom_call", output_to_operand_aliasing={{}: (1, {})} | custom-call | bytes 4194304 | tf_op jit(solution)/shard_map/pallas_call | solution.py:583
Async XLA Ops:
  35.2 67.6 %all-to-all-start.1 = ((f32[16,8,8,1024]{3,2,1,0:T(8,128)}), f32[16,8,8,1024]{3,2,1,0:T(8,128)}, u32[]{:S(2)}, u32[]{:S(2)}) async-start(f32[16,8,8,1024]{3,2,1,0:T(8,128)} %bitcast.20), calls=%async_computation.1 | async-start | bytes 8388608 | tf_op jit(solution)/shard_map/all_to_all | solution.py:621
  102.8 37.9 %all-to-all-start = ((bf16[16,8,8,1024]{3,2,1,0:T(8,128)(2,1)}), bf16[16,8,8,1024]{3,2,1,0:T(8,128)(2,1)S(1)}, u32[]{:S(2)}, u32[]{:S(2)}) async-start(bf16[16,8,8,1024]{3,2,1,0:T(8,128)(2,1)} %bitcast.21), calls=%async_computation | async-start | bytes 4194304 | tf_op jit(solution)/shard_map/all_to_all | solution.py:623
  111.7 1.6 %copy-start = (bf16[1024,1024]{1,0:T(8,128)(2,1)S(1)}, bf16[1024,1024]{1,0:T(8,128)(2,1)}, u32[]{:S(2)}) copy-start(bf16[1024,1024]{1,0:T(8,128)(2,1)} %get-tuple-element.21.high_ref) | copy-start | bytes 6291460
  113.3 1.6 %copy-start.1 = (bf16[1024,1024]{1,0:T(8,128)(2,1)S(1)}, bf16[1024,1024]{1,0:T(8,128)(2,1)}, u32[]{:S(2)}) copy-start(bf16[1024,1024]{1,0:T(8,128)(2,1)} %get-tuple-element.22.low_ref) | copy-start | bytes 6291460

commit v11 on v10

--- a/solution.py
+++ b/solution.py
@@ -578,7 +578,7 @@
 
 def place_late(late, fitted):
     sources, planes, col_count, count = late.shape
-    block = 2
+    block = 1
     first = (fitted.shape[0] - planes) // block
     return pl.pallas_call(
         place_late_kernel,

time: 144 us -> 145 us (level)
  no operation moved by 1% of the time
where the time goes in v11:
time: 145 us; the launch traced here: 144 us
  Pallas kernels  107 us (74%)
  waiting for transfers between devices  16.6 us (11%)
  starting transfers between devices  15.4 us (11%)
  local copies, waits for them, and re-layouts  3.75 us (3%)
    pallas_call x1, Pallas kernels, inverse_and_late_fit(): pl.pallas_call(functools.partial(inverse_kernel, 128), grid=(1 + steps,),...  61.1 us
    pallas_call x1, Pallas kernels, exchange(): pl.pallas_call(functools.partial(exchange_kernel, gz_count, gy_count), in...  26.1 us
    all_to_all x1, waiting for transfers between devices, per_device(): late = swap(late.reshape(gz_count, slab_planes - early, col_pencil, count))  16.6 us
    pallas_call x1, Pallas kernels, early_fit(): pl.pallas_call(early_fit_kernel, grid=(early // block,), in_specs=[pl.Blo...  9.23 us
    all_to_all x1, starting transfers between devices, per_device(): late = swap(late.reshape(gz_count, slab_planes - early, col_pencil, count))  8.89 us
    pallas_call x1, Pallas kernels, filtered_products(): pl.pallas_call(filter_kernel, grid=(count // chunk,), in_specs=[pl.BlockS...  7.87 us
    all_to_all x1, starting transfers between devices, per_device(): slab = swap(first.reshape(gz_count, early, col_pencil, count))  6.46 us
    unnamed x4, local copies, waits for them, and re-layouts  3.17 us
  transfers between devices with their start and end apart: 2, of which 1 were waited for; matrix products, arithmetic and copies ran while one was open for 0% of the time, Pallas kernels for 49%

profile of v11, /device:TPU:0, one launch (start us, length us, event | category | flops | bytes accessed | tf_op | source)
XLA Modules:
  0.0 143.7 jit_solution(9631891090849726695)
XLA Ops:
  0.0 26.1 %shard_map.55 = (bf16[2,16,8,1,8,256]{5,4,3,2,1,0:T(8,128)(2,1)S(1)}, bf16[8,16,2,512]{3,2,1,0:T(2,128)(2,1)S(1)}, bf16[16,8,2,512]{3,2,1,0:T(2,128)(2,1)S(1)}, bf16[8,256,768]{2,1,0:T(8,128)(2,1)S(1)}) custom-call(bf16[2,256,1024]{2,1,0:T(8,128)(2,1)} %orbital_hbm.1, s32[1,1024]{1,0:T(1,128)} %bitcast.23, f32[256,128]{1,0:T(8,128)} %coulomb_hbm.1, ...), custom_call_target="tpu_custom_call" | custom-call | tf_op jit(solution)/shard_map/pallas_call | solution.py:270
  26.1 0.2 copy.11
  26.4 0.6 pad_maximum_fusion
  27.0 0.1 copy.8
  27.1 0.2 copy.9
  27.3 7.9 %shard_map.56 = (f32[128,8,1024]{2,1,0:T(8,128)}, f32[128,8,1024]{2,1,0:T(8,128)}) custom-call(bf16[8,256,256]{2,1,0:T(8,128)(2,1)S(1)} %bitcast.16, bf16[256,1024]{1,0:T(8,128)(2,1)S(1)} %bitcast.17, bf16[8,256,768]{2,1,0:T(8,128)(2,1)S(1)} %get-tuple-element.17.circulant_ref), custom_call_target="tpu_custom_call" | custom-call | flops 4294967296 | bytes 10485760 | tf_op jit(solution)/shard_map/pallas_call | solution.py:512
  35.2 6.5 %all-to-all-start.1 = ((f32[16,8,8,1024]{3,2,1,0:T(8,128)}), f32[16,8,8,1024]{3,2,1,0:T(8,128)}, u32[]{:S(2)}, u32[]{:S(2)}) async-start(f32[16,8,8,1024]{3,2,1,0:T(8,128)} %bitcast.20), calls=%async_computation.1 | async-start | bytes 8388608 | tf_op jit(solution)/shard_map/all_to_all | solution.py:621
  41.7 61.1 %shard_map.57 = (bf16[1024,1024]{1,0:T(8,128)(2,1)}, bf16[1024,1024]{1,0:T(8,128)(2,1)}, bf16[1024,1024]{1,0:T(8,128)(2,1)}) custom-call(bf16[256,1024]{1,0:T(8,128)(2,1)S(1)} %bitcast.18, f32[1024,1024]{1,0:T(8,128)} %bitcast.24), custom_call_target="tpu_custom_call" | custom-call | flops 64424509440 | bytes 8388608 | tf_op jit(solution)/shard_map/pallas_call | solution.py:461
  102.8 0.0 all-to-all-done.1.rows_ref
  102.8 8.9 %all-to-all-start = ((bf16[16,8,8,1024]{3,2,1,0:T(8,128)(2,1)}), bf16[16,8,8,1024]{3,2,1,0:T(8,128)(2,1)S(1)}, u32[]{:S(2)}, u32[]{:S(2)}) async-start(bf16[16,8,8,1024]{3,2,1,0:T(8,128)(2,1)} %bitcast.21), calls=%async_computation | async-start | bytes 4194304 | tf_op jit(solution)/shard_map/all_to_all | solution.py:623
  111.7 0.0 copy-start
  111.7 1.6 %copy-done = bf16[1024,1024]{1,0:T(8,128)(2,1)S(1)} copy-done((bf16[1024,1024]{1,0:T(8,128)(2,1)S(1)}, bf16[1024,1024]{1,0:T(8,128)(2,1)}, u32[]{:S(2)}) %copy-start) | copy-done | bytes 2097176
  113.3 0.0 copy-start.1
  113.3 1.6 %copy-done.1 = bf16[1024,1024]{1,0:T(8,128)(2,1)S(1)} copy-done((bf16[1024,1024]{1,0:T(8,128)(2,1)S(1)}, bf16[1024,1024]{1,0:T(8,128)(2,1)}, u32[]{:S(2)}) %copy-start.1) | copy-done | bytes 2097176
  114.9 9.2 %shard_map.58._ = bf16[16,128,1024]{2,1,0:T(8,128)(2,1)} custom-call(f32[16,8,8,1024]{3,2,1,0:T(8,128)} %all-to-all-done.1.rows_ref, bf16[1024,1024]{1,0:T(8,128)(2,1)S(1)} %copy-done, bf16[1024,1024]{1,0:T(8,128)(2,1)S(1)} %copy-done.1), custom_call_target="tpu_custom_call" | custom-call | flops 6442450944 | bytes 10485760 | tf_op jit(solution)/shard_map/pallas_call | solution.py:555
  124.1 16.6 %all-to-all-done.late_ref = bf16[16,8,8,1024]{3,2,1,0:T(8,128)(2,1)S(1)} async-done(((bf16[16,8,8,1024]{3,2,1,0:T(8,128)(2,1)}), bf16[16,8,8,1024]{3,2,1,0:T(8,128)(2,1)S(1)}, u32[]{:S(2)}, u32[]{:S(2)}) %all-to-all-start) | async-done | bytes 2097184 | tf_op jit(solution)/shard_map/all_to_all | solution.py:623
  140.7 3.0 %shard_map.59 = bf16[16,128,1024]{2,1,0:T(8,128)(2,1)} custom-call(bf16[16,8,8,1024]{3,2,1,0:T(8,128)(2,1)S(1)} %all-to-all-done.late_ref, bf16[16,128,1024]{2,1,0:T(8,128)(2,1)} %shard_map.58._), custom_call_target="tpu_custom_call", output_to_operand_aliasing={{}: (1, {})} | custom-call | bytes 4194304 | tf_op jit(solution)/shard_map/pallas_call | solution.py:583
Async XLA Ops:
  35.2 67.6 %all-to-all-start.1 = ((f32[16,8,8,1024]{3,2,1,0:T(8,128)}), f32[16,8,8,1024]{3,2,1,0:T(8,128)}, u32[]{:S(2)}, u32[]{:S(2)}) async-start(f32[16,8,8,1024]{3,2,1,0:T(8,128)} %bitcast.20), calls=%async_computation.1 | async-start | bytes 8388608 | tf_op jit(solution)/shard_map/all_to_all | solution.py:621
  102.8 37.9 %all-to-all-start = ((bf16[16,8,8,1024]{3,2,1,0:T(8,128)(2,1)}), bf16[16,8,8,1024]{3,2,1,0:T(8,128)(2,1)S(1)}, u32[]{:S(2)}, u32[]{:S(2)}) async-start(bf16[16,8,8,1024]{3,2,1,0:T(8,128)(2,1)} %bitcast.21), calls=%async_computation | async-start | bytes 4194304 | tf_op jit(solution)/shard_map/all_to_all | solution.py:623
  111.7 1.6 %copy-start = (bf16[1024,1024]{1,0:T(8,128)(2,1)S(1)}, bf16[1024,1024]{1,0:T(8,128)(2,1)}, u32[]{:S(2)}) copy-start(bf16[1024,1024]{1,0:T(8,128)(2,1)} %get-tuple-element.21.high_ref) | copy-start | bytes 6291460
  113.3 1.6 %copy-start.1 = (bf16[1024,1024]{1,0:T(8,128)(2,1)S(1)}, bf16[1024,1024]{1,0:T(8,128)(2,1)}, u32[]{:S(2)}) copy-start(bf16[1024,1024]{1,0:T(8,128)(2,1)} %get-tuple-element.22.low_ref) | copy-start | bytes 6291460
